TPU v7x, 256 devices: a whole 4x4x8 slice. The times are simulated.
256 devices in a mesh: rows: 8 (over z), chan: 32 (over y, x, core).
Axes of the slice: x: 4, y: 4, z: 8, core: 2. Of those that a mesh axis runs over, the one named last changes fastest.
Arguments:
- feats: bfloat16 [128, 1024, 1024], P('rows', 'chan'), may hold values from -140 to 140
- norm_gain: float32 [1024], P('chan'), may hold values from 0.1 to 1.9
- proj_weight: float32 [8, 1024], P(None, 'chan'), may hold values from -320 to 320
- chan_bias: float32 [1024], P('chan'), may hold values from -8 to -2
Outputs:
- mixed: bfloat16 [128, 1024, 1024], P('rows', 'chan')
All inputs are finite; a program needn't handle non-finite values.
Results may differ from a plain program's by a relative error of at most 0.001.
Values sent between devices are 32-bit elements; how exact they have to be, the bound alone decides.
No kernel may reach another device: no remote copies, remote signals or barrier semaphores. Data moves between devices by JAX's collectives and lax.ppermute only.
A program may use at most 64 MiB of HBM per device.

v0:
```python
import jax
import jax.numpy as jnp
from jax import lax
from jax.experimental import pallas as pl
from jax.experimental.pallas import tpu as pltpu
from jax.sharding import PartitionSpec as P

CHANNELS = 1024
EPSILON = 1e-05
LANES = 128
SLOTS = 7

VMEM = pl.BlockSpec(memory_space=pltpu.VMEM)


def call(kernel, outs, *args, aliases=None, limit=40, name=None):
    return pl.pallas_call(
        kernel,
        out_shape=outs,
        in_specs=[VMEM] * len(args),
        out_specs=jax.tree.map(lambda _: VMEM, outs),
        input_output_aliases=aliases or {},
        compiler_params=pltpu.CompilerParams(vmem_limit_bytes=limit << 20),
        name=name,
    )(*args)


def f32(*shape):
    return jax.ShapeDtypeStruct(shape, jnp.float32)


def place():
    chan = lax.axis_index("chan")
    return chan & 1, (chan >> 1) & 3


def lane_tile(core, x):
    return pl.ds(pl.multiple_of((core * 4 + (x & 3)) * LANES, LANES), LANES)


def project(feats, gain, weight, keep, send, wide):
    core, x = place()
    rows, chans, _ = feats.shape
    w, g = weight[...], gain[...]
    picked = [w[0:1] - w[1:2], w[2:3] - w[1:2], w[6:7], w[3:4] - w[4:5], w[5:6] - w[4:5], w[7:8]]
    scaled = [p * g for p in picked]
    depth = rows * chans
    spot = lax.broadcasted_iota(jnp.int32, (chans, depth), 1) % chans
    copies = (spot == lax.broadcasted_iota(jnp.int32, (chans, depth), 0)).astype(jnp.bfloat16)
    band = lax.broadcasted_iota(jnp.int32, (rows, depth), 1) // chans
    own = band == lax.broadcasted_iota(jnp.int32, (rows, depth), 0)
    rest = jnp.concatenate(scaled + scaled[:2], axis=0)
    for part in range(3):
        head = rest.astype(jnp.bfloat16)
        rest = rest - head.astype(jnp.float32)
        spread_out = jnp.dot(head, copies, preferred_element_type=jnp.float32)
        for j in range(6):
            row = jnp.broadcast_to(spread_out[j : j + 1], (rows, depth))
            at = (part * 6 + j) * rows
            wide[at : at + rows] = jnp.where(own, row, 0.0).astype(jnp.bfloat16)
    for half, out in ((0, keep), (1, send)):
        for s in range(4):
            block = feats[:, :, lane_tile(core ^ half, x + s)]
            sums = jnp.dot(wide[...], block.reshape(depth, LANES), preferred_element_type=jnp.float32)
            sums = sums[0 : 6 * rows] + sums[6 * rows : 12 * rows] + sums[12 * rows :]
            out[s, 0:6] = sums.reshape(6, rows, LANES)
            values = block.astype(jnp.float32)
            out[s, 6] = jnp.sum(values * values, axis=1)


def join_cores(keep, arrived, *outs):
    for s, out in enumerate(outs):
        out[...] = keep[s] + arrived[s]


def join_x(a, b, c, d, out):
    out[...] = (a[...] + b[...]) + (c[...] + d[...])


def join_y(a, b, c, d, out):
    total = [(a[j] + b[j]) + (c[j] + d[j]) for j in range(SLOTS)]
    inverse = lax.rsqrt(total[6] / CHANNELS + EPSILON)
    scale = inverse * CHANNELS**-0.5
    for base in (0, 3):
        first, last = total[base] * scale, total[base + 1] * scale
        top = jnp.maximum(jnp.maximum(first, last), 0.0)
        first, mid, last = jnp.exp(first - top), jnp.exp(-top), jnp.exp(last - top)
        share = 1.0 / (first + mid + last)
        out[base] = first * share
        out[base + 1] = last * share
        out[base + 2] = total[base + 2] * scale
    out[6] = inverse


def edge_masked(first, last):
    column = lax.broadcasted_iota(jnp.int32, first.shape, 1)
    middle = 1.0 - first - last
    first = jnp.where(column == 0, 0.0, first)
    last = jnp.where(column == first.shape[1] - 1, 0.0, last)
    return first, middle, last


def column_of(row):
    n = row.shape[1]
    eye = lax.broadcasted_iota(jnp.int32, (n, n), 0) == lax.broadcasted_iota(jnp.int32, (n, n), 1)
    return jnp.sum(jnp.where(eye, jnp.broadcast_to(row, (n, n)), 0.0), axis=1, keepdims=True)


def rate_root(gate, bias):
    return lax.rsqrt(1.0 + jnp.exp(-(gate + bias)))


def blended(state, taps, h):
    left = pltpu.roll(state, 1, axis=2)
    right = pltpu.roll(state, state.shape[2] - 1, axis=2)
    a, b, c = (taps[k, pl.ds(h, 1), :] for k in range(3))
    return a * left + b * state + c * right


def row_at(step, upward, rows):
    return jnp.where(upward, rows - 1 - step, step)


def parity():
    return lax.axis_index("rows") & 1


def row_coefficients(feats, gates, inverse, gain, bias, h):
    values = feats[h].astype(jnp.float32)
    root = rate_root(gates[pl.ds(h, 1), :], bias)
    drive = root * (values * inverse[pl.ds(h, 1), :] * gain)
    shape = (values.shape[0] // 8, 8, values.shape[1])
    return (1.0 - root * root).reshape(shape), drive.reshape(shape)


def near_side(p0, p1, p2, p3, q0, q1, q2, q3, feats, gain, bias, near_taps, far_taps, far_gate, inverse, raw, decay, drive, kept, end):
    core, x = place()
    odd = parity()
    rows = feats.shape[0]
    near, far = odd * 3, 3 - odd * 3
    for other, pieces in ((0, (p0, p1, p2, p3)), (1, (q0, q1, q2, q3))):
        for s, piece in enumerate(pieces):
            at = lane_tile(core ^ other, x - s + 4)
            for k in range(3):
                raw[k, :, at] = piece[near + k]
            for k in range(2):
                far_taps[k, :, at] = piece[far + k]
            far_gate[:, at] = piece[far + 2]
            inverse[:, at] = piece[6]
    for k, tap in enumerate(edge_masked(raw[0], raw[1])):
        near_taps[k] = tap
    for k, tap in enumerate(edge_masked(far_taps[0], far_taps[1])):
        far_taps[k] = tap
    gain_column, bias_column = column_of(gain[...]), column_of(bias[...])
    gates = raw.at[2]

    def step(r, state):
        h = row_at(r, odd == 1, rows)
        d, q = row_coefficients(feats, gates, inverse, gain_column, bias_column, h)
        decay[h] = d
        drive[h] = q
        state = d * blended(state, near_taps, h) + q
        kept[h] = state
        return state

    end[...] = lax.fori_loop(0, rows, step, jnp.zeros(end.shape, jnp.float32))


def far_side(far_gate, inverse, feats, gain, bias, decay, drive):
    gain_column, bias_column = column_of(gain[...]), column_of(bias[...])

    def step(h, carry):
        decay[h], drive[h] = row_coefficients(feats, far_gate, inverse, gain_column, bias_column, h)
        return carry

    lax.fori_loop(0, feats.shape[0], step, 0)


def partner_side(raw, bias, taps, decay):
    bias_column = column_of(bias[...])
    for k, tap in enumerate(edge_masked(raw[0], raw[1])):
        taps[k] = tap

    def step(h, carry):
        root = rate_root(raw[2, pl.ds(h, 1), :], bias_column)
        decay[h] = (1.0 - root * root).reshape(decay.shape[1:])
        return carry

    lax.fori_loop(0, decay.shape[0], step, 0)


def scan_rows(state, upward, decay, drive, taps, emit):
    rows = decay.shape[0]

    def step(r, state):
        h = row_at(r, upward, rows)
        state = decay[h] * blended(state, taps, h)
        if drive is not None:
            state = state + drive[h]
        if emit is not None:
            emit(h, state)
        return state

    return lax.fori_loop(0, rows, step, state)


def turns(stage):
    position = lax.axis_index("rows")
    pair, odd = position >> 1, position & 1
    last = 3 - pair
    far = jnp.where(odd == 1, pair, last)
    return odd, far == stage, 3 - far == stage


def first_stage(partner_end, decay, drive, taps, kept_in, kept, leaving):
    odd, far, _ = turns(0)

    def emit(h, state):
        kept[h] = state

    @pl.when(far)
    def _():
        leaving[...] = scan_rows(partner_end[...], odd == 0, decay, drive, taps, emit)

    @pl.when(jnp.logical_not(far))
    def _():
        kept[...] = kept_in[...]


def later_stage(stage, final, *refs):
    if final:
        kept, refs = refs[0], refs[1:]
    far_in, near_in, partner_end, pd, pt, nd, nq, nt, fd, fq, ft = refs[:11]
    *before, out, leaving = refs[11:]
    odd, far, near = turns(stage)

    def emit(h, state):
        if final:
            out[h] = (kept[h] * state).reshape(out.shape[1:]).astype(out.dtype)
        else:
            out[h] = state

    @pl.when(far)
    def _():
        state = scan_rows(far_in[...], odd == 0, pd, None, pt, None) + partner_end[...]
        leaving[...] = scan_rows(state, odd == 0, fd, fq, ft, emit)

    @pl.when(near)
    def _():
        leaving[...] = scan_rows(near_in[...], odd == 1, nd, nq, nt, emit)

    if before:

        @pl.when(jnp.logical_not(far | near))
        def _():
            out[...] = before[0][...]


def chan_shift(value, target):
    return lax.ppermute(value, "chan", [(i, target(i)) for i in range(32)])


def along_x(value, s):
    return chan_shift(value, lambda i: (i & ~6) | ((((i >> 1) + s) & 3) << 1))


def along_y(value, s):
    return chan_shift(value, lambda i: (i & 7) | ((((i >> 3) + s) & 3) << 3))


def other_core(value):
    return chan_shift(value, lambda i: i ^ 1)


def shards(feats, norm_gain, proj_weight, chan_bias):
    rows, chans, cols = feats.shape
    gain, bias = norm_gain.reshape(1, chans), chan_bias.reshape(1, chans)
    piece = f32(SLOTS, rows, LANES)
    half = f32(4, SLOTS, rows, LANES)
    keep, send = pl.pallas_call(
        project,
        out_shape=(half, half),
        in_specs=[VMEM] * 3,
        out_specs=(VMEM, VMEM),
        scratch_shapes=[pltpu.VMEM((18 * rows, rows * chans), jnp.bfloat16)],
        compiler_params=pltpu.CompilerParams(vmem_limit_bytes=40 << 20),
    )(feats, gain, proj_weight)
    mine, *others = call(join_cores, (piece,) * 4, keep, other_core(send))
    part = call(join_x, piece, mine, *(along_x(v, s + 1) for s, v in enumerate(others)))
    whole = call(join_y, piece, part, *(along_y(part, s) for s in (1, 2, 3)))
    pieces = [whole] + [along_x(whole, s) for s in (1, 2, 3)]
    pieces = pieces + [other_core(v) for v in pieces]

    state = f32(chans // 8, 8, cols)
    block = f32(rows, chans // 8, 8, cols)
    taps = f32(3, rows, cols)
    line = f32(rows, cols)
    near_taps, far_taps, far_gate, inverse, raw, near_decay, near_drive, kept, end = call(
        near_side, (taps, taps, line, line, taps, block, block, block, state), *pieces, feats, gain, bias
    )

    def swapped(value):
        return lax.ppermute(value, "rows", [(p, p ^ 1) for p in range(8)])

    partner_end = swapped(end)
    partner_raw = swapped(raw)
    far_decay, far_drive = call(far_side, (block, block), far_gate, inverse, feats, gain, bias)
    kept, leaving = call(
        first_stage, (block, state), partner_end, far_decay, far_drive, far_taps, kept, aliases={4: 0}
    )
    partner_taps, partner_decay = call(partner_side, (taps, block), partner_raw, bias)
    shared = (
        partner_end, partner_decay, partner_taps, near_decay, near_drive, near_taps, far_decay, far_drive, far_taps,
    )
    out = None
    for stage in (1, 2, 3):
        t = stage - 1
        far_in = lax.ppermute(leaving, "rows", [(2 * t + 1, 2 * t + 3), (6 - 2 * t, 4 - 2 * t)])
        near_in = lax.ppermute(leaving, "rows", [(2 * t + 1, 2 * t + 2), (6 - 2 * t, 5 - 2 * t)])

        def kernel(*refs, stage=stage):
            later_stage(stage, stage > 1, *refs)

        args = (far_in, near_in, *shared)
        if stage == 1:
            kept, leaving = call(kernel, (block, state), *args, kept, aliases={11: 0})
        elif stage == 2:
            made = jax.ShapeDtypeStruct(feats.shape, jnp.bfloat16)
            out, leaving = call(kernel, (made, state), kept, *args)
        else:
            out, _ = call(kernel, (made, state), kept, *args, out, aliases={12: 0})
    return out


def solution(mesh):
    in_specs = (P("rows", "chan", None), P("chan"), P(None, "chan"), P("chan"))
    out_specs = P("rows", "chan", None)
    return jax.shard_map(shards, mesh=mesh, in_specs=in_specs, out_specs=out_specs, check_vma=False)
```

profile of v0, /device:TPU:24, one launch (start us, length us, event | category | flops | bytes accessed | tf_op | source)
XLA Modules:
  0.0 86.7 jit_solution(6477280237111814612)
XLA Ops:
  0.0 1.2 %copy-done = bf16[16,32,1024]{2,1,0:T(8,128)(2,1)S(1)} copy-done((bf16[16,32,1024]{2,1,0:T(8,128)(2,1)S(1)}, bf16[16,32,1024]{2,1,0:T(8,128)(2,1)}, u32[]{:S(2)}) %copy-start) | copy-done | bytes 1048600
  1.9 0.7 copy-done.4
  2.6 0.9 %shard_map.46 = (f32[4,7,16,128]{3,2,1,0:T(8,128)S(1)}, f32[4,7,16,128]{3,2,1,0:T(8,128)S(1)}) custom-call(bf16[16,32,1024]{2,1,0:T(8,128)(2,1)S(1)} %copy-done, f32[1,32]{1,0:T(1,128)S(1)} %bitcast.2, f32[8,32]{1,0:T(8,128)S(1)} %copy-done.4), custom_call_target="tpu_custom_call" | custom-call | tf_op jit(solution)/shard_map/pallas_call | solution.py:280
  3.6 1.5 %collective-permute-done.arrived = f32[4,7,16,128]{3,2,1,0:T(8,128)S(1)} collective-permute-done((f32[4,7,16,128]{3,2,1,0:T(8,128)S(1)}, f32[4,7,16,128]{3,2,1,0:T(8,128)S(1)}, u32[]{:S(2)}, u32[]{:S(2)}) %collective-permute-start) | collective-permute-done | bytes 229408 | tf_op jit(solution)/shard_map/ppermute | solution.py:260
  5.1 1.6 %collective-permute-start.1 = (f32[7,16,128]{2,1,0:T(8,128)S(1)}, f32[7,16,128]{2,1,0:T(8,128)S(1)}, u32[]{:S(2)}, u32[]{:S(2)}) collective-permute-start(f32[7,16,128]{2,1,0:T(8,128)S(1)} %get-tuple-element.34), channel_id=1, source_target_pairs={{0,2},{1,3},{2,4},{3,5},{4,6},{5,7},{6,0},{7,1},{8,10},{9,11},{10,... | collective-permute-start | bytes 172040 | tf_op jit(solution)/shard_map/ppermute | solution.py:260
  6.7 2.7 %collective-permute-start.2 = (f32[7,16,128]{2,1,0:T(8,128)S(1)}, f32[7,16,128]{2,1,0:T(8,128)S(1)}, u32[]{:S(2)}, u32[]{:S(2)}) collective-permute-start(f32[7,16,128]{2,1,0:T(8,128)S(1)} %get-tuple-element.35), channel_id=1, source_target_pairs={{0,4},{1,5},{2,6},{3,7},{4,0},{5,1},{6,2},{7,3},{8,12},{9,13},{10,... | collective-permute-start | bytes 172040 | tf_op jit(solution)/shard_map/ppermute | solution.py:260
  9.4 1.4 %collective-permute-start.3 = (f32[7,16,128]{2,1,0:T(8,128)S(1)}, f32[7,16,128]{2,1,0:T(8,128)S(1)}, u32[]{:S(2)}, u32[]{:S(2)}) collective-permute-start(f32[7,16,128]{2,1,0:T(8,128)S(1)} %get-tuple-element.36), channel_id=1, source_target_pairs={{0,6},{1,7},{2,0},{3,1},{4,2},{5,3},{6,4},{7,5},{8,14},{9,15},{10,... | collective-permute-start | bytes 172040 | tf_op jit(solution)/shard_map/ppermute | solution.py:260
  10.8 1.7 %collective-permute-done.2.c = f32[7,16,128]{2,1,0:T(8,128)S(1)} collective-permute-done((f32[7,16,128]{2,1,0:T(8,128)S(1)}, f32[7,16,128]{2,1,0:T(8,128)S(1)}, u32[]{:S(2)}, u32[]{:S(2)}) %collective-permute-start.2) | collective-permute-done | bytes 57376 | tf_op jit(solution)/shard_map/ppermute | solution.py:260
  12.6 1.0 %collective-permute-done.3.d = f32[7,16,128]{2,1,0:T(8,128)S(1)} collective-permute-done((f32[7,16,128]{2,1,0:T(8,128)S(1)}, f32[7,16,128]{2,1,0:T(8,128)S(1)}, u32[]{:S(2)}, u32[]{:S(2)}) %collective-permute-start.3) | collective-permute-done | bytes 57376 | tf_op jit(solution)/shard_map/ppermute | solution.py:260
  13.6 0.8 collective-permute-start.6
  14.4 1.2 %collective-permute-start.5 = (f32[7,16,128]{2,1,0:T(8,128)S(1)}, f32[7,16,128]{2,1,0:T(8,128)S(1)}, u32[]{:S(2)}, u32[]{:S(2)}) collective-permute-start(f32[7,16,128]{2,1,0:T(8,128)S(1)} %shard_map.48.a), channel_id=1, source_target_pairs={{0,16},{1,17},{2,18},{3,19},{4,20},{5,21},{6,22},{7,23},{8,24},{9,... | collective-permute-start | bytes 172040 | tf_op jit(solution)/shard_map/ppermute | solution.py:260
  15.7 1.9 %collective-permute-start.4 = (f32[7,16,128]{2,1,0:T(8,128)S(1)}, f32[7,16,128]{2,1,0:T(8,128)S(1)}, u32[]{:S(2)}, u32[]{:S(2)}) collective-permute-start(f32[7,16,128]{2,1,0:T(8,128)S(1)} %shard_map.48.a), channel_id=1, source_target_pairs={{0,8},{1,9},{2,10},{3,11},{4,12},{5,13},{6,14},{7,15},{8,16},{9,17... | collective-permute-start | bytes 172040 | tf_op jit(solution)/shard_map/ppermute | solution.py:260
  17.5 1.5 %collective-permute-done.6.d = f32[7,16,128]{2,1,0:T(8,128)S(1)} collective-permute-done((f32[7,16,128]{2,1,0:T(8,128)S(1)}, f32[7,16,128]{2,1,0:T(8,128)S(1)}, u32[]{:S(2)}, u32[]{:S(2)}) %collective-permute-start.6) | collective-permute-done | bytes 57376 | tf_op jit(solution)/shard_map/ppermute | solution.py:260
  19.1 1.0 %collective-permute-done.5.c = f32[7,16,128]{2,1,0:T(8,128)S(1)} collective-permute-done((f32[7,16,128]{2,1,0:T(8,128)S(1)}, f32[7,16,128]{2,1,0:T(8,128)S(1)}, u32[]{:S(2)}, u32[]{:S(2)}) %collective-permute-start.5) | collective-permute-done | bytes 57376 | tf_op jit(solution)/shard_map/ppermute | solution.py:260
  20.6 2.7 %collective-permute-start.9 = (f32[7,16,128]{2,1,0:T(8,128)S(1)}, f32[7,16,128]{2,1,0:T(8,128)S(1)}, u32[]{:S(2)}, u32[]{:S(2)}) collective-permute-start(f32[7,16,128]{2,1,0:T(8,128)S(1)} %shard_map.49.p0), channel_id=1, source_target_pairs={{0,6},{1,7},{2,0},{3,1},{4,2},{5,3},{6,4},{7,5},{8,14},{9,15},{10,... | collective-permute-start | bytes 172040 | tf_op jit(solution)/shard_map/ppermute | solution.py:260
  23.3 0.9 %collective-permute-start.7 = (f32[7,16,128]{2,1,0:T(8,128)S(1)}, f32[7,16,128]{2,1,0:T(8,128)S(1)}, u32[]{:S(2)}, u32[]{:S(2)}) collective-permute-start(f32[7,16,128]{2,1,0:T(8,128)S(1)} %shard_map.49.p0), channel_id=1, source_target_pairs={{0,2},{1,3},{2,4},{3,5},{4,6},{5,7},{6,0},{7,1},{8,10},{9,11},{10,... | collective-permute-start | bytes 172040 | tf_op jit(solution)/shard_map/ppermute | solution.py:260
  24.2 0.9 %collective-permute-done.9.p3 = f32[7,16,128]{2,1,0:T(8,128)S(1)} collective-permute-done((f32[7,16,128]{2,1,0:T(8,128)S(1)}, f32[7,16,128]{2,1,0:T(8,128)S(1)}, u32[]{:S(2)}, u32[]{:S(2)}) %collective-permute-start.9) | collective-permute-done | bytes 57376 | tf_op jit(solution)/shard_map/ppermute | solution.py:260
  25.1 4.0 %collective-permute-done.8.p2 = f32[7,16,128]{2,1,0:T(8,128)S(1)} collective-permute-done((f32[7,16,128]{2,1,0:T(8,128)S(1)}, f32[7,16,128]{2,1,0:T(8,128)S(1)}, u32[]{:S(2)}, u32[]{:S(2)}) %collective-permute-start.8) | collective-permute-done | bytes 57376 | tf_op jit(solution)/shard_map/ppermute | solution.py:260
  29.6 0.7 collective-permute-done.12.q2
  30.6 2.4 %shard_map.50 = (f32[3,16,1024]{2,1,0:T(8,128)S(1)}, f32[3,16,1024]{2,1,0:T(8,128)S(1)}, f32[16,1024]{1,0:T(8,128)S(1)}, f32[16,1024]{1,0:T(8,128)S(1)}, f32[3,1...) custom-call(f32[7,16,128]{2,1,0:T(8,128)S(1)} %shard_map.49.p0, ...), custom_call_target="tpu_custom_call" | custom-call | tf_op jit(solution)/shard_map/pallas_call | solution.py:17
  33.0 2.0 %collective-permute-start.14 = (f32[4,8,1024]{2,1,0:T(8,128)S(1)}, f32[4,8,1024]{2,1,0:T(8,128)S(1)}, u32[]{:S(2)}, u32[]{:S(2)}) collective-permute-start(f32[4,8,1024]{2,1,0:T(8,128)S(1)} %get-tuple-element.37), channel_id=1, source_target_pairs={{0,32},{32,0},{64,96},{96,64},{128,160},{160,128},{192,224},{224,1... | collective-permute-start | bytes 393224 | tf_op jit(solution)/shard_map/ppermute | solution.py:303
  35.1 1.0 %shard_map.51 = (f32[16,4,8,1024]{3,2,1,0:T(8,128)S(1)}, f32[16,4,8,1024]{3,2,1,0:T(8,128)S(1)}) custom-call(f32[16,1024]{1,0:T(8,128)S(1)} %get-tuple-element.38.far_gate, f32[16,1024]{1,0:T(8,128)S(1)} %get-tuple-element.39.inverse, bf16[16,32,1024]{2,1,0:T(8,128)(2,1)S(1)} %copy-done.1, f32[1,32]{1,0:T(1,128)S(1)} %bitcast.4, f32[1,32]{1,0:T(1,128)S(1)} %bitcast.6), custom_call_target="tpu_custom_call" | custom-call | tf_op jit(solution)/shard_map/pallas_call | solution.py:17
  36.1 3.2 %collective-permute-done.14.partner_end.refs_2_.refs_3_ = f32[4,8,1024]{2,1,0:T(8,128)S(1)} collective-permute-done((f32[4,8,1024]{2,1,0:T(8,128)S(1)}, f32[4,8,1024]{2,1,0:T(8,128)S(1)}, u32[]{:S(2)}, u32[]{:S(2)}) %collective-permute-start.14) | collective-permute-done | bytes 131104 | tf_op jit(solution)/shard_map/ppermute | solution.py:303
  39.6 0.7 collective-permute-start.16
  40.3 0.7 collective-permute-start.15
  41.0 2.1 %collective-permute-done.17.raw = f32[3,16,1024]{2,1,0:T(8,128)S(1)} collective-permute-done((f32[3,16,1024]{2,1,0:T(8,128)S(1)}, f32[3,16,1024]{2,1,0:T(8,128)S(1)}, u32[]{:S(2)}, u32[]{:S(2)}) %collective-permute-start.17) | collective-permute-done | bytes 196640 | tf_op jit(solution)/shard_map/ppermute | solution.py:303
  43.1 0.9 %shard_map.53 = (f32[3,16,1024]{2,1,0:T(8,128)S(1)}, f32[16,4,8,1024]{3,2,1,0:T(8,128)S(1)}) custom-call(f32[3,16,1024]{2,1,0:T(8,128)S(1)} %collective-permute-done.17.raw, f32[1,32]{1,0:T(1,128)S(1)} %bitcast.7), custom_call_target="tpu_custom_call" | custom-call | tf_op jit(solution)/shard_map/pallas_call | solution.py:17
  44.4 0.7 collective-permute-start.19
  45.7 1.0 %shard_map.55 = (bf16[16,32,1024]{2,1,0:T(8,128)(2,1)}, f32[4,8,1024]{2,1,0:T(8,128)S(1)}) custom-call(f32[16,4,8,1024]{3,2,1,0:T(8,128)S(1)} %get-tuple-element.52.refs_0_, f32[4,8,1024]{2,1,0:T(8,128)S(1)} %collective-permute-done.18.refs_1_, f32[4,8,1024]{2,1,0:T(8,128)S(1)} %collective-permute-done.19.refs_2_, ...), custom_call_target="tpu_custom_call" | custom-call | tf_op jit(solution)/shard_map/pallas_call | solution.py:17
  47.4 1.3 %collective-permute-start.20 = (f32[4,8,1024]{2,1,0:T(8,128)S(1)}, f32[4,8,1024]{2,1,0:T(8,128)S(1)}, u32[]{:S(2)}, u32[]{:S(2)}) collective-permute-start(f32[4,8,1024]{2,1,0:T(8,128)S(1)} %get-tuple-element.54), channel_id=1, source_target_pairs={{160,224},{64,0},{161,225},{65,1},{162,226},{66,2},{163,227},{67,3... | collective-permute-start | bytes 393224 | tf_op jit(solution)/shard_map/ppermute | solution.py:318
  48.7 31.1 %collective-permute-done.20.refs_1_ = f32[4,8,1024]{2,1,0:T(8,128)S(1)} collective-permute-done((f32[4,8,1024]{2,1,0:T(8,128)S(1)}, f32[4,8,1024]{2,1,0:T(8,128)S(1)}, u32[]{:S(2)}, u32[]{:S(2)}) %collective-permute-start.20) | collective-permute-done | bytes 131104 | tf_op jit(solution)/shard_map/ppermute | solution.py:318
  79.8 6.9 %shard_map.56 = (bf16[16,32,1024]{2,1,0:T(8,128)(2,1)}, f32[4,8,1024]{2,1,0:T(8,128)}) custom-call(f32[16,4,8,1024]{3,2,1,0:T(8,128)S(1)} %get-tuple-element.52.refs_0_, f32[4,8,1024]{2,1,0:T(8,128)S(1)} %collective-permute-done.20.refs_1_, f32[4,8,1024]{2,1,0:T(8,128)S(1)} %collective-permute-done.21.refs_2_, ...), custom_call_target="tpu_custom_call", output_to_operand_aliasing={{0}: (12, {})} | custom-call | tf_op jit(solution)/shard_map/pallas_call | solution.py:17
  (33 shorter events, 4.1 us)
Async XLA Ops:
  0.0 30.6 %copy-start.3 = (f32[32]{0:T(128)S(1)}, f32[32]{0:T(128)}, u32[]{:S(2)}) copy-start(f32[32]{0:T(128)} %param.7) | copy-start | bytes 388
  0.0 1.2 %copy-start = (bf16[16,32,1024]{2,1,0:T(8,128)(2,1)S(1)}, bf16[16,32,1024]{2,1,0:T(8,128)(2,1)}, u32[]{:S(2)}) copy-start(bf16[16,32,1024]{2,1,0:T(8,128)(2,1)} %feats.5) | copy-start | bytes 3145732
  1.2 0.7 copy-start.2
  1.9 0.7 copy-start.4
  2.6 28.0 %copy-start.1 = (bf16[16,32,1024]{2,1,0:T(8,128)(2,1)S(1)}, bf16[16,32,1024]{2,1,0:T(8,128)(2,1)}, u32[]{:S(2)}) copy-start(bf16[16,32,1024]{2,1,0:T(8,128)(2,1)} %feats.5) | copy-start | bytes 3145732
  3.5 1.6 %collective-permute-start = (f32[4,7,16,128]{3,2,1,0:T(8,128)S(1)}, f32[4,7,16,128]{3,2,1,0:T(8,128)S(1)}, u32[]{:S(2)}, u32[]{:S(2)}) collective-permute-start(f32[4,7,16,128]{3,2,1,0:T(8,128)S(1)} %get-tuple-element.32), channel_id=1, source_target_pairs={{0,1},{1,0},{2,3},{3,2},{4,5},{5,4},{6,7},{7,6},{8,9},{9,8},{10,11... | collective-permute-start | bytes 688136 | tf_op jit(solution)/shard_map/ppermute | solution.py:260
  5.1 5.7 %collective-permute-start.1 = (f32[7,16,128]{2,1,0:T(8,128)S(1)}, f32[7,16,128]{2,1,0:T(8,128)S(1)}, u32[]{:S(2)}, u32[]{:S(2)}) collective-permute-start(f32[7,16,128]{2,1,0:T(8,128)S(1)} %get-tuple-element.34), channel_id=1, source_target_pairs={{0,2},{1,3},{2,4},{3,5},{4,6},{5,7},{6,0},{7,1},{8,10},{9,11},{10,... | collective-permute-start | bytes 172040 | tf_op jit(solution)/shard_map/ppermute | solution.py:260
  6.7 5.9 %collective-permute-start.2 = (f32[7,16,128]{2,1,0:T(8,128)S(1)}, f32[7,16,128]{2,1,0:T(8,128)S(1)}, u32[]{:S(2)}, u32[]{:S(2)}) collective-permute-start(f32[7,16,128]{2,1,0:T(8,128)S(1)} %get-tuple-element.35), channel_id=1, source_target_pairs={{0,4},{1,5},{2,6},{3,7},{4,0},{5,1},{6,2},{7,3},{8,12},{9,13},{10,... | collective-permute-start | bytes 172040 | tf_op jit(solution)/shard_map/ppermute | solution.py:260
  9.4 4.2 %collective-permute-start.3 = (f32[7,16,128]{2,1,0:T(8,128)S(1)}, f32[7,16,128]{2,1,0:T(8,128)S(1)}, u32[]{:S(2)}, u32[]{:S(2)}) collective-permute-start(f32[7,16,128]{2,1,0:T(8,128)S(1)} %get-tuple-element.36), channel_id=1, source_target_pairs={{0,6},{1,7},{2,0},{3,1},{4,2},{5,3},{6,4},{7,5},{8,14},{9,15},{10,... | collective-permute-start | bytes 172040 | tf_op jit(solution)/shard_map/ppermute | solution.py:260
  13.6 5.5 %collective-permute-start.6 = (f32[7,16,128]{2,1,0:T(8,128)S(1)}, f32[7,16,128]{2,1,0:T(8,128)S(1)}, u32[]{:S(2)}, u32[]{:S(2)}) collective-permute-start(f32[7,16,128]{2,1,0:T(8,128)S(1)} %shard_map.48.a), channel_id=1, source_target_pairs={{0,24},{1,25},{2,26},{3,27},{4,28},{5,29},{6,30},{7,31},{8,0},{9,1... | collective-permute-start | bytes 172040 | tf_op jit(solution)/shard_map/ppermute | solution.py:260
  14.4 5.7 %collective-permute-start.5 = (f32[7,16,128]{2,1,0:T(8,128)S(1)}, f32[7,16,128]{2,1,0:T(8,128)S(1)}, u32[]{:S(2)}, u32[]{:S(2)}) collective-permute-start(f32[7,16,128]{2,1,0:T(8,128)S(1)} %shard_map.48.a), channel_id=1, source_target_pairs={{0,16},{1,17},{2,18},{3,19},{4,20},{5,21},{6,22},{7,23},{8,24},{9,... | collective-permute-start | bytes 172040 | tf_op jit(solution)/shard_map/ppermute | solution.py:260
  15.7 4.9 %collective-permute-start.4 = (f32[7,16,128]{2,1,0:T(8,128)S(1)}, f32[7,16,128]{2,1,0:T(8,128)S(1)}, u32[]{:S(2)}, u32[]{:S(2)}) collective-permute-start(f32[7,16,128]{2,1,0:T(8,128)S(1)} %shard_map.48.a), channel_id=1, source_target_pairs={{0,8},{1,9},{2,10},{3,11},{4,12},{5,13},{6,14},{7,15},{8,16},{9,17... | collective-permute-start | bytes 172040 | tf_op jit(solution)/shard_map/ppermute | solution.py:260
  20.6 4.5 %collective-permute-start.9 = (f32[7,16,128]{2,1,0:T(8,128)S(1)}, f32[7,16,128]{2,1,0:T(8,128)S(1)}, u32[]{:S(2)}, u32[]{:S(2)}) collective-permute-start(f32[7,16,128]{2,1,0:T(8,128)S(1)} %shard_map.49.p0), channel_id=1, source_target_pairs={{0,6},{1,7},{2,0},{3,1},{4,2},{5,3},{6,4},{7,5},{8,14},{9,15},{10,... | collective-permute-start | bytes 172040 | tf_op jit(solution)/shard_map/ppermute | solution.py:260
  23.3 5.8 %collective-permute-start.8 = (f32[7,16,128]{2,1,0:T(8,128)S(1)}, f32[7,16,128]{2,1,0:T(8,128)S(1)}, u32[]{:S(2)}, u32[]{:S(2)}) collective-permute-start(f32[7,16,128]{2,1,0:T(8,128)S(1)} %shard_map.49.p0), channel_id=1, source_target_pairs={{0,4},{1,5},{2,6},{3,7},{4,0},{5,1},{6,2},{7,3},{8,12},{9,13},{10,... | collective-permute-start | bytes 172040 | tf_op jit(solution)/shard_map/ppermute | solution.py:260
  23.3 6.0 %collective-permute-start.7 = (f32[7,16,128]{2,1,0:T(8,128)S(1)}, f32[7,16,128]{2,1,0:T(8,128)S(1)}, u32[]{:S(2)}, u32[]{:S(2)}) collective-permute-start(f32[7,16,128]{2,1,0:T(8,128)S(1)} %shard_map.49.p0), channel_id=1, source_target_pairs={{0,2},{1,3},{2,4},{3,5},{4,6},{5,7},{6,0},{7,1},{8,10},{9,11},{10,... | collective-permute-start | bytes 172040 | tf_op jit(solution)/shard_map/ppermute | solution.py:260
  24.2 5.4 %collective-permute-start.10 = (f32[7,16,128]{2,1,0:T(8,128)S(1)}, f32[7,16,128]{2,1,0:T(8,128)S(1)}, u32[]{:S(2)}, u32[]{:S(2)}) collective-permute-start(f32[7,16,128]{2,1,0:T(8,128)S(1)} %shard_map.49.p0), channel_id=1, source_target_pairs={{0,1},{1,0},{2,3},{3,2},{4,5},{5,4},{6,7},{7,6},{8,9},{9,8},{10,11... | collective-permute-start | bytes 172040 | tf_op jit(solution)/shard_map/ppermute | solution.py:260
  25.1 4.5 %collective-permute-start.13 = (f32[7,16,128]{2,1,0:T(8,128)S(1)}, f32[7,16,128]{2,1,0:T(8,128)S(1)}, u32[]{:S(2)}, u32[]{:S(2)}) collective-permute-start(f32[7,16,128]{2,1,0:T(8,128)S(1)} %collective-permute-done.9.p3), channel_id=1, source_target_pairs={{0,1},{1,0},{2,3},{3,2},{4,5},{5,4},{6,7},{7,6},{8,9},{9,8},{10,11... | collective-permute-start | bytes 172040 | tf_op jit(solution)/shard_map/ppermute | solution.py:260
  29.1 1.2 %collective-permute-start.12 = (f32[7,16,128]{2,1,0:T(8,128)S(1)}, f32[7,16,128]{2,1,0:T(8,128)S(1)}, u32[]{:S(2)}, u32[]{:S(2)}) collective-permute-start(f32[7,16,128]{2,1,0:T(8,128)S(1)} %collective-permute-done.8.p2), channel_id=1, source_target_pairs={{0,1},{1,0},{2,3},{3,2},{4,5},{5,4},{6,7},{7,6},{8,9},{9,8},{10,11... | collective-permute-start | bytes 172040 | tf_op jit(solution)/shard_map/ppermute | solution.py:260
  29.3 1.2 %collective-permute-start.11 = (f32[7,16,128]{2,1,0:T(8,128)S(1)}, f32[7,16,128]{2,1,0:T(8,128)S(1)}, u32[]{:S(2)}, u32[]{:S(2)}) collective-permute-start(f32[7,16,128]{2,1,0:T(8,128)S(1)} %collective-permute-done.7.p1), channel_id=1, source_target_pairs={{0,1},{1,0},{2,3},{3,2},{4,5},{5,4},{6,7},{7,6},{8,9},{9,8},{10,11... | collective-permute-start | bytes 172040 | tf_op jit(solution)/shard_map/ppermute | solution.py:260
  33.0 6.4 %collective-permute-start.14 = (f32[4,8,1024]{2,1,0:T(8,128)S(1)}, f32[4,8,1024]{2,1,0:T(8,128)S(1)}, u32[]{:S(2)}, u32[]{:S(2)}) collective-permute-start(f32[4,8,1024]{2,1,0:T(8,128)S(1)} %get-tuple-element.37), channel_id=1, source_target_pairs={{0,32},{32,0},{64,96},{96,64},{128,160},{160,128},{192,224},{224,1... | collective-permute-start | bytes 393224 | tf_op jit(solution)/shard_map/ppermute | solution.py:303
  35.0 8.2 %collective-permute-start.17 = (f32[3,16,1024]{2,1,0:T(8,128)S(1)}, f32[3,16,1024]{2,1,0:T(8,128)S(1)}, u32[]{:S(2)}, u32[]{:S(2)}) collective-permute-start(f32[3,16,1024]{2,1,0:T(8,128)S(1)} %get-tuple-element.45), channel_id=1, source_target_pairs={{0,32},{32,0},{64,96},{96,64},{128,160},{160,128},{192,224},{224,1... | collective-permute-start | bytes 589832 | tf_op jit(solution)/shard_map/ppermute | solution.py:303
  39.6 4.4 %collective-permute-start.16 = (f32[4,8,1024]{2,1,0:T(8,128)S(1)}, f32[4,8,1024]{2,1,0:T(8,128)S(1)}, u32[]{:S(2)}, u32[]{:S(2)}) collective-permute-start(f32[4,8,1024]{2,1,0:T(8,128)S(1)} %get-tuple-element.44), channel_id=1, source_target_pairs={{32,64},{192,160},{33,65},{193,161},{34,66},{194,162},{35,67},{195... | collective-permute-start | bytes 393224 | tf_op jit(solution)/shard_map/ppermute | solution.py:319
  40.3 3.7 %collective-permute-start.15 = (f32[4,8,1024]{2,1,0:T(8,128)S(1)}, f32[4,8,1024]{2,1,0:T(8,128)S(1)}, u32[]{:S(2)}, u32[]{:S(2)}) collective-permute-start(f32[4,8,1024]{2,1,0:T(8,128)S(1)} %get-tuple-element.44), channel_id=1, source_target_pairs={{32,96},{192,128},{33,97},{193,129},{34,98},{194,130},{35,99},{195... | collective-permute-start | bytes 393224 | tf_op jit(solution)/shard_map/ppermute | solution.py:318
  44.4 1.4 %collective-permute-start.19 = (f32[4,8,1024]{2,1,0:T(8,128)S(1)}, f32[4,8,1024]{2,1,0:T(8,128)S(1)}, u32[]{:S(2)}, u32[]{:S(2)}) collective-permute-start(f32[4,8,1024]{2,1,0:T(8,128)S(1)} %get-tuple-element.53), channel_id=1, source_target_pairs={{96,128},{128,96},{97,129},{129,97},{98,130},{130,98},{99,131},{13... | collective-permute-start | bytes 393224 | tf_op jit(solution)/shard_map/ppermute | solution.py:319
  45.0 0.7 collective-permute-start.18
  46.7 2.0 %collective-permute-start.21 = (f32[4,8,1024]{2,1,0:T(8,128)S(1)}, f32[4,8,1024]{2,1,0:T(8,128)S(1)}, u32[]{:S(2)}, u32[]{:S(2)}) collective-permute-start(f32[4,8,1024]{2,1,0:T(8,128)S(1)} %get-tuple-element.54), channel_id=1, source_target_pairs={{160,192},{64,32},{161,193},{65,33},{162,194},{66,34},{163,195},{6... | collective-permute-start | bytes 393224 | tf_op jit(solution)/shard_map/ppermute | solution.py:319
  47.4 32.4 %collective-permute-start.20 = (f32[4,8,1024]{2,1,0:T(8,128)S(1)}, f32[4,8,1024]{2,1,0:T(8,128)S(1)}, u32[]{:S(2)}, u32[]{:S(2)}) collective-permute-start(f32[4,8,1024]{2,1,0:T(8,128)S(1)} %get-tuple-element.54), channel_id=1, source_target_pairs={{160,224},{64,0},{161,225},{65,1},{162,226},{66,2},{163,227},{67,3... | collective-permute-start | bytes 393224 | tf_op jit(solution)/shard_map/ppermute | solution.py:318
where the time goes:
time: 87.8 us; the launch traced here: 86.7 us
  waiting for transfers between devices  49.7 us (57%)
  starting transfers between devices  20.4 us (23%)
  Pallas kernels  13.8 us (16%)
  local copies, waits for them, and re-layouts  2.59 us (3%)
    ppermute x3, waiting for transfers between devices, shards(): lax.ppermute(leaving, 'rows', [(2 * t + 1, 2 * t + 3), (6 - 2 * t, 4 - 2...  31.1 us
    ppermute x14, starting transfers between devices, chan_shift(): return lax.ppermute(value, 'chan', [(i, target(i)) for i in range(32)])  13.7 us
    ppermute x14, waiting for transfers between devices, chan_shift(): return lax.ppermute(value, 'chan', [(i, target(i)) for i in range(32)])  13.3 us
    pallas_call x10, Pallas kernels, call(): pl.pallas_call(kernel, out_shape=outs, in_specs=[VMEM] * len(args), out_s...  12.9 us
    ppermute x2, waiting for transfers between devices, swapped(): return lax.ppermute(value, 'rows', [(p, p ^ 1) for p in range(8)])  5.37 us
    ppermute x3, starting transfers between devices, shards(): lax.ppermute(leaving, 'rows', [(2 * t + 1, 2 * t + 3), (6 - 2 * t, 4 - 2...  2.63 us
    unnamed x10, local copies, waits for them, and re-layouts  2.59 us
    ppermute x2, starting transfers between devices, swapped(): return lax.ppermute(value, 'rows', [(p, p ^ 1) for p in range(8)])  2.11 us
  transfers between devices with their start and end apart: 22, of which 14 were waited for; matrix products, arithmetic and copies ran while one was open for 0% of the time, Pallas kernels for 3%

commit v1 on v0

--- a/solution.py
+++ b/solution.py
@@ -1,3 +1,5 @@
+import functools
+
 import jax
 import jax.numpy as jnp
 from jax import lax
@@ -8,6 +10,7 @@
 CHANNELS = 1024
 EPSILON = 1e-05
 LANES = 128
+UNROLL = 16
 SLOTS = 7
 
 VMEM = pl.BlockSpec(memory_space=pltpu.VMEM)
@@ -38,34 +41,43 @@
     return pl.ds(pl.multiple_of((core * 4 + (x & 3)) * LANES, LANES), LANES)
 
 
-def project(feats, gain, weight, keep, send, wide):
+def project(feats_in, gain_in, weight_in, keep, send, feats, gain, weight, wide, sems):
     core, x = place()
     rows, chans, _ = feats.shape
+    order = [(half, s, lane_tile(core ^ half, x + s)) for half in (1, 0) for s in range(4)]
+    sources = [(gain_in, gain), (weight_in, weight)]
+    sources += [(feats_in.at[:, :, at], feats.at[:, :, at]) for _, _, at in order]
+    copies = [pltpu.make_async_copy(a, b, sems.at[k]) for k, (a, b) in enumerate(sources)]
+    for copy in copies:
+        copy.start()
+    copies[0].wait()
+    copies[1].wait()
     w, g = weight[...], gain[...]
     picked = [w[0:1] - w[1:2], w[2:3] - w[1:2], w[6:7], w[3:4] - w[4:5], w[5:6] - w[4:5], w[7:8]]
     scaled = [p * g for p in picked]
     depth = rows * chans
     spot = lax.broadcasted_iota(jnp.int32, (chans, depth), 1) % chans
-    copies = (spot == lax.broadcasted_iota(jnp.int32, (chans, depth), 0)).astype(jnp.bfloat16)
+    picks = (spot == lax.broadcasted_iota(jnp.int32, (chans, depth), 0)).astype(jnp.bfloat16)
     band = lax.broadcasted_iota(jnp.int32, (rows, depth), 1) // chans
     own = band == lax.broadcasted_iota(jnp.int32, (rows, depth), 0)
     rest = jnp.concatenate(scaled + scaled[:2], axis=0)
     for part in range(3):
         head = rest.astype(jnp.bfloat16)
         rest = rest - head.astype(jnp.float32)
-        spread_out = jnp.dot(head, copies, preferred_element_type=jnp.float32)
+        spread_out = jnp.dot(head, picks, preferred_element_type=jnp.float32)
         for j in range(6):
             row = jnp.broadcast_to(spread_out[j : j + 1], (rows, depth))
             at = (part * 6 + j) * rows
             wide[at : at + rows] = jnp.where(own, row, 0.0).astype(jnp.bfloat16)
-    for half, out in ((0, keep), (1, send)):
-        for s in range(4):
-            block = feats[:, :, lane_tile(core ^ half, x + s)]
-            sums = jnp.dot(wide[...], block.reshape(depth, LANES), preferred_element_type=jnp.float32)
-            sums = sums[0 : 6 * rows] + sums[6 * rows : 12 * rows] + sums[12 * rows :]
-            out[s, 0:6] = sums.reshape(6, rows, LANES)
-            values = block.astype(jnp.float32)
-            out[s, 6] = jnp.sum(values * values, axis=1)
+    for (half, s, at), copy in zip(order, copies[2:]):
+        copy.wait()
+        out = send if half else keep
+        block = feats[:, :, at]
+        sums = jnp.dot(wide[...], block.reshape(depth, LANES), preferred_element_type=jnp.float32)
+        sums = sums[0 : 6 * rows] + sums[6 * rows : 12 * rows] + sums[12 * rows :]
+        out[s, 0:6] = sums.reshape(6, rows, LANES)
+        values = block.astype(jnp.float32)
+        out[s, 6] = jnp.sum(values * values, axis=1)
 
 
 def join_cores(keep, arrived, *outs):
@@ -163,7 +175,7 @@
         kept[h] = state
         return state
 
-    end[...] = lax.fori_loop(0, rows, step, jnp.zeros(end.shape, jnp.float32))
+    end[...] = lax.fori_loop(0, rows, step, jnp.zeros(end.shape, jnp.float32), unroll=2)
 
 
 def far_side(far_gate, inverse, feats, gain, bias, decay, drive):
@@ -201,59 +213,66 @@
             emit(h, state)
         return state
 
-    return lax.fori_loop(0, rows, step, state)
-
-
-def turns(stage):
+    return lax.fori_loop(0, rows, step, state, unroll=UNROLL)
+
+
+def turn():
     position = lax.axis_index("rows")
     pair, odd = position >> 1, position & 1
-    last = 3 - pair
-    far = jnp.where(odd == 1, pair, last)
-    return odd, far == stage, 3 - far == stage
-
-
-def first_stage(partner_end, decay, drive, taps, kept_in, kept, leaving):
-    odd, far, _ = turns(0)
+    return odd, jnp.where(odd == 1, pair, 3 - pair)
+
+
+def far_stage(stage, *refs):
+    arrived, partner_end = refs[0], refs[1]
+    if stage:
+        pd, pt, refs = refs[2], refs[3], refs[4:]
+    else:
+        refs = refs[1:]
+    if stage:
+        fd, fq, ft, kept_in, leaving_in, kept, leaving = refs
+    else:
+        fd, fq, ft, kept_in, kept, leaving = refs[1:]
+    odd, when = turn()
 
     def emit(h, state):
         kept[h] = state
 
-    @pl.when(far)
+    @pl.when(when == stage)
     def _():
-        leaving[...] = scan_rows(partner_end[...], odd == 0, decay, drive, taps, emit)
-
-    @pl.when(jnp.logical_not(far))
+        state = arrived[...]
+        if stage:
+            state = scan_rows(state, odd == 0, pd, None, pt, None) + partner_end[...]
+        leaving[...] = scan_rows(state, odd == 0, fd, fq, ft, emit)
+
+    @pl.when(when != stage)
     def _():
         kept[...] = kept_in[...]
-
-
-def later_stage(stage, final, *refs):
-    if final:
-        kept, refs = refs[0], refs[1:]
-    far_in, near_in, partner_end, pd, pt, nd, nq, nt, fd, fq, ft = refs[:11]
-    *before, out, leaving = refs[11:]
-    odd, far, near = turns(stage)
+        if stage:
+            leaving[...] = leaving_in[...]
+
+
+def last_stage(near_in, far_in, partner_end, pd, pt, fd, fq, ft, nd, nq, nt, kept, out, held, sems):
+    odd, when = turn()
+    rows = held.shape[0]
+
+    def copy(h):
+        return pltpu.make_async_copy(held.at[h], out.at[h], sems.at[h])
 
     def emit(h, state):
-        if final:
-            out[h] = (kept[h] * state).reshape(out.shape[1:]).astype(out.dtype)
-        else:
-            out[h] = state
-
-    @pl.when(far)
+        held[h] = (kept[h] * state).reshape(held.shape[1:]).astype(held.dtype)
+        copy(h).start()
+
+    @pl.when(when == 3)
     def _():
         state = scan_rows(far_in[...], odd == 0, pd, None, pt, None) + partner_end[...]
-        leaving[...] = scan_rows(state, odd == 0, fd, fq, ft, emit)
-
-    @pl.when(near)
+        scan_rows(state, odd == 0, fd, fq, ft, emit)
+
+    @pl.when(when != 3)
     def _():
-        leaving[...] = scan_rows(near_in[...], odd == 1, nd, nq, nt, emit)
-
-    if before:
-
-        @pl.when(jnp.logical_not(far | near))
-        def _():
-            out[...] = before[0][...]
+        scan_rows(near_in[...], odd == 1, nd, nq, nt, emit)
+
+    for h in range(rows):
+        copy(h).wait()
 
 
 def chan_shift(value, target):
@@ -280,11 +299,17 @@
     keep, send = pl.pallas_call(
         project,
         out_shape=(half, half),
-        in_specs=[VMEM] * 3,
+        in_specs=[pl.BlockSpec(memory_space=pltpu.HBM)] * 3,
         out_specs=(VMEM, VMEM),
-        scratch_shapes=[pltpu.VMEM((18 * rows, rows * chans), jnp.bfloat16)],
+        scratch_shapes=[
+            pltpu.VMEM(feats.shape, feats.dtype),
+            pltpu.VMEM(gain.shape, gain.dtype),
+            pltpu.VMEM(proj_weight.shape, proj_weight.dtype),
+            pltpu.VMEM((18 * rows, rows * chans), jnp.bfloat16),
+            pltpu.SemaphoreType.DMA((10,)),
+        ],
         compiler_params=pltpu.CompilerParams(vmem_limit_bytes=40 << 20),
-    )(feats, gain, proj_weight)
+    )(*(pltpu.with_memory_space_constraint(v, pltpu.HBM) for v in (feats, gain, proj_weight)))
     mine, *others = call(join_cores, (piece,) * 4, keep, other_core(send))
     part = call(join_x, piece, mine, *(along_x(v, s + 1) for s, v in enumerate(others)))
     whole = call(join_y, piece, part, *(along_y(part, s) for s in (1, 2, 3)))
@@ -299,37 +324,36 @@
         near_side, (taps, taps, line, line, taps, block, block, block, state), *pieces, feats, gain, bias
     )
 
-    def swapped(value):
-        return lax.ppermute(value, "rows", [(p, p ^ 1) for p in range(8)])
-
-    partner_end = swapped(end)
-    partner_raw = swapped(raw)
+    def along_rows(value, pairs):
+        return lax.ppermute(value, "rows", pairs)
+
+    swap = [(p, p ^ 1) for p in range(8)]
+    partner_end = along_rows(end, swap)
     far_decay, far_drive = call(far_side, (block, block), far_gate, inverse, feats, gain, bias)
+    far = (far_decay, far_drive, far_taps)
+    partner_raw = along_rows(raw, swap)
     kept, leaving = call(
-        first_stage, (block, state), partner_end, far_decay, far_drive, far_taps, kept, aliases={4: 0}
+        functools.partial(far_stage, 0), (block, state), partner_end, partner_end, *far, kept, aliases={5: 0}
     )
     partner_taps, partner_decay = call(partner_side, (taps, block), partner_raw, bias)
-    shared = (
-        partner_end, partner_decay, partner_taps, near_decay, near_drive, near_taps, far_decay, far_drive, far_taps,
-    )
-    out = None
-    for stage in (1, 2, 3):
+    partner = (partner_end, partner_decay, partner_taps)
+    for stage in (1, 2):
         t = stage - 1
-        far_in = lax.ppermute(leaving, "rows", [(2 * t + 1, 2 * t + 3), (6 - 2 * t, 4 - 2 * t)])
-        near_in = lax.ppermute(leaving, "rows", [(2 * t + 1, 2 * t + 2), (6 - 2 * t, 5 - 2 * t)])
-
-        def kernel(*refs, stage=stage):
-            later_stage(stage, stage > 1, *refs)
-
-        args = (far_in, near_in, *shared)
-        if stage == 1:
-            kept, leaving = call(kernel, (block, state), *args, kept, aliases={11: 0})
-        elif stage == 2:
-            made = jax.ShapeDtypeStruct(feats.shape, jnp.bfloat16)
-            out, leaving = call(kernel, (made, state), kept, *args)
-        else:
-            out, _ = call(kernel, (made, state), kept, *args, out, aliases={12: 0})
-    return out
+        arrived = along_rows(leaving, [(2 * t + 1, 2 * t + 3), (6 - 2 * t, 4 - 2 * t)])
+        kept, leaving = call(
+            functools.partial(far_stage, stage), (block, state), arrived, *partner, *far, kept, leaving,
+            aliases={7: 0, 8: 1},
+        )
+    near_in = along_rows(leaving, [(1, 2), (2, 1), (3, 4), (4, 3), (5, 6), (6, 5)])
+    far_in = along_rows(leaving, [(5, 7), (2, 0)])
+    return pl.pallas_call(
+        last_stage,
+        out_shape=jax.ShapeDtypeStruct(feats.shape, jnp.bfloat16),
+        in_specs=[VMEM] * 12,
+        out_specs=pl.BlockSpec(memory_space=pl.ANY),
+        scratch_shapes=[pltpu.VMEM(feats.shape, jnp.bfloat16), pltpu.SemaphoreType.DMA((rows,))],
+        compiler_params=pltpu.CompilerParams(vmem_limit_bytes=40 << 20),
+    )(near_in, far_in, *partner, *far, near_decay, near_drive, near_taps, kept)
 
 
 def solution(mesh):

time: 87.8 us -> 76.8 us (0.87)
  waiting for transfers between devices: 49.7 us -> 42.7 us
  local copies, waits for them, and re-layouts: 2.59 us -> 0.01 us
  starting transfers between devices: 20.4 us -> 19.1 us
    pallas_call x10 -> x9, Pallas kernels: 12.9 us -> 5.12 us  [call(): pl.pallas_call(kernel, out_shape=outs, in_specs=[VMEM] * len(args), out_s...]
    pallas_call x1 -> x2, Pallas kernels: 0.89 us -> 7.95 us  [the longest x1 4.39 us: shards(): pl.pallas_call(last_stage, out_shape=jax.ShapeDtypeStruct(feats.shape, jn...]
    ppermute x8 -> x6, waiting for transfers between devices: 36.4 us -> 29.5 us  [along_rows(): return lax.ppermute(value, 'rows', pairs)]
    unnamed x10 -> x6, local copies, waits for them, and re-layouts: 2.59 us -> 0.01 us
    ppermute x8 -> x6, starting transfers between devices: 6.74 us -> 5.41 us  [along_rows(): return lax.ppermute(value, 'rows', pairs)]
  transfers between devices with their start and end apart: 22 -> 20, of which waited for: 14 -> 14; matrix products, arithmetic and copies ran while one was open for 0% -> 0% of each run, Pallas kernels for 3% -> 3%
where the time goes in v1:
time: 76.8 us; the launch traced here: 75.2 us
  waiting for transfers between devices  42.7 us (56%)
  starting transfers between devices  19.1 us (25%)
  Pallas kernels  13.1 us (17%)
    ppermute x6, waiting for transfers between devices, along_rows(): return lax.ppermute(value, 'rows', pairs)  29.5 us
    ppermute x14, starting transfers between devices, chan_shift(): return lax.ppermute(value, 'chan', [(i, target(i)) for i in range(32)])  13.7 us
    ppermute x14, waiting for transfers between devices, chan_shift(): return lax.ppermute(value, 'chan', [(i, target(i)) for i in range(32)])  13.2 us
    ppermute x6, starting transfers between devices, along_rows(): return lax.ppermute(value, 'rows', pairs)  5.41 us
    pallas_call x9, Pallas kernels, call(): pl.pallas_call(kernel, out_shape=outs, in_specs=[VMEM] * len(args), out_s...  5.12 us
    pallas_call x1, Pallas kernels, shards(): pl.pallas_call(last_stage, out_shape=jax.ShapeDtypeStruct(feats.shape, jn...  4.39 us
    pallas_call x1, Pallas kernels, shards(): pl.pallas_call(project, out_shape=(half, half), in_specs=[pl.BlockSpec(me...  3.55 us
  transfers between devices with their start and end apart: 20, of which 14 were waited for; matrix products, arithmetic and copies ran while one was open for 0% of the time, Pallas kernels for 3%

profile of v1, /device:TPU:24, one launch (start us, length us, event | category | flops | bytes accessed | tf_op | source)
XLA Modules:
  0.0 75.2 jit_solution(9704436033834427785)
XLA Ops:
  0.0 3.6 %shard_map.46 = (f32[4,7,16,128]{3,2,1,0:T(8,128)S(1)}, f32[4,7,16,128]{3,2,1,0:T(8,128)S(1)}) custom-call(bf16[16,32,1024]{2,1,0:T(8,128)(2,1)} %feats.3, f32[1,32]{1,0:T(1,128)} %bitcast.2, f32[8,32]{1,0:T(8,128)} %weight_in.1), custom_call_target="tpu_custom_call" | custom-call | tf_op jit(solution)/shard_map/pallas_call | solution.py:299
  3.7 1.5 %collective-permute-done.arrived = f32[4,7,16,128]{3,2,1,0:T(8,128)S(1)} collective-permute-done((f32[4,7,16,128]{3,2,1,0:T(8,128)S(1)}, f32[4,7,16,128]{3,2,1,0:T(8,128)S(1)}, u32[]{:S(2)}, u32[]{:S(2)}) %collective-permute-start) | collective-permute-done | bytes 229408 | tf_op jit(solution)/shard_map/ppermute | solution.py:279
  5.2 1.6 %collective-permute-start.1 = (f32[7,16,128]{2,1,0:T(8,128)S(1)}, f32[7,16,128]{2,1,0:T(8,128)S(1)}, u32[]{:S(2)}, u32[]{:S(2)}) collective-permute-start(f32[7,16,128]{2,1,0:T(8,128)S(1)} %get-tuple-element.33), channel_id=1, source_target_pairs={{0,2},{1,3},{2,4},{3,5},{4,6},{5,7},{6,0},{7,1},{8,10},{9,11},{10,... | collective-permute-start | bytes 172040 | tf_op jit(solution)/shard_map/ppermute | solution.py:279
  6.7 2.7 %collective-permute-start.2 = (f32[7,16,128]{2,1,0:T(8,128)S(1)}, f32[7,16,128]{2,1,0:T(8,128)S(1)}, u32[]{:S(2)}, u32[]{:S(2)}) collective-permute-start(f32[7,16,128]{2,1,0:T(8,128)S(1)} %get-tuple-element.34), channel_id=1, source_target_pairs={{0,4},{1,5},{2,6},{3,7},{4,0},{5,1},{6,2},{7,3},{8,12},{9,13},{10,... | collective-permute-start | bytes 172040 | tf_op jit(solution)/shard_map/ppermute | solution.py:279
  9.5 1.4 %collective-permute-start.3 = (f32[7,16,128]{2,1,0:T(8,128)S(1)}, f32[7,16,128]{2,1,0:T(8,128)S(1)}, u32[]{:S(2)}, u32[]{:S(2)}) collective-permute-start(f32[7,16,128]{2,1,0:T(8,128)S(1)} %get-tuple-element.35), channel_id=1, source_target_pairs={{0,6},{1,7},{2,0},{3,1},{4,2},{5,3},{6,4},{7,5},{8,14},{9,15},{10,... | collective-permute-start | bytes 172040 | tf_op jit(solution)/shard_map/ppermute | solution.py:279
  10.9 1.7 %collective-permute-done.2.c = f32[7,16,128]{2,1,0:T(8,128)S(1)} collective-permute-done((f32[7,16,128]{2,1,0:T(8,128)S(1)}, f32[7,16,128]{2,1,0:T(8,128)S(1)}, u32[]{:S(2)}, u32[]{:S(2)}) %collective-permute-start.2) | collective-permute-done | bytes 57376 | tf_op jit(solution)/shard_map/ppermute | solution.py:279
  12.6 1.0 %collective-permute-done.3.d = f32[7,16,128]{2,1,0:T(8,128)S(1)} collective-permute-done((f32[7,16,128]{2,1,0:T(8,128)S(1)}, f32[7,16,128]{2,1,0:T(8,128)S(1)}, u32[]{:S(2)}, u32[]{:S(2)}) %collective-permute-start.3) | collective-permute-done | bytes 57376 | tf_op jit(solution)/shard_map/ppermute | solution.py:279
  13.7 0.8 %collective-permute-start.6 = (f32[7,16,128]{2,1,0:T(8,128)S(1)}, f32[7,16,128]{2,1,0:T(8,128)S(1)}, u32[]{:S(2)}, u32[]{:S(2)}) collective-permute-start(f32[7,16,128]{2,1,0:T(8,128)S(1)} %shard_map.48.a), channel_id=1, source_target_pairs={{0,24},{1,25},{2,26},{3,27},{4,28},{5,29},{6,30},{7,31},{8,0},{9,1... | collective-permute-start | bytes 172040 | tf_op jit(solution)/shard_map/ppermute | solution.py:279
  14.5 1.2 %collective-permute-start.5 = (f32[7,16,128]{2,1,0:T(8,128)S(1)}, f32[7,16,128]{2,1,0:T(8,128)S(1)}, u32[]{:S(2)}, u32[]{:S(2)}) collective-permute-start(f32[7,16,128]{2,1,0:T(8,128)S(1)} %shard_map.48.a), channel_id=1, source_target_pairs={{0,16},{1,17},{2,18},{3,19},{4,20},{5,21},{6,22},{7,23},{8,24},{9,... | collective-permute-start | bytes 172040 | tf_op jit(solution)/shard_map/ppermute | solution.py:279
  15.7 1.9 %collective-permute-start.4 = (f32[7,16,128]{2,1,0:T(8,128)S(1)}, f32[7,16,128]{2,1,0:T(8,128)S(1)}, u32[]{:S(2)}, u32[]{:S(2)}) collective-permute-start(f32[7,16,128]{2,1,0:T(8,128)S(1)} %shard_map.48.a), channel_id=1, source_target_pairs={{0,8},{1,9},{2,10},{3,11},{4,12},{5,13},{6,14},{7,15},{8,16},{9,17... | collective-permute-start | bytes 172040 | tf_op jit(solution)/shard_map/ppermute | solution.py:279
  17.6 1.5 %collective-permute-done.6.d = f32[7,16,128]{2,1,0:T(8,128)S(1)} collective-permute-done((f32[7,16,128]{2,1,0:T(8,128)S(1)}, f32[7,16,128]{2,1,0:T(8,128)S(1)}, u32[]{:S(2)}, u32[]{:S(2)}) %collective-permute-start.6) | collective-permute-done | bytes 57376 | tf_op jit(solution)/shard_map/ppermute | solution.py:279
  19.1 1.0 %collective-permute-done.5.c = f32[7,16,128]{2,1,0:T(8,128)S(1)} collective-permute-done((f32[7,16,128]{2,1,0:T(8,128)S(1)}, f32[7,16,128]{2,1,0:T(8,128)S(1)}, u32[]{:S(2)}, u32[]{:S(2)}) %collective-permute-start.5) | collective-permute-done | bytes 57376 | tf_op jit(solution)/shard_map/ppermute | solution.py:279
  20.2 0.4 collective-permute-done.4.b
  20.6 2.7 %collective-permute-start.9 = (f32[7,16,128]{2,1,0:T(8,128)S(1)}, f32[7,16,128]{2,1,0:T(8,128)S(1)}, u32[]{:S(2)}, u32[]{:S(2)}) collective-permute-start(f32[7,16,128]{2,1,0:T(8,128)S(1)} %shard_map.49.p0), channel_id=1, source_target_pairs={{0,6},{1,7},{2,0},{3,1},{4,2},{5,3},{6,4},{7,5},{8,14},{9,15},{10,... | collective-permute-start | bytes 172040 | tf_op jit(solution)/shard_map/ppermute | solution.py:279
  23.4 0.9 %collective-permute-start.7 = (f32[7,16,128]{2,1,0:T(8,128)S(1)}, f32[7,16,128]{2,1,0:T(8,128)S(1)}, u32[]{:S(2)}, u32[]{:S(2)}) collective-permute-start(f32[7,16,128]{2,1,0:T(8,128)S(1)} %shard_map.49.p0), channel_id=1, source_target_pairs={{0,2},{1,3},{2,4},{3,5},{4,6},{5,7},{6,0},{7,1},{8,10},{9,11},{10,... | collective-permute-start | bytes 172040 | tf_op jit(solution)/shard_map/ppermute | solution.py:279
  24.3 0.9 %collective-permute-done.9.p3 = f32[7,16,128]{2,1,0:T(8,128)S(1)} collective-permute-done((f32[7,16,128]{2,1,0:T(8,128)S(1)}, f32[7,16,128]{2,1,0:T(8,128)S(1)}, u32[]{:S(2)}, u32[]{:S(2)}) %collective-permute-start.9) | collective-permute-done | bytes 57376 | tf_op jit(solution)/shard_map/ppermute | solution.py:279
  25.2 4.0 %collective-permute-done.8.p2 = f32[7,16,128]{2,1,0:T(8,128)S(1)} collective-permute-done((f32[7,16,128]{2,1,0:T(8,128)S(1)}, f32[7,16,128]{2,1,0:T(8,128)S(1)}, u32[]{:S(2)}, u32[]{:S(2)}) %collective-permute-start.8) | collective-permute-done | bytes 57376 | tf_op jit(solution)/shard_map/ppermute | solution.py:279
  29.7 0.7 collective-permute-done.12.q2
  30.7 2.2 %shard_map.50 = (f32[3,16,1024]{2,1,0:T(8,128)S(1)}, f32[3,16,1024]{2,1,0:T(8,128)S(1)}, f32[16,1024]{1,0:T(8,128)S(1)}, f32[16,1024]{1,0:T(8,128)S(1)}, f32[3,1...) custom-call(f32[7,16,128]{2,1,0:T(8,128)S(1)} %shard_map.49.p0, ...), custom_call_target="tpu_custom_call" | custom-call | tf_op jit(solution)/shard_map/pallas_call | solution.py:20
  32.9 2.0 %collective-permute-start.14 = (f32[4,8,1024]{2,1,0:T(8,128)S(1)}, f32[4,8,1024]{2,1,0:T(8,128)S(1)}, u32[]{:S(2)}, u32[]{:S(2)}) collective-permute-start(f32[4,8,1024]{2,1,0:T(8,128)S(1)} %get-tuple-element.36), channel_id=1, source_target_pairs={{0,32},{32,0},{64,96},{96,64},{128,160},{160,128},{192,224},{224,1... | collective-permute-start | bytes 393224 | tf_op jit(solution)/shard_map/ppermute | solution.py:328
  35.0 1.0 %shard_map.51 = (f32[16,4,8,1024]{3,2,1,0:T(8,128)S(1)}, f32[16,4,8,1024]{3,2,1,0:T(8,128)S(1)}) custom-call(f32[16,1024]{1,0:T(8,128)S(1)} %get-tuple-element.37.far_gate, f32[16,1024]{1,0:T(8,128)S(1)} %get-tuple-element.38.inverse, bf16[16,32,1024]{2,1,0:T(8,128)(2,1)S(1)} %copy-done, f32[1,32]{1,0:T(1,128)S(1)} %bitcast.4, f32[1,32]{1,0:T(1,128)S(1)} %bitcast.6), custom_call_target="tpu_custom_call" | custom-call | tf_op jit(solution)/shard_map/pallas_call | solution.py:20
  36.0 3.2 %collective-permute-done.14.refs_0_.refs_1_.partner_end = f32[4,8,1024]{2,1,0:T(8,128)S(1)} collective-permute-done((f32[4,8,1024]{2,1,0:T(8,128)S(1)}, f32[4,8,1024]{2,1,0:T(8,128)S(1)}, u32[]{:S(2)}, u32[]{:S(2)}) %collective-permute-start.14) | collective-permute-done | bytes 131104 | tf_op jit(solution)/shard_map/ppermute | solution.py:328
  39.5 0.7 collective-permute-start.15
  40.2 2.8 %collective-permute-done.16.raw = f32[3,16,1024]{2,1,0:T(8,128)S(1)} collective-permute-done((f32[3,16,1024]{2,1,0:T(8,128)S(1)}, f32[3,16,1024]{2,1,0:T(8,128)S(1)}, u32[]{:S(2)}, u32[]{:S(2)}) %collective-permute-start.16) | collective-permute-done | bytes 196640 | tf_op jit(solution)/shard_map/ppermute | solution.py:328
  43.0 0.9 %shard_map.53 = (f32[3,16,1024]{2,1,0:T(8,128)S(1)}, f32[16,4,8,1024]{3,2,1,0:T(8,128)S(1)}) custom-call(f32[3,16,1024]{2,1,0:T(8,128)S(1)} %collective-permute-done.16.raw, f32[1,32]{1,0:T(1,128)S(1)} %bitcast.7), custom_call_target="tpu_custom_call" | custom-call | tf_op jit(solution)/shard_map/pallas_call | solution.py:20
  43.9 0.3 shard_map.54
  44.3 0.7 collective-permute-start.17
  45.0 0.3 shard_map.55
  45.3 1.3 %collective-permute-start.19 = (f32[4,8,1024]{2,1,0:T(8,128)S(1)}, f32[4,8,1024]{2,1,0:T(8,128)S(1)}, u32[]{:S(2)}, u32[]{:S(2)}) collective-permute-start(f32[4,8,1024]{2,1,0:T(8,128)S(1)} %get-tuple-element.50), channel_id=1, source_target_pairs={{160,224},{64,0},{161,225},{65,1},{162,226},{66,2},{163,227},{67,3... | collective-permute-start | bytes 393224 | tf_op jit(solution)/shard_map/ppermute | solution.py:328
  46.6 0.7 collective-permute-start.18
  47.2 23.4 %collective-permute-done.19.far_in = f32[4,8,1024]{2,1,0:T(8,128)S(1)} collective-permute-done((f32[4,8,1024]{2,1,0:T(8,128)S(1)}, f32[4,8,1024]{2,1,0:T(8,128)S(1)}, u32[]{:S(2)}, u32[]{:S(2)}) %collective-permute-start.19) | collective-permute-done | bytes 131104 | tf_op jit(solution)/shard_map/ppermute | solution.py:328
  70.7 4.4 %shard_map.56 = bf16[16,32,1024]{2,1,0:T(8,128)(2,1)} custom-call(f32[4,8,1024]{2,1,0:T(8,128)S(1)} %collective-permute-done.18.near_in, f32[4,8,1024]{2,1,0:T(8,128)S(1)} %collective-permute-done.19.far_in, f32[4,8,1024]{2,1,0:T(8,128)S(1)} %collective-permute-done.14.refs_0_.refs_1_.partner_end, f32[16,4,8,1024]{3,2,1,0:T(8,128)S(1)} %get-tuple-element.45.refs_2_.pd, ...), custom_call_target="tpu_custom_call" | custom-call | tf_op jit(solution)/shard_map/pallas_call | solution.py:349
  (25 shorter events, 1.4 us)
Async XLA Ops:
  0.0 30.7 %copy-start = (bf16[16,32,1024]{2,1,0:T(8,128)(2,1)S(1)}, bf16[16,32,1024]{2,1,0:T(8,128)(2,1)}, u32[]{:S(2)}) copy-start(bf16[16,32,1024]{2,1,0:T(8,128)(2,1)} %feats.3) | copy-start | bytes 3145732
  0.0 30.7 %copy-start.1 = (f32[32]{0:T(128)S(1)}, f32[32]{0:T(128)}, u32[]{:S(2)}) copy-start(f32[32]{0:T(128)} %param.5) | copy-start | bytes 388
  0.0 30.7 %copy-start.2 = (f32[32]{0:T(128)S(1)}, f32[32]{0:T(128)}, u32[]{:S(2)}) copy-start(f32[32]{0:T(128)} %param.7) | copy-start | bytes 388
  3.6 1.6 %collective-permute-start = (f32[4,7,16,128]{3,2,1,0:T(8,128)S(1)}, f32[4,7,16,128]{3,2,1,0:T(8,128)S(1)}, u32[]{:S(2)}, u32[]{:S(2)}) collective-permute-start(f32[4,7,16,128]{3,2,1,0:T(8,128)S(1)} %get-tuple-element.31), channel_id=1, source_target_pairs={{0,1},{1,0},{2,3},{3,2},{4,5},{5,4},{6,7},{7,6},{8,9},{9,8},{10,11... | collective-permute-start | bytes 688136 | tf_op jit(solution)/shard_map/ppermute | solution.py:279
  5.2 5.7 %collective-permute-start.1 = (f32[7,16,128]{2,1,0:T(8,128)S(1)}, f32[7,16,128]{2,1,0:T(8,128)S(1)}, u32[]{:S(2)}, u32[]{:S(2)}) collective-permute-start(f32[7,16,128]{2,1,0:T(8,128)S(1)} %get-tuple-element.33), channel_id=1, source_target_pairs={{0,2},{1,3},{2,4},{3,5},{4,6},{5,7},{6,0},{7,1},{8,10},{9,11},{10,... | collective-permute-start | bytes 172040 | tf_op jit(solution)/shard_map/ppermute | solution.py:279
  6.7 5.9 %collective-permute-start.2 = (f32[7,16,128]{2,1,0:T(8,128)S(1)}, f32[7,16,128]{2,1,0:T(8,128)S(1)}, u32[]{:S(2)}, u32[]{:S(2)}) collective-permute-start(f32[7,16,128]{2,1,0:T(8,128)S(1)} %get-tuple-element.34), channel_id=1, source_target_pairs={{0,4},{1,5},{2,6},{3,7},{4,0},{5,1},{6,2},{7,3},{8,12},{9,13},{10,... | collective-permute-start | bytes 172040 | tf_op jit(solution)/shard_map/ppermute | solution.py:279
  9.5 4.2 %collective-permute-start.3 = (f32[7,16,128]{2,1,0:T(8,128)S(1)}, f32[7,16,128]{2,1,0:T(8,128)S(1)}, u32[]{:S(2)}, u32[]{:S(2)}) collective-permute-start(f32[7,16,128]{2,1,0:T(8,128)S(1)} %get-tuple-element.35), channel_id=1, source_target_pairs={{0,6},{1,7},{2,0},{3,1},{4,2},{5,3},{6,4},{7,5},{8,14},{9,15},{10,... | collective-permute-start | bytes 172040 | tf_op jit(solution)/shard_map/ppermute | solution.py:279
  13.7 5.5 %collective-permute-start.6 = (f32[7,16,128]{2,1,0:T(8,128)S(1)}, f32[7,16,128]{2,1,0:T(8,128)S(1)}, u32[]{:S(2)}, u32[]{:S(2)}) collective-permute-start(f32[7,16,128]{2,1,0:T(8,128)S(1)} %shard_map.48.a), channel_id=1, source_target_pairs={{0,24},{1,25},{2,26},{3,27},{4,28},{5,29},{6,30},{7,31},{8,0},{9,1... | collective-permute-start | bytes 172040 | tf_op jit(solution)/shard_map/ppermute | solution.py:279
  14.5 5.7 %collective-permute-start.5 = (f32[7,16,128]{2,1,0:T(8,128)S(1)}, f32[7,16,128]{2,1,0:T(8,128)S(1)}, u32[]{:S(2)}, u32[]{:S(2)}) collective-permute-start(f32[7,16,128]{2,1,0:T(8,128)S(1)} %shard_map.48.a), channel_id=1, source_target_pairs={{0,16},{1,17},{2,18},{3,19},{4,20},{5,21},{6,22},{7,23},{8,24},{9,... | collective-permute-start | bytes 172040 | tf_op jit(solution)/shard_map/ppermute | solution.py:279
  15.7 4.9 %collective-permute-start.4 = (f32[7,16,128]{2,1,0:T(8,128)S(1)}, f32[7,16,128]{2,1,0:T(8,128)S(1)}, u32[]{:S(2)}, u32[]{:S(2)}) collective-permute-start(f32[7,16,128]{2,1,0:T(8,128)S(1)} %shard_map.48.a), channel_id=1, source_target_pairs={{0,8},{1,9},{2,10},{3,11},{4,12},{5,13},{6,14},{7,15},{8,16},{9,17... | collective-permute-start | bytes 172040 | tf_op jit(solution)/shard_map/ppermute | solution.py:279
  20.6 4.6 %collective-permute-start.9 = (f32[7,16,128]{2,1,0:T(8,128)S(1)}, f32[7,16,128]{2,1,0:T(8,128)S(1)}, u32[]{:S(2)}, u32[]{:S(2)}) collective-permute-start(f32[7,16,128]{2,1,0:T(8,128)S(1)} %shard_map.49.p0), channel_id=1, source_target_pairs={{0,6},{1,7},{2,0},{3,1},{4,2},{5,3},{6,4},{7,5},{8,14},{9,15},{10,... | collective-permute-start | bytes 172040 | tf_op jit(solution)/shard_map/ppermute | solution.py:279
  23.4 5.8 %collective-permute-start.8 = (f32[7,16,128]{2,1,0:T(8,128)S(1)}, f32[7,16,128]{2,1,0:T(8,128)S(1)}, u32[]{:S(2)}, u32[]{:S(2)}) collective-permute-start(f32[7,16,128]{2,1,0:T(8,128)S(1)} %shard_map.49.p0), channel_id=1, source_target_pairs={{0,4},{1,5},{2,6},{3,7},{4,0},{5,1},{6,2},{7,3},{8,12},{9,13},{10,... | collective-permute-start | bytes 172040 | tf_op jit(solution)/shard_map/ppermute | solution.py:279
  23.4 6.0 %collective-permute-start.7 = (f32[7,16,128]{2,1,0:T(8,128)S(1)}, f32[7,16,128]{2,1,0:T(8,128)S(1)}, u32[]{:S(2)}, u32[]{:S(2)}) collective-permute-start(f32[7,16,128]{2,1,0:T(8,128)S(1)} %shard_map.49.p0), channel_id=1, source_target_pairs={{0,2},{1,3},{2,4},{3,5},{4,6},{5,7},{6,0},{7,1},{8,10},{9,11},{10,... | collective-permute-start | bytes 172040 | tf_op jit(solution)/shard_map/ppermute | solution.py:279
  24.3 5.3 %collective-permute-start.10 = (f32[7,16,128]{2,1,0:T(8,128)S(1)}, f32[7,16,128]{2,1,0:T(8,128)S(1)}, u32[]{:S(2)}, u32[]{:S(2)}) collective-permute-start(f32[7,16,128]{2,1,0:T(8,128)S(1)} %shard_map.49.p0), channel_id=1, source_target_pairs={{0,1},{1,0},{2,3},{3,2},{4,5},{5,4},{6,7},{7,6},{8,9},{9,8},{10,11... | collective-permute-start | bytes 172040 | tf_op jit(solution)/shard_map/ppermute | solution.py:279
  25.2 4.5 %collective-permute-start.13 = (f32[7,16,128]{2,1,0:T(8,128)S(1)}, f32[7,16,128]{2,1,0:T(8,128)S(1)}, u32[]{:S(2)}, u32[]{:S(2)}) collective-permute-start(f32[7,16,128]{2,1,0:T(8,128)S(1)} %collective-permute-done.9.p3), channel_id=1, source_target_pairs={{0,1},{1,0},{2,3},{3,2},{4,5},{5,4},{6,7},{7,6},{8,9},{9,8},{10,11... | collective-permute-start | bytes 172040 | tf_op jit(solution)/shard_map/ppermute | solution.py:279
  29.2 1.2 %collective-permute-start.12 = (f32[7,16,128]{2,1,0:T(8,128)S(1)}, f32[7,16,128]{2,1,0:T(8,128)S(1)}, u32[]{:S(2)}, u32[]{:S(2)}) collective-permute-start(f32[7,16,128]{2,1,0:T(8,128)S(1)} %collective-permute-done.8.p2), channel_id=1, source_target_pairs={{0,1},{1,0},{2,3},{3,2},{4,5},{5,4},{6,7},{7,6},{8,9},{9,8},{10,11... | collective-permute-start | bytes 172040 | tf_op jit(solution)/shard_map/ppermute | solution.py:279
  29.4 1.2 %collective-permute-start.11 = (f32[7,16,128]{2,1,0:T(8,128)S(1)}, f32[7,16,128]{2,1,0:T(8,128)S(1)}, u32[]{:S(2)}, u32[]{:S(2)}) collective-permute-start(f32[7,16,128]{2,1,0:T(8,128)S(1)} %collective-permute-done.7.p1), channel_id=1, source_target_pairs={{0,1},{1,0},{2,3},{3,2},{4,5},{5,4},{6,7},{7,6},{8,9},{9,8},{10,11... | collective-permute-start | bytes 172040 | tf_op jit(solution)/shard_map/ppermute | solution.py:279
  32.9 6.4 %collective-permute-start.14 = (f32[4,8,1024]{2,1,0:T(8,128)S(1)}, f32[4,8,1024]{2,1,0:T(8,128)S(1)}, u32[]{:S(2)}, u32[]{:S(2)}) collective-permute-start(f32[4,8,1024]{2,1,0:T(8,128)S(1)} %get-tuple-element.36), channel_id=1, source_target_pairs={{0,32},{32,0},{64,96},{96,64},{128,160},{160,128},{192,224},{224,1... | collective-permute-start | bytes 393224 | tf_op jit(solution)/shard_map/ppermute | solution.py:328
  34.9 8.2 %collective-permute-start.16 = (f32[3,16,1024]{2,1,0:T(8,128)S(1)}, f32[3,16,1024]{2,1,0:T(8,128)S(1)}, u32[]{:S(2)}, u32[]{:S(2)}) collective-permute-start(f32[3,16,1024]{2,1,0:T(8,128)S(1)} %get-tuple-element.44), channel_id=1, source_target_pairs={{0,32},{32,0},{64,96},{96,64},{128,160},{160,128},{192,224},{224,1... | collective-permute-start | bytes 589832 | tf_op jit(solution)/shard_map/ppermute | solution.py:328
  39.5 4.4 %collective-permute-start.15 = (f32[4,8,1024]{2,1,0:T(8,128)S(1)}, f32[4,8,1024]{2,1,0:T(8,128)S(1)}, u32[]{:S(2)}, u32[]{:S(2)}) collective-permute-start(f32[4,8,1024]{2,1,0:T(8,128)S(1)} %get-tuple-element.43.refs_8_), channel_id=1, source_target_pairs={{32,96},{192,128},{33,97},{193,129},{34,98},{194,130},{35,99},{195... | collective-permute-start | bytes 393224 | tf_op jit(solution)/shard_map/ppermute | solution.py:328
  44.3 0.7 collective-permute-start.17
  45.3 25.4 %collective-permute-start.19 = (f32[4,8,1024]{2,1,0:T(8,128)S(1)}, f32[4,8,1024]{2,1,0:T(8,128)S(1)}, u32[]{:S(2)}, u32[]{:S(2)}) collective-permute-start(f32[4,8,1024]{2,1,0:T(8,128)S(1)} %get-tuple-element.50), channel_id=1, source_target_pairs={{160,224},{64,0},{161,225},{65,1},{162,226},{66,2},{163,227},{67,3... | collective-permute-start | bytes 393224 | tf_op jit(solution)/shard_map/ppermute | solution.py:328
  46.6 24.1 %collective-permute-start.18 = (f32[4,8,1024]{2,1,0:T(8,128)S(1)}, f32[4,8,1024]{2,1,0:T(8,128)S(1)}, u32[]{:S(2)}, u32[]{:S(2)}) collective-permute-start(f32[4,8,1024]{2,1,0:T(8,128)S(1)} %get-tuple-element.50), channel_id=1, source_target_pairs={{32,64},{64,32},{96,128},{128,96},{160,192},{192,160},{33,65},{65,... | collective-permute-start | bytes 393224 | tf_op jit(solution)/shard_map/ppermute | solution.py:328

commit v2 on v1

v2 whole, which is shorter than its diff:
```python
import functools

import jax
import jax.numpy as jnp
from jax import lax
from jax.experimental import pallas as pl
from jax.experimental.pallas import tpu as pltpu
from jax.sharding import PartitionSpec as P

CHANNELS = 1024
EPSILON = 1e-05
LANES = 128
TILES = 8
CHUNK = 8
SLOTS = 7

VMEM = pl.BlockSpec(memory_space=pltpu.VMEM)


def call(kernel, outs, *args, aliases=None, limit=24, name=None):
    return pl.pallas_call(
        kernel,
        out_shape=outs,
        in_specs=[VMEM] * len(args),
        out_specs=jax.tree.map(lambda _: VMEM, outs),
        input_output_aliases=aliases or {},
        compiler_params=pltpu.CompilerParams(vmem_limit_bytes=limit << 20),
        name=name,
    )(*args)


def f32(*shape):
    return jax.ShapeDtypeStruct(shape, jnp.float32)


def place():
    chan = lax.axis_index("chan")
    return chan & 1, (chan >> 1) & 3


def lane_tile(core, x):
    return pl.ds(pl.multiple_of((core * 4 + (x & 3)) * LANES, LANES), LANES)


def exchanged(tiles):
    size = LANES // TILES
    block = lax.broadcasted_iota(jnp.int32, tiles[0].shape, 1) // size
    tiles = list(tiles)
    for bit in range(3):
        step = 1 << bit
        upper = (block >> bit) & 1 == 1
        for m in range(TILES):
            if m & step:
                continue
            low, high = tiles[m], tiles[m + step]
            tiles[m] = jnp.where(upper, turned(high, size * step), low)
            tiles[m + step] = jnp.where(upper, high, turned(low, -size * step))
    return tiles


def shuffled(tiles, outer):
    lane = lax.broadcasted_iota(jnp.int32, tiles[0].shape, 1)
    source = (lane % outer) * (LANES // outer) + lane // outer
    return [jnp.take_along_axis(tile, source, axis=1) for tile in tiles]


def woven(tiles):
    return exchanged(shuffled(tiles, LANES // TILES))


def unwoven(tiles):
    return shuffled(exchanged(tiles), TILES)


def project(feats_in, gain_in, weight_in, bias_in, keep, send, feats, gain_column, bias_column, gain, weight, bias, wide, sums, sems):
    core, x = place()
    rows, chans, cols = feats.shape
    sources = [(gain_in, gain), (weight_in, weight), (bias_in, bias)]
    sources += [(feats_in.at[at], feats.at[at]) for at in (pl.ds(k, CHUNK) for k in range(0, rows, CHUNK))]
    copies = [pltpu.make_async_copy(a, b, sems.at[k]) for k, (a, b) in enumerate(sources)]
    for copy in copies:
        copy.start()
    for copy in copies[:3]:
        copy.wait()
    w, g = weight[...], gain[...]
    gain_column[...] = jnp.broadcast_to(column_of(g), gain_column.shape)
    bias_column[...] = jnp.broadcast_to(column_of(bias[...]), bias_column.shape)
    picked = [w[0:1] - w[1:2], w[2:3] - w[1:2], w[6:7], w[3:4] - w[4:5], w[5:6] - w[4:5], w[7:8]]
    scaled = [p * g for p in picked]
    depth = rows * chans
    spot = lax.broadcasted_iota(jnp.int32, (chans, depth), 1) % chans
    picks = (spot == lax.broadcasted_iota(jnp.int32, (chans, depth), 0)).astype(jnp.bfloat16)
    band = lax.broadcasted_iota(jnp.int32, (rows, depth), 1) // chans
    own = band == lax.broadcasted_iota(jnp.int32, (rows, depth), 0)
    rest = jnp.concatenate(scaled + scaled[:2], axis=0)
    for part in range(3):
        head = rest.astype(jnp.bfloat16)
        rest = rest - head.astype(jnp.float32)
        spread_out = jnp.dot(head, picks, preferred_element_type=jnp.float32)
        for j in range(6):
            row = jnp.broadcast_to(spread_out[j : j + 1], (rows, depth))
            at = (part * 6 + j) * rows
            wide[at : at + rows] = jnp.where(own, row, 0.0).astype(jnp.bfloat16)
    for copy in copies[3:]:
        copy.wait()
    for m in range(TILES):
        block = feats[:, :, m * LANES : (m + 1) * LANES]
        made = jnp.dot(wide[...], block.reshape(depth, LANES), preferred_element_type=jnp.float32)
        sums[m, 0 : 6 * rows] = made[0 : 6 * rows] + made[6 * rows : 12 * rows] + made[12 * rows :]
        values = block.astype(jnp.float32)
        sums[m, 6 * rows :] = jnp.sum(values * values, axis=1)
    tiles = woven([sums[m] for m in range(TILES)])
    for side in range(2):

        @pl.when(core == side)
        def _():
            for m, tile in enumerate(tiles):
                out = keep if m >> 2 == side else send
                out[((m & 3) - x) & 3] = tile.reshape(SLOTS, rows, LANES)


def weave_rows(first, feats, gain_column, gained):
    def step(h, carry):
        line = feats[first + h].astype(jnp.float32) * gain_column[:, :1]
        put(gained, h, [tile.reshape(-1, 8, LANES) for tile in woven(tiles_of(line))])
        return carry

    lax.fori_loop(0, gained.shape[0], step, 0, unroll=4)


def join_cores(keep, arrived, *outs):
    for s, out in enumerate(outs):
        out[...] = keep[s] + arrived[s]


def join_x(a, b, c, d, out):
    out[...] = (a[...] + b[...]) + (c[...] + d[...])


def join_y(a, b, c, d, out):
    total = [(a[j] + b[j]) + (c[j] + d[j]) for j in range(SLOTS)]
    inverse = lax.rsqrt(total[6] / CHANNELS + EPSILON)
    scale = inverse * CHANNELS**-0.5
    for base in (0, 3):
        first, last = total[base] * scale, total[base + 1] * scale
        top = jnp.maximum(jnp.maximum(first, last), 0.0)
        first, mid, last = jnp.exp(first - top), jnp.exp(-top), jnp.exp(last - top)
        share = 1.0 / (first + mid + last)
        out[base] = first * share
        out[base + 1] = last * share
        out[base + 2] = total[base + 2] * scale
    out[6] = inverse


def edge_masked(first, last):
    column = lax.broadcasted_iota(jnp.int32, first.shape, 1)
    middle = 1.0 - first - last
    first = jnp.where(column == 0, 0.0, first)
    last = jnp.where(column == first.shape[1] - 1, 0.0, last)
    return first, middle, last


def column_of(row):
    n = row.shape[1]
    eye = lax.broadcasted_iota(jnp.int32, (n, n), 0) == lax.broadcasted_iota(jnp.int32, (n, n), 1)
    return jnp.sum(jnp.where(eye, jnp.broadcast_to(row, (n, n)), 0.0), axis=1, keepdims=True)


def rate_root(gate, bias):
    return lax.rsqrt(1.0 + jnp.exp(-(gate + bias)))


def turned(tile, by):
    return pltpu.roll(tile, by % LANES, axis=tile.ndim - 1)


def tiles_of(line):
    return [line[..., m * LANES : (m + 1) * LANES] for m in range(TILES)]


def widen(ref, index, tiles):
    for m, tile in enumerate([turned(tiles[-1], 1), *tiles, turned(tiles[0], -1)]):
        ref[(*index, slice(m * LANES, (m + 1) * LANES))] = tile


def row_step(state, first, h, decay, drive, taps):
    after = []
    lines = [taps[j, pl.ds(h, 1), :] for j in range(3)]
    for k in range(1, len(state) - 1):
        m = first + k
        at = slice(m * LANES, (m + 1) * LANES)
        a, b, c = (line[:, at] for line in lines)
        value = decay[h, :, :, at] * (a * state[k - 1] + b * state[k] + c * state[k + 1])
        after.append(value if drive is None else value + drive[h, :, :, at])
    return after


def two_rows(state, h1, h2, decay, drive, taps):
    ends = [turned(state[-2], 1), turned(state[-1], 1)], [turned(state[0], -1), turned(state[1], -1)]
    middle = row_step(ends[0] + state + ends[1], -1, h1, decay, drive, taps)
    return middle[1:-1], row_step(middle, 0, h2, decay, drive, taps)


def put(ref, h, tiles):
    for m, tile in enumerate(tiles):
        ref[h, :, :, m * LANES : (m + 1) * LANES] = tile


def whole(tiles):
    return jnp.concatenate(tiles, axis=2)


def row_at(step, upward, rows):
    return jnp.where(upward, rows - 1 - step, step)


def parity():
    return lax.axis_index("rows") & 1


def row_coefficients(upper, lower, gates, inverse, bias, h, decay, drive):
    half = upper.shape[0]
    values = jnp.where(h < half, upper[h & (half - 1)], lower[h & (half - 1)])
    root = rate_root(gates[pl.ds(h, 1), :], bias)
    root = root.reshape(values.shape)
    force = root * (values * inverse[pl.ds(h, 1), :])
    every = slice(None)
    widen(decay, (h, every, every), tiles_of(1.0 - root * root))
    widen(drive, (h, every, every), tiles_of(force))


def put_taps(taps, first, last):
    for k, tap in enumerate(edge_masked(first, last)):
        widen(taps, (k, slice(None)), tiles_of(tap))


def near_side(p0, p1, p2, p3, q0, q1, q2, q3, upper, lower, bias, near_taps, far_taps, far_gate, inverse, raw, decay, drive, kept, end, far_raw):
    core, x = place()
    odd = parity()
    rows = raw.shape[1]
    near, far = odd * 3, 3 - odd * 3
    for other, pieces in ((0, (p0, p1, p2, p3)), (1, (q0, q1, q2, q3))):
        for s, piece in enumerate(pieces):
            at = lane_tile(core ^ other, x + s)
            for k in range(3):
                raw[k, :, at] = piece[near + k]
            for k in range(2):
                far_raw[k, :, at] = piece[far + k]
            far_gate[:, at] = piece[far + 2]
            inverse[:, at] = piece[6]
    put_taps(near_taps, raw[0], raw[1])
    put_taps(far_taps, far_raw[0], far_raw[1])
    bias_column = bias[:, :1]
    gates = raw.at[2]

    def step(r, state):
        h1, h2 = (row_at(2 * r + k, odd == 1, rows) for k in range(2))
        for h in (h1, h2):
            row_coefficients(upper, lower, gates, inverse, bias_column, h, decay, drive)
        middle, state = two_rows(state, h1, h2, decay, drive, near_taps)
        put(kept, h1, middle)
        put(kept, h2, state)
        return state

    state = tiles_of(jnp.zeros(end.shape, jnp.float32))
    end[...] = whole(lax.fori_loop(0, rows // 2, step, state, unroll=4))


def far_side(far_gate, inverse, upper, lower, bias, decay, drive):
    bias_column = bias[:, :1]

    def step(h, carry):
        row_coefficients(upper, lower, far_gate, inverse, bias_column, h, decay, drive)
        return carry

    lax.fori_loop(0, decay.shape[0], step, 0, unroll=4)


def partner_side(raw, bias, taps, decay):
    bias_column = bias[:, :1]
    put_taps(taps, raw[0], raw[1])
    every = slice(None)

    def step(h, carry):
        root = rate_root(raw[2, pl.ds(h, 1), :], bias_column)
        line = (1.0 - root * root).reshape(*decay.shape[1:3], raw.shape[2])
        widen(decay, (h, every, every), tiles_of(line))
        return carry

    lax.fori_loop(0, decay.shape[0], step, 0, unroll=4)


def scan_rows(state, upward, decay, drive, taps, emit):
    rows = decay.shape[0]

    def step(r, state):
        h1, h2 = (row_at(2 * r + k, upward, rows) for k in range(2))
        middle, state = two_rows(state, h1, h2, decay, drive, taps)
        if emit is not None:
            emit(h1, middle)
            emit(h2, state)
        return state

    return lax.fori_loop(0, rows // 2, step, state, unroll=rows // 2)


def carried_in(arrived, partner_end, odd, decay, taps):
    state = scan_rows(tiles_of(arrived[...]), odd == 0, decay, None, taps, None)
    return [a + b for a, b in zip(state, tiles_of(partner_end[...]))]


def turn():
    position = lax.axis_index("rows")
    pair, odd = position >> 1, position & 1
    return odd, jnp.where(odd == 1, pair, 3 - pair)


def far_stage(stage, *refs):
    arrived, partner_end = refs[0], refs[1]
    if stage:
        pd, pt, refs = refs[2], refs[3], refs[4:]
    else:
        refs = refs[1:]
    if stage:
        fd, fq, ft, kept_in, leaving_in, kept, leaving = refs
    else:
        fd, fq, ft, kept_in, kept, leaving = refs[1:]
    odd, when = turn()

    @pl.when(when == stage)
    def _():
        if stage:
            state = carried_in(arrived, partner_end, odd, pd, pt)
        else:
            state = tiles_of(arrived[...])
        leaving[...] = whole(scan_rows(state, odd == 0, fd, fq, ft, functools.partial(put, kept)))

    @pl.when(when != stage)
    def _():
        kept[...] = kept_in[...]
        if stage:
            leaving[...] = leaving_in[...]


def last_stage(near_in, far_in, partner_end, pd, pt, fd, fq, ft, nd, nq, nt, kept, out, mixed, made, sems):
    odd, when = turn()
    rows, chans, _ = made.shape

    def copy(h, k):
        return pltpu.make_async_copy(made.at[h], out.at[h], sems.at[k])

    def mix(h, tiles):
        for m, tile in enumerate(tiles):
            at = slice(m * LANES, (m + 1) * LANES)
            mixed[h, :, :, at] = kept[h, :, :, at] * tile

    def finish(h):
        tiles = [mixed[h, :, :, m * LANES : (m + 1) * LANES].reshape(chans, LANES) for m in range(TILES)]
        for m, tile in enumerate(unwoven(tiles)):
            made[h, :, m * LANES : (m + 1) * LANES] = tile.astype(made.dtype)
        copy(h, h).start()

    def scan_all(state, upward, decay, drive, taps):
        def pair(r):
            return [row_at(2 * r + k, upward, rows) for k in range(2)]

        def advance(r, state):
            middle, state = two_rows(state, *pair(r), decay, drive, taps)
            for h, tiles in zip(pair(r), (middle, state)):
                mix(h, tiles)
            return state

        def step(r, state):
            for h in pair(r - 1):
                finish(h)
            return advance(r, state)

        lax.fori_loop(1, rows // 2, step, advance(0, state))
        for h in pair(rows // 2 - 1):
            finish(h)

    @pl.when(when == 3)
    def _():
        scan_all(carried_in(far_in, partner_end, odd, pd, pt), odd == 0, fd, fq, ft)

    @pl.when(when != 3)
    def _():
        scan_all(tiles_of(near_in[...]), odd == 1, nd, nq, nt)

    for k in range(rows):
        copy(k, k).wait()


def chan_shift(value, target):
    return lax.ppermute(value, "chan", [(i, target(i)) for i in range(32)])


def along_x(value, s):
    return chan_shift(value, lambda i: (i & ~6) | ((((i >> 1) + s) & 3) << 1))


def along_y(value, s):
    return chan_shift(value, lambda i: (i & 7) | ((((i >> 3) + s) & 3) << 3))


def other_core(value):
    return chan_shift(value, lambda i: i ^ 1)


def shards(feats, norm_gain, proj_weight, chan_bias):
    rows, chans, cols = feats.shape
    gain, bias = norm_gain.reshape(1, chans), chan_bias.reshape(1, chans)
    piece = f32(SLOTS, rows, LANES)
    half = f32(4, SLOTS, rows, LANES)
    column = f32(chans, LANES)
    arguments = (feats, gain, proj_weight, bias)
    keep, send, feats, gain, bias = pl.pallas_call(
        project,
        out_shape=(half, half, jax.ShapeDtypeStruct(feats.shape, feats.dtype), column, column),
        in_specs=[pl.BlockSpec(memory_space=pltpu.HBM)] * 4,
        out_specs=(VMEM,) * 5,
        scratch_shapes=[
            pltpu.VMEM(gain.shape, gain.dtype),
            pltpu.VMEM(proj_weight.shape, proj_weight.dtype),
            pltpu.VMEM(bias.shape, bias.dtype),
            pltpu.VMEM((18 * rows, rows * chans), jnp.bfloat16),
            pltpu.VMEM((TILES, SLOTS * rows, LANES), jnp.float32),
            pltpu.SemaphoreType.DMA((3 + rows // CHUNK,)),
        ],
        compiler_params=pltpu.CompilerParams(vmem_limit_bytes=24 << 20),
    )(*(pltpu.with_memory_space_constraint(v, pltpu.HBM) for v in arguments))
    block = f32(rows, chans // 8, 8, cols)
    rows_half = f32(rows // 2, chans // 8, 8, cols)
    gained = [call(functools.partial(weave_rows, at), rows_half, feats, gain) for at in (0, rows // 2)]
    mine, *others = call(join_cores, (piece,) * 4, keep, other_core(send))
    part = call(join_x, piece, mine, *(along_x(v, s + 1) for s, v in enumerate(others)))
    part, gained[0] = lax.optimization_barrier((part, gained[0]))
    whole = call(join_y, piece, part, *(along_y(part, s) for s in (3, 2, 1)))
    whole, gained[1] = lax.optimization_barrier((whole, gained[1]))
    pieces = [whole] + [along_x(whole, s) for s in (3, 2, 1)]
    pieces = pieces + [other_core(v) for v in pieces]

    state = f32(chans // 8, 8, cols)
    wider = f32(rows, chans // 8, 8, cols + 2 * LANES)
    taps = f32(3, rows, cols + 2 * LANES)
    line, lines = f32(rows, cols), f32(3, rows, cols)
    near_taps, far_taps, far_gate, inverse, raw, near_decay, near_drive, kept, end = pl.pallas_call(
        near_side,
        out_shape=(taps, taps, line, line, lines, wider, wider, block, state),
        in_specs=[VMEM] * 11,
        out_specs=(VMEM,) * 9,
        scratch_shapes=[pltpu.VMEM((2, rows, cols), jnp.float32)],
        compiler_params=pltpu.CompilerParams(vmem_limit_bytes=24 << 20),
    )(*pieces, *gained, bias)

    def along_rows(value, pairs):
        return lax.ppermute(value, "rows", pairs)

    swap = [(p, p ^ 1) for p in range(8)]
    partner_end = along_rows(end, swap)
    far_decay, far_drive = call(far_side, (wider, wider), far_gate, inverse, *gained, bias)
    far = (far_decay, far_drive, far_taps)
    partner_raw = along_rows(raw, swap)
    kept, leaving = call(
        functools.partial(far_stage, 0), (block, state), partner_end, partner_end, *far, kept, aliases={5: 0}
    )
    partner_taps, partner_decay = call(partner_side, (taps, wider), partner_raw, bias)
    partner = (partner_end, partner_decay, partner_taps)
    for stage in (1, 2):
        t = stage - 1
        arrived = along_rows(leaving, [(2 * t + 1, 2 * t + 3), (6 - 2 * t, 4 - 2 * t)])
        kept, leaving = call(
            functools.partial(far_stage, stage), (block, state), arrived, *partner, *far, kept, leaving,
            aliases={7: 0, 8: 1},
        )
    near_in = along_rows(leaving, [(1, 2), (2, 1), (3, 4), (4, 3), (5, 6), (6, 5)])
    far_in = along_rows(leaving, [(5, 7), (2, 0)])
    return pl.pallas_call(
        last_stage,
        out_shape=jax.ShapeDtypeStruct(feats.shape, jnp.bfloat16),
        in_specs=[VMEM] * 12,
        out_specs=pl.BlockSpec(memory_space=pl.ANY),
        scratch_shapes=[
            pltpu.VMEM(block.shape, block.dtype),
            pltpu.VMEM(feats.shape, jnp.bfloat16),
            pltpu.SemaphoreType.DMA((rows,)),
        ],
        compiler_params=pltpu.CompilerParams(vmem_limit_bytes=24 << 20),
    )(near_in, far_in, *partner, *far, near_decay, near_drive, near_taps, kept)


def solution(mesh):
    in_specs = (P("rows", "chan", None), P("chan"), P(None, "chan"), P("chan"))
    out_specs = P("rows", "chan", None)
    return jax.shard_map(shards, mesh=mesh, in_specs=in_specs, out_specs=out_specs, check_vma=False)
```

time: 76.8 us -> 71.5 us (0.931); the launches traced: 75.2 us -> 70.9 us
  waiting for transfers between devices: 42.7 us -> 34.9 us
  Pallas kernels: 13.1 us -> 17.2 us
    ppermute x6, waiting for transfers between devices: 29.5 us -> 24.5 us  [along_rows(): return lax.ppermute(value, 'rows', pairs)]
    pallas_call x9 -> x10, Pallas kernels: 5.12 us -> 8.03 us  [call(): pl.pallas_call(kernel, out_shape=outs, in_specs=[VMEM] * len(args), out_s...]
    ppermute x14, waiting for transfers between devices: 13.2 us -> 10.4 us  [chan_shift(): return lax.ppermute(value, 'chan', [(i, target(i)) for i in range(32)])]
    pallas_call x1 -> x2, Pallas kernels: 3.55 us -> 4.83 us  [the longest x1 2.72 us: shards(): pl.pallas_call(project, out_shape=(half, half, jax.ShapeDtypeStruct(feats...]
  transfers between devices with their start and end apart: 20 -> 20, of which waited for: 14 -> 11; matrix products, arithmetic and copies ran while one was open for 0% -> 0% of each run, Pallas kernels for 3% -> 10%
where the time goes in v2:
time: 71.5 us; the launch traced here: 70.9 us
  waiting for transfers between devices  34.9 us (49%)
  starting transfers between devices  18.4 us (26%)
  Pallas kernels  17.2 us (24%)
    ppermute x6, waiting for transfers between devices, along_rows(): return lax.ppermute(value, 'rows', pairs)  24.5 us
    ppermute x14, starting transfers between devices, chan_shift(): return lax.ppermute(value, 'chan', [(i, target(i)) for i in range(32)])  13 us
    ppermute x14, waiting for transfers between devices, chan_shift(): return lax.ppermute(value, 'chan', [(i, target(i)) for i in range(32)])  10.4 us
    pallas_call x10, Pallas kernels, call(): pl.pallas_call(kernel, out_shape=outs, in_specs=[VMEM] * len(args), out_s...  8.03 us
    ppermute x6, starting transfers between devices, along_rows(): return lax.ppermute(value, 'rows', pairs)  5.41 us
    pallas_call x1, Pallas kernels, shards(): pl.pallas_call(last_stage, out_shape=jax.ShapeDtypeStruct(feats.shape, jn...  4.34 us
    pallas_call x1, Pallas kernels, shards(): pl.pallas_call(project, out_shape=(half, half, jax.ShapeDtypeStruct(feats...  2.72 us
    pallas_call x1, Pallas kernels, shards(): pl.pallas_call(near_side, out_shape=(taps, taps, line, line, lines, wider...  2.11 us
  transfers between devices with their start and end apart: 20, of which 11 were waited for; matrix products, arithmetic and copies ran while one was open for 0% of the time, Pallas kernels for 10%

profile of v2, /device:TPU:24, one launch (start us, length us, event | category | flops | bytes accessed | tf_op | source)
XLA Modules:
  0.0 70.9 jit_solution(8302725253189968676)
XLA Ops:
  0.0 2.7 %shard_map.46 = (f32[4,7,16,128]{3,2,1,0:T(8,128)S(1)}, f32[4,7,16,128]{3,2,1,0:T(8,128)S(1)}, bf16[16,32,1024]{2,1,0:T(8,128)(2,1)S(1)}, f32[32,128]{1,0:T(8,128)S(1)}, f32[32,128]{1,0:T(8,128)S(1)}) custom-call(bf16[16,32,1024]{2,1,0:T(8,128)(2,1)} %feats_in.1, f32[1,32]{1,0:T(1,128)} %bitcast.2, f32[8,32]{1,0:T(8,128)} %weight_in.1, f32[1,32]{1,0:T(1,128)} %bitcast.3), custom_call_target="tpu_custom_call" | custom-call | tf_op jit(solution)/shard_map/pallas_call | solution.py:417
  2.8 1.5 %collective-permute-done.arrived = f32[4,7,16,128]{3,2,1,0:T(8,128)S(1)} collective-permute-done((f32[4,7,16,128]{3,2,1,0:T(8,128)S(1)}, f32[4,7,16,128]{3,2,1,0:T(8,128)S(1)}, u32[]{:S(2)}, u32[]{:S(2)}) %collective-permute-start) | collective-permute-done | bytes 229408 | tf_op jit(solution)/shard_map/ppermute | solution.py:395
  4.3 1.6 %collective-permute-start.1 = (f32[7,16,128]{2,1,0:T(8,128)S(1)}, f32[7,16,128]{2,1,0:T(8,128)S(1)}, u32[]{:S(2)}, u32[]{:S(2)}) collective-permute-start(f32[7,16,128]{2,1,0:T(8,128)S(1)} %get-tuple-element.40), channel_id=1, source_target_pairs={{0,2},{1,3},{2,4},{3,5},{4,6},{5,7},{6,0},{7,1},{8,10},{9,11},{10,... | collective-permute-start | bytes 172040 | tf_op jit(solution)/shard_map/ppermute | solution.py:395
  5.9 2.7 %collective-permute-start.2 = (f32[7,16,128]{2,1,0:T(8,128)S(1)}, f32[7,16,128]{2,1,0:T(8,128)S(1)}, u32[]{:S(2)}, u32[]{:S(2)}) collective-permute-start(f32[7,16,128]{2,1,0:T(8,128)S(1)} %get-tuple-element.41), channel_id=1, source_target_pairs={{0,4},{1,5},{2,6},{3,7},{4,0},{5,1},{6,2},{7,3},{8,12},{9,13},{10,... | collective-permute-start | bytes 172040 | tf_op jit(solution)/shard_map/ppermute | solution.py:395
  8.6 1.4 %collective-permute-start.3 = (f32[7,16,128]{2,1,0:T(8,128)S(1)}, f32[7,16,128]{2,1,0:T(8,128)S(1)}, u32[]{:S(2)}, u32[]{:S(2)}) collective-permute-start(f32[7,16,128]{2,1,0:T(8,128)S(1)} %get-tuple-element.42), channel_id=1, source_target_pairs={{0,6},{1,7},{2,0},{3,1},{4,2},{5,3},{6,4},{7,5},{8,14},{9,15},{10,... | collective-permute-start | bytes 172040 | tf_op jit(solution)/shard_map/ppermute | solution.py:395
  10.1 2.2 %shard_map.49.upper = f32[8,4,8,1024]{3,2,1,0:T(8,128)S(1)} custom-call(bf16[16,32,1024]{2,1,0:T(8,128)(2,1)S(1)} %get-tuple-element.43.feats, f32[32,128]{1,0:T(8,128)S(1)} %get-tuple-element.44.gain_column), custom_call_target="tpu_custom_call" | custom-call | tf_op jit(solution)/shard_map/pallas_call | solution.py:21
  12.3 0.5 collective-permute-done.3.d
  12.8 0.6 collective-permute-start.6
  13.4 2.3 %collective-permute-start.5 = (f32[7,16,128]{2,1,0:T(8,128)S(1)}, f32[7,16,128]{2,1,0:T(8,128)S(1)}, u32[]{:S(2)}, u32[]{:S(2)}) collective-permute-start(f32[7,16,128]{2,1,0:T(8,128)S(1)} %shard_map.48.a), channel_id=1, source_target_pairs={{0,16},{1,17},{2,18},{3,19},{4,20},{5,21},{6,22},{7,23},{8,24},{9,... | collective-permute-start | bytes 172040 | tf_op jit(solution)/shard_map/ppermute | solution.py:395
  15.7 2.2 %shard_map.51.lower = f32[8,4,8,1024]{3,2,1,0:T(8,128)S(1)} custom-call(bf16[16,32,1024]{2,1,0:T(8,128)(2,1)S(1)} %get-tuple-element.43.feats, f32[32,128]{1,0:T(8,128)S(1)} %get-tuple-element.44.gain_column), custom_call_target="tpu_custom_call" | custom-call | tf_op jit(solution)/shard_map/pallas_call | solution.py:21
  18.0 1.2 %collective-permute-done.5.c = f32[7,16,128]{2,1,0:T(8,128)S(1)} collective-permute-done((f32[7,16,128]{2,1,0:T(8,128)S(1)}, f32[7,16,128]{2,1,0:T(8,128)S(1)}, u32[]{:S(2)}, u32[]{:S(2)}) %collective-permute-start.5) | collective-permute-done | bytes 57376 | tf_op jit(solution)/shard_map/ppermute | solution.py:395
  19.1 2.0 %collective-permute-done.4.b = f32[7,16,128]{2,1,0:T(8,128)S(1)} collective-permute-done((f32[7,16,128]{2,1,0:T(8,128)S(1)}, f32[7,16,128]{2,1,0:T(8,128)S(1)}, u32[]{:S(2)}, u32[]{:S(2)}) %collective-permute-start.4) | collective-permute-done | bytes 57376 | tf_op jit(solution)/shard_map/ppermute | solution.py:395
  21.2 0.6 collective-permute-start.9
  21.7 3.6 %collective-permute-start.8 = (f32[7,16,128]{2,1,0:T(8,128)S(1)}, f32[7,16,128]{2,1,0:T(8,128)S(1)}, u32[]{:S(2)}, u32[]{:S(2)}) collective-permute-start(f32[7,16,128]{2,1,0:T(8,128)S(1)} %shard_map.50.p0), channel_id=1, source_target_pairs={{0,4},{1,5},{2,6},{3,7},{4,0},{5,1},{6,2},{7,3},{8,12},{9,13},{10,... | collective-permute-start | bytes 172040 | tf_op jit(solution)/shard_map/ppermute | solution.py:395
  25.5 1.2 %collective-permute-done.9.p3 = f32[7,16,128]{2,1,0:T(8,128)S(1)} collective-permute-done((f32[7,16,128]{2,1,0:T(8,128)S(1)}, f32[7,16,128]{2,1,0:T(8,128)S(1)}, u32[]{:S(2)}, u32[]{:S(2)}) %collective-permute-start.9) | collective-permute-done | bytes 57376 | tf_op jit(solution)/shard_map/ppermute | solution.py:395
  26.6 1.5 %collective-permute-done.8.p2 = f32[7,16,128]{2,1,0:T(8,128)S(1)} collective-permute-done((f32[7,16,128]{2,1,0:T(8,128)S(1)}, f32[7,16,128]{2,1,0:T(8,128)S(1)}, u32[]{:S(2)}, u32[]{:S(2)}) %collective-permute-start.8) | collective-permute-done | bytes 57376 | tf_op jit(solution)/shard_map/ppermute | solution.py:395
  28.1 1.4 %collective-permute-done.7.p1 = f32[7,16,128]{2,1,0:T(8,128)S(1)} collective-permute-done((f32[7,16,128]{2,1,0:T(8,128)S(1)}, f32[7,16,128]{2,1,0:T(8,128)S(1)}, u32[]{:S(2)}, u32[]{:S(2)}) %collective-permute-start.7) | collective-permute-done | bytes 57376 | tf_op jit(solution)/shard_map/ppermute | solution.py:395
  29.5 1.2 %collective-permute-done.11.q1 = f32[7,16,128]{2,1,0:T(8,128)S(1)} collective-permute-done((f32[7,16,128]{2,1,0:T(8,128)S(1)}, f32[7,16,128]{2,1,0:T(8,128)S(1)}, u32[]{:S(2)}, u32[]{:S(2)}) %collective-permute-start.11) | collective-permute-done | bytes 57376 | tf_op jit(solution)/shard_map/ppermute | solution.py:395
  30.8 2.1 %shard_map.52 = (f32[3,16,1280]{2,1,0:T(8,128)S(1)}, f32[3,16,1280]{2,1,0:T(8,128)S(1)}, f32[16,1024]{1,0:T(8,128)S(1)}, f32[16,1024]{1,0:T(8,128)S(1)}, f32[3,1...) custom-call(f32[7,16,128]{2,1,0:T(8,128)S(1)} %shard_map.50.p0, ...), custom_call_target="tpu_custom_call" | custom-call | tf_op jit(solution)/shard_map/pallas_call | solution.py:447
  32.9 2.0 %collective-permute-start.14 = (f32[4,8,1024]{2,1,0:T(8,128)S(1)}, f32[4,8,1024]{2,1,0:T(8,128)S(1)}, u32[]{:S(2)}, u32[]{:S(2)}) collective-permute-start(f32[4,8,1024]{2,1,0:T(8,128)S(1)} %get-tuple-element.50), channel_id=1, source_target_pairs={{0,32},{32,0},{64,96},{96,64},{128,160},{160,128},{192,224},{224,1... | collective-permute-start | bytes 393224 | tf_op jit(solution)/shard_map/ppermute | solution.py:457
  35.0 1.4 %shard_map.53 = (f32[16,4,8,1280]{3,2,1,0:T(8,128)S(1)}, f32[16,4,8,1280]{3,2,1,0:T(8,128)S(1)}) custom-call(f32[16,1024]{1,0:T(8,128)S(1)} %get-tuple-element.51.far_gate, f32[16,1024]{1,0:T(8,128)S(1)} %get-tuple-element.52.inverse, f32[8,4,8,1024]{3,2,1,0:T(8,128)S(1)} %shard_map.49.upper, f32[8,4,8,1024]{3,2,1,0:T(8,128)S(1)} %shard_map.51.lower, ...), custom_call_target="tpu_custom_call" | custom-call | tf_op jit(solution)/shard_map/pallas_call | solution.py:21
  36.4 2.9 %collective-permute-done.14.refs_0_.refs_1_.partner_end = f32[4,8,1024]{2,1,0:T(8,128)S(1)} collective-permute-done((f32[4,8,1024]{2,1,0:T(8,128)S(1)}, f32[4,8,1024]{2,1,0:T(8,128)S(1)}, u32[]{:S(2)}, u32[]{:S(2)}) %collective-permute-start.14) | collective-permute-done | bytes 131104 | tf_op jit(solution)/shard_map/ppermute | solution.py:457
  39.6 0.7 collective-permute-start.15
  40.2 2.7 %collective-permute-done.16.raw = f32[3,16,1024]{2,1,0:T(8,128)S(1)} collective-permute-done((f32[3,16,1024]{2,1,0:T(8,128)S(1)}, f32[3,16,1024]{2,1,0:T(8,128)S(1)}, u32[]{:S(2)}, u32[]{:S(2)}) %collective-permute-start.16) | collective-permute-done | bytes 196640 | tf_op jit(solution)/shard_map/ppermute | solution.py:457
  42.9 1.2 %shard_map.55 = (f32[3,16,1280]{2,1,0:T(8,128)S(1)}, f32[16,4,8,1280]{3,2,1,0:T(8,128)S(1)}) custom-call(f32[3,16,1024]{2,1,0:T(8,128)S(1)} %collective-permute-done.16.raw, f32[32,128]{1,0:T(8,128)S(1)} %get-tuple-element.49.bias), custom_call_target="tpu_custom_call" | custom-call | tf_op jit(solution)/shard_map/pallas_call | solution.py:21
  44.2 0.3 shard_map.56
  44.5 0.7 collective-permute-start.17
  45.2 0.3 shard_map.57
  45.5 1.3 %collective-permute-start.19 = (f32[4,8,1024]{2,1,0:T(8,128)S(1)}, f32[4,8,1024]{2,1,0:T(8,128)S(1)}, u32[]{:S(2)}, u32[]{:S(2)}) collective-permute-start(f32[4,8,1024]{2,1,0:T(8,128)S(1)} %get-tuple-element.64), channel_id=1, source_target_pairs={{160,224},{64,0},{161,225},{65,1},{162,226},{66,2},{163,227},{67,3... | collective-permute-start | bytes 393224 | tf_op jit(solution)/shard_map/ppermute | solution.py:457
  46.8 0.7 collective-permute-start.18
  47.5 19.0 %collective-permute-done.19.far_in = f32[4,8,1024]{2,1,0:T(8,128)S(1)} collective-permute-done((f32[4,8,1024]{2,1,0:T(8,128)S(1)}, f32[4,8,1024]{2,1,0:T(8,128)S(1)}, u32[]{:S(2)}, u32[]{:S(2)}) %collective-permute-start.19) | collective-permute-done | bytes 131104 | tf_op jit(solution)/shard_map/ppermute | solution.py:457
  66.4 4.3 %shard_map.58 = bf16[16,32,1024]{2,1,0:T(8,128)(2,1)} custom-call(f32[4,8,1024]{2,1,0:T(8,128)S(1)} %collective-permute-done.18.near_in, f32[4,8,1024]{2,1,0:T(8,128)S(1)} %collective-permute-done.19.far_in, f32[4,8,1024]{2,1,0:T(8,128)S(1)} %collective-permute-done.14.refs_0_.refs_1_.partner_end, f32[16,4,8,1280]{3,2,1,0:T(8,128)S(1)} %get-tuple-element.59.refs_2_.pd, ...), custom_call_target="tpu_custom_call" | custom-call | tf_op jit(solution)/shard_map/pallas_call | solution.py:478
  (21 shorter events, 0.7 us)
Async XLA Ops:
  2.7 1.6 %collective-permute-start = (f32[4,7,16,128]{3,2,1,0:T(8,128)S(1)}, f32[4,7,16,128]{3,2,1,0:T(8,128)S(1)}, u32[]{:S(2)}, u32[]{:S(2)}) collective-permute-start(f32[4,7,16,128]{3,2,1,0:T(8,128)S(1)} %get-tuple-element.38), channel_id=1, source_target_pairs={{0,1},{1,0},{2,3},{3,2},{4,5},{5,4},{6,7},{7,6},{8,9},{9,8},{10,11... | collective-permute-start | bytes 688136 | tf_op jit(solution)/shard_map/ppermute | solution.py:395
  4.3 8.0 %collective-permute-start.1 = (f32[7,16,128]{2,1,0:T(8,128)S(1)}, f32[7,16,128]{2,1,0:T(8,128)S(1)}, u32[]{:S(2)}, u32[]{:S(2)}) collective-permute-start(f32[7,16,128]{2,1,0:T(8,128)S(1)} %get-tuple-element.40), channel_id=1, source_target_pairs={{0,2},{1,3},{2,4},{3,5},{4,6},{5,7},{6,0},{7,1},{8,10},{9,11},{10,... | collective-permute-start | bytes 172040 | tf_op jit(solution)/shard_map/ppermute | solution.py:395
  5.9 6.4 %collective-permute-start.2 = (f32[7,16,128]{2,1,0:T(8,128)S(1)}, f32[7,16,128]{2,1,0:T(8,128)S(1)}, u32[]{:S(2)}, u32[]{:S(2)}) collective-permute-start(f32[7,16,128]{2,1,0:T(8,128)S(1)} %get-tuple-element.41), channel_id=1, source_target_pairs={{0,4},{1,5},{2,6},{3,7},{4,0},{5,1},{6,2},{7,3},{8,12},{9,13},{10,... | collective-permute-start | bytes 172040 | tf_op jit(solution)/shard_map/ppermute | solution.py:395
  8.6 4.2 %collective-permute-start.3 = (f32[7,16,128]{2,1,0:T(8,128)S(1)}, f32[7,16,128]{2,1,0:T(8,128)S(1)}, u32[]{:S(2)}, u32[]{:S(2)}) collective-permute-start(f32[7,16,128]{2,1,0:T(8,128)S(1)} %get-tuple-element.42), channel_id=1, source_target_pairs={{0,6},{1,7},{2,0},{3,1},{4,2},{5,3},{6,4},{7,5},{8,14},{9,15},{10,... | collective-permute-start | bytes 172040 | tf_op jit(solution)/shard_map/ppermute | solution.py:395
  12.8 5.1 %collective-permute-start.6 = (f32[7,16,128]{2,1,0:T(8,128)S(1)}, f32[7,16,128]{2,1,0:T(8,128)S(1)}, u32[]{:S(2)}, u32[]{:S(2)}) collective-permute-start(f32[7,16,128]{2,1,0:T(8,128)S(1)} %shard_map.48.a), channel_id=1, source_target_pairs={{0,8},{1,9},{2,10},{3,11},{4,12},{5,13},{6,14},{7,15},{8,16},{9,17... | collective-permute-start | bytes 172040 | tf_op jit(solution)/shard_map/ppermute | solution.py:395
  13.4 5.7 %collective-permute-start.5 = (f32[7,16,128]{2,1,0:T(8,128)S(1)}, f32[7,16,128]{2,1,0:T(8,128)S(1)}, u32[]{:S(2)}, u32[]{:S(2)}) collective-permute-start(f32[7,16,128]{2,1,0:T(8,128)S(1)} %shard_map.48.a), channel_id=1, source_target_pairs={{0,16},{1,17},{2,18},{3,19},{4,20},{5,21},{6,22},{7,23},{8,24},{9,... | collective-permute-start | bytes 172040 | tf_op jit(solution)/shard_map/ppermute | solution.py:395
  15.7 5.4 %collective-permute-start.4 = (f32[7,16,128]{2,1,0:T(8,128)S(1)}, f32[7,16,128]{2,1,0:T(8,128)S(1)}, u32[]{:S(2)}, u32[]{:S(2)}) collective-permute-start(f32[7,16,128]{2,1,0:T(8,128)S(1)} %shard_map.48.a), channel_id=1, source_target_pairs={{0,24},{1,25},{2,26},{3,27},{4,28},{5,29},{6,30},{7,31},{8,0},{9,1... | collective-permute-start | bytes 172040 | tf_op jit(solution)/shard_map/ppermute | solution.py:395
  21.2 5.5 %collective-permute-start.9 = (f32[7,16,128]{2,1,0:T(8,128)S(1)}, f32[7,16,128]{2,1,0:T(8,128)S(1)}, u32[]{:S(2)}, u32[]{:S(2)}) collective-permute-start(f32[7,16,128]{2,1,0:T(8,128)S(1)} %shard_map.50.p0), channel_id=1, source_target_pairs={{0,2},{1,3},{2,4},{3,5},{4,6},{5,7},{6,0},{7,1},{8,10},{9,11},{10,... | collective-permute-start | bytes 172040 | tf_op jit(solution)/shard_map/ppermute | solution.py:395
  21.7 6.4 %collective-permute-start.8 = (f32[7,16,128]{2,1,0:T(8,128)S(1)}, f32[7,16,128]{2,1,0:T(8,128)S(1)}, u32[]{:S(2)}, u32[]{:S(2)}) collective-permute-start(f32[7,16,128]{2,1,0:T(8,128)S(1)} %shard_map.50.p0), channel_id=1, source_target_pairs={{0,4},{1,5},{2,6},{3,7},{4,0},{5,1},{6,2},{7,3},{8,12},{9,13},{10,... | collective-permute-start | bytes 172040 | tf_op jit(solution)/shard_map/ppermute | solution.py:395
  25.3 4.2 %collective-permute-start.7 = (f32[7,16,128]{2,1,0:T(8,128)S(1)}, f32[7,16,128]{2,1,0:T(8,128)S(1)}, u32[]{:S(2)}, u32[]{:S(2)}) collective-permute-start(f32[7,16,128]{2,1,0:T(8,128)S(1)} %shard_map.50.p0), channel_id=1, source_target_pairs={{0,6},{1,7},{2,0},{3,1},{4,2},{5,3},{6,4},{7,5},{8,14},{9,15},{10,... | collective-permute-start | bytes 172040 | tf_op jit(solution)/shard_map/ppermute | solution.py:395
  25.5 4.1 %collective-permute-start.10 = (f32[7,16,128]{2,1,0:T(8,128)S(1)}, f32[7,16,128]{2,1,0:T(8,128)S(1)}, u32[]{:S(2)}, u32[]{:S(2)}) collective-permute-start(f32[7,16,128]{2,1,0:T(8,128)S(1)} %shard_map.50.p0), channel_id=1, source_target_pairs={{0,1},{1,0},{2,3},{3,2},{4,5},{5,4},{6,7},{7,6},{8,9},{9,8},{10,11... | collective-permute-start | bytes 172040 | tf_op jit(solution)/shard_map/ppermute | solution.py:395
  26.6 2.9 %collective-permute-start.13 = (f32[7,16,128]{2,1,0:T(8,128)S(1)}, f32[7,16,128]{2,1,0:T(8,128)S(1)}, u32[]{:S(2)}, u32[]{:S(2)}) collective-permute-start(f32[7,16,128]{2,1,0:T(8,128)S(1)} %collective-permute-done.9.p3), channel_id=1, source_target_pairs={{0,1},{1,0},{2,3},{3,2},{4,5},{5,4},{6,7},{7,6},{8,9},{9,8},{10,11... | collective-permute-start | bytes 172040 | tf_op jit(solution)/shard_map/ppermute | solution.py:395
  28.1 1.4 %collective-permute-start.12 = (f32[7,16,128]{2,1,0:T(8,128)S(1)}, f32[7,16,128]{2,1,0:T(8,128)S(1)}, u32[]{:S(2)}, u32[]{:S(2)}) collective-permute-start(f32[7,16,128]{2,1,0:T(8,128)S(1)} %collective-permute-done.8.p2), channel_id=1, source_target_pairs={{0,1},{1,0},{2,3},{3,2},{4,5},{5,4},{6,7},{7,6},{8,9},{9,8},{10,11... | collective-permute-start | bytes 172040 | tf_op jit(solution)/shard_map/ppermute | solution.py:395
  29.5 1.2 %collective-permute-start.11 = (f32[7,16,128]{2,1,0:T(8,128)S(1)}, f32[7,16,128]{2,1,0:T(8,128)S(1)}, u32[]{:S(2)}, u32[]{:S(2)}) collective-permute-start(f32[7,16,128]{2,1,0:T(8,128)S(1)} %collective-permute-done.7.p1), channel_id=1, source_target_pairs={{0,1},{1,0},{2,3},{3,2},{4,5},{5,4},{6,7},{7,6},{8,9},{9,8},{10,11... | collective-permute-start | bytes 172040 | tf_op jit(solution)/shard_map/ppermute | solution.py:395
  32.9 6.4 %collective-permute-start.14 = (f32[4,8,1024]{2,1,0:T(8,128)S(1)}, f32[4,8,1024]{2,1,0:T(8,128)S(1)}, u32[]{:S(2)}, u32[]{:S(2)}) collective-permute-start(f32[4,8,1024]{2,1,0:T(8,128)S(1)} %get-tuple-element.50), channel_id=1, source_target_pairs={{0,32},{32,0},{64,96},{96,64},{128,160},{160,128},{192,224},{224,1... | collective-permute-start | bytes 393224 | tf_op jit(solution)/shard_map/ppermute | solution.py:457
  34.9 8.0 %collective-permute-start.16 = (f32[3,16,1024]{2,1,0:T(8,128)S(1)}, f32[3,16,1024]{2,1,0:T(8,128)S(1)}, u32[]{:S(2)}, u32[]{:S(2)}) collective-permute-start(f32[3,16,1024]{2,1,0:T(8,128)S(1)} %get-tuple-element.58), channel_id=1, source_target_pairs={{0,32},{32,0},{64,96},{96,64},{128,160},{160,128},{192,224},{224,1... | collective-permute-start | bytes 589832 | tf_op jit(solution)/shard_map/ppermute | solution.py:457
  39.6 4.6 %collective-permute-start.15 = (f32[4,8,1024]{2,1,0:T(8,128)S(1)}, f32[4,8,1024]{2,1,0:T(8,128)S(1)}, u32[]{:S(2)}, u32[]{:S(2)}) collective-permute-start(f32[4,8,1024]{2,1,0:T(8,128)S(1)} %get-tuple-element.57.refs_8_), channel_id=1, source_target_pairs={{32,96},{192,128},{33,97},{193,129},{34,98},{194,130},{35,99},{195... | collective-permute-start | bytes 393224 | tf_op jit(solution)/shard_map/ppermute | solution.py:457
  44.5 0.7 collective-permute-start.17
  45.5 20.9 %collective-permute-start.19 = (f32[4,8,1024]{2,1,0:T(8,128)S(1)}, f32[4,8,1024]{2,1,0:T(8,128)S(1)}, u32[]{:S(2)}, u32[]{:S(2)}) collective-permute-start(f32[4,8,1024]{2,1,0:T(8,128)S(1)} %get-tuple-element.64), channel_id=1, source_target_pairs={{160,224},{64,0},{161,225},{65,1},{162,226},{66,2},{163,227},{67,3... | collective-permute-start | bytes 393224 | tf_op jit(solution)/shard_map/ppermute | solution.py:457
  46.8 19.6 %collective-permute-start.18 = (f32[4,8,1024]{2,1,0:T(8,128)S(1)}, f32[4,8,1024]{2,1,0:T(8,128)S(1)}, u32[]{:S(2)}, u32[]{:S(2)}) collective-permute-start(f32[4,8,1024]{2,1,0:T(8,128)S(1)} %get-tuple-element.64), channel_id=1, source_target_pairs={{32,64},{64,32},{96,128},{128,96},{160,192},{192,160},{33,65},{65,... | collective-permute-start | bytes 393224 | tf_op jit(solution)/shard_map/ppermute | solution.py:457

commit v3 on v2

--- a/solution.py
+++ b/solution.py
@@ -12,6 +12,11 @@
 LANES = 128
 TILES = 8
 CHUNK = 8
+
+FIRST_HOP = [(1, 3), (6, 4), (0, 1), (7, 6), (3, 2), (4, 5), (2, 0), (5, 7)]
+SECOND_HOP = [(3, 5), (4, 2), (1, 3), (6, 4), (5, 6), (2, 1), (0, 7), (7, 0)]
+THIRD_HOP = [(5, 7), (2, 0), (4, 5), (3, 2), (7, 6), (0, 1), (1, 3), (6, 4)]
+LAST_PAIRS = [(1, 2), (2, 1), (3, 4), (4, 3), (5, 6), (6, 5), (0, 7), (7, 0)]
 SLOTS = 7
 
 VMEM = pl.BlockSpec(memory_space=pltpu.VMEM)
@@ -42,34 +47,33 @@
     return pl.ds(pl.multiple_of((core * 4 + (x & 3)) * LANES, LANES), LANES)
 
 
+def turned(tile, by):
+    return pltpu.roll(tile, by % LANES, axis=tile.ndim - 1)
+
+
+def lane_of(tile):
+    return lax.broadcasted_iota(jnp.int32, tile.shape, tile.ndim - 1)
+
+
+def neighbour(tile, by):
+    lane = lane_of(tile)
+    wraps = lane < TILES if by > 0 else lane >= LANES - TILES
+    return jnp.where(wraps, turned(tile, by * (TILES + 1)), turned(tile, by * TILES))
+
+
 def exchanged(tiles):
-    size = LANES // TILES
-    block = lax.broadcasted_iota(jnp.int32, tiles[0].shape, 1) // size
+    lane = lane_of(tiles[0])
     tiles = list(tiles)
     for bit in range(3):
         step = 1 << bit
-        upper = (block >> bit) & 1 == 1
+        upper = (lane >> bit) & 1 == 1
         for m in range(TILES):
             if m & step:
                 continue
             low, high = tiles[m], tiles[m + step]
-            tiles[m] = jnp.where(upper, turned(high, size * step), low)
-            tiles[m + step] = jnp.where(upper, high, turned(low, -size * step))
+            tiles[m] = jnp.where(upper, turned(high, step), low)
+            tiles[m + step] = jnp.where(upper, high, turned(low, -step))
     return tiles
-
-
-def shuffled(tiles, outer):
-    lane = lax.broadcasted_iota(jnp.int32, tiles[0].shape, 1)
-    source = (lane % outer) * (LANES // outer) + lane // outer
-    return [jnp.take_along_axis(tile, source, axis=1) for tile in tiles]
-
-
-def woven(tiles):
-    return exchanged(shuffled(tiles, LANES // TILES))
-
-
-def unwoven(tiles):
-    return shuffled(exchanged(tiles), TILES)
 
 
 def project(feats_in, gain_in, weight_in, bias_in, keep, send, feats, gain_column, bias_column, gain, weight, bias, wide, sums, sems):
@@ -109,7 +113,7 @@
         sums[m, 0 : 6 * rows] = made[0 : 6 * rows] + made[6 * rows : 12 * rows] + made[12 * rows :]
         values = block.astype(jnp.float32)
         sums[m, 6 * rows :] = jnp.sum(values * values, axis=1)
-    tiles = woven([sums[m] for m in range(TILES)])
+    tiles = exchanged([sums[m] for m in range(TILES)])
     for side in range(2):
 
         @pl.when(core == side)
@@ -121,8 +125,9 @@
 
 def weave_rows(first, feats, gain_column, gained):
     def step(h, carry):
-        line = feats[first + h].astype(jnp.float32) * gain_column[:, :1]
-        put(gained, h, [tile.reshape(-1, 8, LANES) for tile in woven(tiles_of(line))])
+        tiles = exchanged(tiles_of(feats[first + h]))
+        tiles = [tile.astype(jnp.float32) * gain_column[:, :1] for tile in tiles]
+        put(gained, h, [tile.reshape(-1, 8, LANES) for tile in tiles])
         return carry
 
     lax.fori_loop(0, gained.shape[0], step, 0, unroll=4)
@@ -170,16 +175,12 @@
     return lax.rsqrt(1.0 + jnp.exp(-(gate + bias)))
 
 
-def turned(tile, by):
-    return pltpu.roll(tile, by % LANES, axis=tile.ndim - 1)
-
-
 def tiles_of(line):
     return [line[..., m * LANES : (m + 1) * LANES] for m in range(TILES)]
 
 
 def widen(ref, index, tiles):
-    for m, tile in enumerate([turned(tiles[-1], 1), *tiles, turned(tiles[0], -1)]):
+    for m, tile in enumerate([neighbour(tiles[-1], 1), *tiles, neighbour(tiles[0], -1)]):
         ref[(*index, slice(m * LANES, (m + 1) * LANES))] = tile
 
 
@@ -196,7 +197,7 @@
 
 
 def two_rows(state, h1, h2, decay, drive, taps):
-    ends = [turned(state[-2], 1), turned(state[-1], 1)], [turned(state[0], -1), turned(state[1], -1)]
+    ends = [neighbour(tile, 1) for tile in state[-2:]], [neighbour(tile, -1) for tile in state[:2]]
     middle = row_step(ends[0] + state + ends[1], -1, h1, decay, drive, taps)
     return middle[1:-1], row_step(middle, 0, h2, decay, drive, taps)
 
@@ -352,12 +353,11 @@
     def mix(h, tiles):
         for m, tile in enumerate(tiles):
             at = slice(m * LANES, (m + 1) * LANES)
-            mixed[h, :, :, at] = kept[h, :, :, at] * tile
+            mixed[h, :, at] = (kept[h, :, :, at] * tile).reshape(chans, LANES).astype(mixed.dtype)
 
     def finish(h):
-        tiles = [mixed[h, :, :, m * LANES : (m + 1) * LANES].reshape(chans, LANES) for m in range(TILES)]
-        for m, tile in enumerate(unwoven(tiles)):
-            made[h, :, m * LANES : (m + 1) * LANES] = tile.astype(made.dtype)
+        for m, tile in enumerate(exchanged(tiles_of(mixed[h]))):
+            made[h, :, m * LANES : (m + 1) * LANES] = tile
         copy(h, h).start()
 
     def scan_all(state, upward, decay, drive, taps):
@@ -466,22 +466,21 @@
     )
     partner_taps, partner_decay = call(partner_side, (taps, wider), partner_raw, bias)
     partner = (partner_end, partner_decay, partner_taps)
-    for stage in (1, 2):
-        t = stage - 1
-        arrived = along_rows(leaving, [(2 * t + 1, 2 * t + 3), (6 - 2 * t, 4 - 2 * t)])
+    for stage, pairs in ((1, FIRST_HOP), (2, SECOND_HOP)):
+        arrived = along_rows(leaving, pairs)
         kept, leaving = call(
             functools.partial(far_stage, stage), (block, state), arrived, *partner, *far, kept, leaving,
             aliases={7: 0, 8: 1},
         )
-    near_in = along_rows(leaving, [(1, 2), (2, 1), (3, 4), (4, 3), (5, 6), (6, 5)])
-    far_in = along_rows(leaving, [(5, 7), (2, 0)])
+    near_in = along_rows(leaving, LAST_PAIRS)
+    far_in = along_rows(leaving, THIRD_HOP)
     return pl.pallas_call(
         last_stage,
         out_shape=jax.ShapeDtypeStruct(feats.shape, jnp.bfloat16),
         in_specs=[VMEM] * 12,
         out_specs=pl.BlockSpec(memory_space=pl.ANY),
         scratch_shapes=[
-            pltpu.VMEM(block.shape, block.dtype),
+            pltpu.VMEM(feats.shape, jnp.bfloat16),
             pltpu.VMEM(feats.shape, jnp.bfloat16),
             pltpu.SemaphoreType.DMA((rows,)),
         ],

time: 71.5 us -> 67.8 us (0.948)
  waiting for transfers between devices: 34.9 us -> 25.8 us
  starting transfers between devices: 18.4 us -> 27 us
  Pallas kernels: 17.2 us -> 14.5 us
    ppermute x6, waiting for transfers between devices: 24.5 us -> 12.7 us  [along_rows(): return lax.ppermute(value, 'rows', pairs)]
    ppermute x6, starting transfers between devices: 5.41 us -> 13.9 us  [along_rows(): return lax.ppermute(value, 'rows', pairs)]
    ppermute x14, waiting for transfers between devices: 10.4 us -> 13.1 us  [chan_shift(): return lax.ppermute(value, 'chan', [(i, target(i)) for i in range(32)])]
    pallas_call x10, Pallas kernels: 8.03 us -> 5.63 us  [call(): pl.pallas_call(kernel, out_shape=outs, in_specs=[VMEM] * len(args), out_s...]
  transfers between devices with their start and end apart: 20 -> 20, of which waited for: 11 -> 15; matrix products, arithmetic and copies ran while one was open for 0% -> 0% of each run, Pallas kernels for 10% -> 7%
where the time goes in v3:
time: 67.8 us; the launch traced here: 67.6 us
  starting transfers between devices  27 us (40%)
  waiting for transfers between devices  25.8 us (38%)
  Pallas kernels  14.5 us (21%)
    ppermute x6, starting transfers between devices, along_rows(): return lax.ppermute(value, 'rows', pairs)  13.9 us
    ppermute x14, waiting for transfers between devices, chan_shift(): return lax.ppermute(value, 'chan', [(i, target(i)) for i in range(32)])  13.1 us
    ppermute x14, starting transfers between devices, chan_shift(): return lax.ppermute(value, 'chan', [(i, target(i)) for i in range(32)])  13.1 us
    ppermute x6, waiting for transfers between devices, along_rows(): return lax.ppermute(value, 'rows', pairs)  12.7 us
    pallas_call x10, Pallas kernels, call(): pl.pallas_call(kernel, out_shape=outs, in_specs=[VMEM] * len(args), out_s...  5.63 us
    pallas_call x1, Pallas kernels, shards(): pl.pallas_call(last_stage, out_shape=jax.ShapeDtypeStruct(feats.shape, jn...  3.94 us
    pallas_call x1, Pallas kernels, shards(): pl.pallas_call(project, out_shape=(half, half, jax.ShapeDtypeStruct(feats...  2.57 us
    pallas_call x1, Pallas kernels, shards(): pl.pallas_call(near_side, out_shape=(taps, taps, line, line, lines, wider...  2.39 us
  transfers between devices with their start and end apart: 20, of which 15 were waited for; matrix products, arithmetic and copies ran while one was open for 0% of the time, Pallas kernels for 7%

profile of v3, /device:TPU:24, one launch (start us, length us, event | category | flops | bytes accessed | tf_op | source)
XLA Modules:
  0.0 67.6 jit_solution(17226241233196511863)
XLA Ops:
  0.0 2.6 %shard_map.46 = (f32[4,7,16,128]{3,2,1,0:T(8,128)S(1)}, f32[4,7,16,128]{3,2,1,0:T(8,128)S(1)}, bf16[16,32,1024]{2,1,0:T(8,128)(2,1)S(1)}, f32[32,128]{1,0:T(8,128)S(1)}, f32[32,128]{1,0:T(8,128)S(1)}) custom-call(bf16[16,32,1024]{2,1,0:T(8,128)(2,1)} %feats_in.1, f32[1,32]{1,0:T(1,128)} %bitcast.2, f32[8,32]{1,0:T(8,128)} %weight_in.1, f32[1,32]{1,0:T(1,128)} %bitcast.3), custom_call_target="tpu_custom_call" | custom-call | tf_op jit(solution)/shard_map/pallas_call | solution.py:417
  2.7 1.5 %collective-permute-done.arrived = f32[4,7,16,128]{3,2,1,0:T(8,128)S(1)} collective-permute-done((f32[4,7,16,128]{3,2,1,0:T(8,128)S(1)}, f32[4,7,16,128]{3,2,1,0:T(8,128)S(1)}, u32[]{:S(2)}, u32[]{:S(2)}) %collective-permute-start) | collective-permute-done | bytes 229408 | tf_op jit(solution)/shard_map/ppermute | solution.py:395
  4.2 1.6 %collective-permute-start.1 = (f32[7,16,128]{2,1,0:T(8,128)S(1)}, f32[7,16,128]{2,1,0:T(8,128)S(1)}, u32[]{:S(2)}, u32[]{:S(2)}) collective-permute-start(f32[7,16,128]{2,1,0:T(8,128)S(1)} %get-tuple-element.40), channel_id=1, source_target_pairs={{0,2},{1,3},{2,4},{3,5},{4,6},{5,7},{6,0},{7,1},{8,10},{9,11},{10,... | collective-permute-start | bytes 172040 | tf_op jit(solution)/shard_map/ppermute | solution.py:395
  5.8 2.7 %collective-permute-start.2 = (f32[7,16,128]{2,1,0:T(8,128)S(1)}, f32[7,16,128]{2,1,0:T(8,128)S(1)}, u32[]{:S(2)}, u32[]{:S(2)}) collective-permute-start(f32[7,16,128]{2,1,0:T(8,128)S(1)} %get-tuple-element.41), channel_id=1, source_target_pairs={{0,4},{1,5},{2,6},{3,7},{4,0},{5,1},{6,2},{7,3},{8,12},{9,13},{10,... | collective-permute-start | bytes 172040 | tf_op jit(solution)/shard_map/ppermute | solution.py:395
  8.5 1.4 %collective-permute-start.3 = (f32[7,16,128]{2,1,0:T(8,128)S(1)}, f32[7,16,128]{2,1,0:T(8,128)S(1)}, u32[]{:S(2)}, u32[]{:S(2)}) collective-permute-start(f32[7,16,128]{2,1,0:T(8,128)S(1)} %get-tuple-element.42), channel_id=1, source_target_pairs={{0,6},{1,7},{2,0},{3,1},{4,2},{5,3},{6,4},{7,5},{8,14},{9,15},{10,... | collective-permute-start | bytes 172040 | tf_op jit(solution)/shard_map/ppermute | solution.py:395
  9.9 0.8 %shard_map.49.upper = f32[8,4,8,1024]{3,2,1,0:T(8,128)S(1)} custom-call(bf16[16,32,1024]{2,1,0:T(8,128)(2,1)S(1)} %get-tuple-element.43.feats, f32[32,128]{1,0:T(8,128)S(1)} %get-tuple-element.44.gain_column), custom_call_target="tpu_custom_call" | custom-call | tf_op jit(solution)/shard_map/pallas_call | solution.py:26
  10.8 0.8 %collective-permute-done.2.c = f32[7,16,128]{2,1,0:T(8,128)S(1)} collective-permute-done((f32[7,16,128]{2,1,0:T(8,128)S(1)}, f32[7,16,128]{2,1,0:T(8,128)S(1)}, u32[]{:S(2)}, u32[]{:S(2)}) %collective-permute-start.2) | collective-permute-done | bytes 57376 | tf_op jit(solution)/shard_map/ppermute | solution.py:395
  11.6 1.0 %collective-permute-done.3.d = f32[7,16,128]{2,1,0:T(8,128)S(1)} collective-permute-done((f32[7,16,128]{2,1,0:T(8,128)S(1)}, f32[7,16,128]{2,1,0:T(8,128)S(1)}, u32[]{:S(2)}, u32[]{:S(2)}) %collective-permute-start.3) | collective-permute-done | bytes 57376 | tf_op jit(solution)/shard_map/ppermute | solution.py:395
  12.7 0.6 collective-permute-start.6
  13.3 2.3 %collective-permute-start.5 = (f32[7,16,128]{2,1,0:T(8,128)S(1)}, f32[7,16,128]{2,1,0:T(8,128)S(1)}, u32[]{:S(2)}, u32[]{:S(2)}) collective-permute-start(f32[7,16,128]{2,1,0:T(8,128)S(1)} %shard_map.48.a), channel_id=1, source_target_pairs={{0,16},{1,17},{2,18},{3,19},{4,20},{5,21},{6,22},{7,23},{8,24},{9,... | collective-permute-start | bytes 172040 | tf_op jit(solution)/shard_map/ppermute | solution.py:395
  15.6 0.8 %shard_map.51.lower = f32[8,4,8,1024]{3,2,1,0:T(8,128)S(1)} custom-call(bf16[16,32,1024]{2,1,0:T(8,128)(2,1)S(1)} %get-tuple-element.43.feats, f32[32,128]{1,0:T(8,128)S(1)} %get-tuple-element.44.gain_column), custom_call_target="tpu_custom_call" | custom-call | tf_op jit(solution)/shard_map/pallas_call | solution.py:26
  16.4 0.5 collective-permute-done.6.d
  16.9 2.0 %collective-permute-done.5.c = f32[7,16,128]{2,1,0:T(8,128)S(1)} collective-permute-done((f32[7,16,128]{2,1,0:T(8,128)S(1)}, f32[7,16,128]{2,1,0:T(8,128)S(1)}, u32[]{:S(2)}, u32[]{:S(2)}) %collective-permute-start.5) | collective-permute-done | bytes 57376 | tf_op jit(solution)/shard_map/ppermute | solution.py:395
  19.0 2.0 %collective-permute-done.4.b = f32[7,16,128]{2,1,0:T(8,128)S(1)} collective-permute-done((f32[7,16,128]{2,1,0:T(8,128)S(1)}, f32[7,16,128]{2,1,0:T(8,128)S(1)}, u32[]{:S(2)}, u32[]{:S(2)}) %collective-permute-start.4) | collective-permute-done | bytes 57376 | tf_op jit(solution)/shard_map/ppermute | solution.py:395
  21.0 0.6 collective-permute-start.9
  21.6 3.6 %collective-permute-start.8 = (f32[7,16,128]{2,1,0:T(8,128)S(1)}, f32[7,16,128]{2,1,0:T(8,128)S(1)}, u32[]{:S(2)}, u32[]{:S(2)}) collective-permute-start(f32[7,16,128]{2,1,0:T(8,128)S(1)} %shard_map.50.p0), channel_id=1, source_target_pairs={{0,4},{1,5},{2,6},{3,7},{4,0},{5,1},{6,2},{7,3},{8,12},{9,13},{10,... | collective-permute-start | bytes 172040 | tf_op jit(solution)/shard_map/ppermute | solution.py:395
  25.3 1.1 %collective-permute-done.9.p3 = f32[7,16,128]{2,1,0:T(8,128)S(1)} collective-permute-done((f32[7,16,128]{2,1,0:T(8,128)S(1)}, f32[7,16,128]{2,1,0:T(8,128)S(1)}, u32[]{:S(2)}, u32[]{:S(2)}) %collective-permute-start.9) | collective-permute-done | bytes 57376 | tf_op jit(solution)/shard_map/ppermute | solution.py:395
  26.5 1.5 %collective-permute-done.8.p2 = f32[7,16,128]{2,1,0:T(8,128)S(1)} collective-permute-done((f32[7,16,128]{2,1,0:T(8,128)S(1)}, f32[7,16,128]{2,1,0:T(8,128)S(1)}, u32[]{:S(2)}, u32[]{:S(2)}) %collective-permute-start.8) | collective-permute-done | bytes 57376 | tf_op jit(solution)/shard_map/ppermute | solution.py:395
  28.0 1.4 %collective-permute-done.7.p1 = f32[7,16,128]{2,1,0:T(8,128)S(1)} collective-permute-done((f32[7,16,128]{2,1,0:T(8,128)S(1)}, f32[7,16,128]{2,1,0:T(8,128)S(1)}, u32[]{:S(2)}, u32[]{:S(2)}) %collective-permute-start.7) | collective-permute-done | bytes 57376 | tf_op jit(solution)/shard_map/ppermute | solution.py:395
  29.4 1.2 %collective-permute-done.11.q1 = f32[7,16,128]{2,1,0:T(8,128)S(1)} collective-permute-done((f32[7,16,128]{2,1,0:T(8,128)S(1)}, f32[7,16,128]{2,1,0:T(8,128)S(1)}, u32[]{:S(2)}, u32[]{:S(2)}) %collective-permute-start.11) | collective-permute-done | bytes 57376 | tf_op jit(solution)/shard_map/ppermute | solution.py:395
  30.6 2.4 %shard_map.52 = (f32[3,16,1280]{2,1,0:T(8,128)S(1)}, f32[3,16,1280]{2,1,0:T(8,128)S(1)}, f32[16,1024]{1,0:T(8,128)S(1)}, f32[16,1024]{1,0:T(8,128)S(1)}, f32[3,1...) custom-call(f32[7,16,128]{2,1,0:T(8,128)S(1)} %shard_map.50.p0, ...), custom_call_target="tpu_custom_call" | custom-call | tf_op jit(solution)/shard_map/pallas_call | solution.py:447
  33.0 2.2 %collective-permute-start.14 = (f32[4,8,1024]{2,1,0:T(8,128)S(1)}, f32[4,8,1024]{2,1,0:T(8,128)S(1)}, u32[]{:S(2)}, u32[]{:S(2)}) collective-permute-start(f32[4,8,1024]{2,1,0:T(8,128)S(1)} %get-tuple-element.50), channel_id=1, source_target_pairs={{0,32},{32,0},{64,96},{96,64},{128,160},{160,128},{192,224},{224,1... | collective-permute-start | bytes 393224 | tf_op jit(solution)/shard_map/ppermute | solution.py:457
  35.3 1.7 %shard_map.53 = (f32[16,4,8,1280]{3,2,1,0:T(8,128)S(1)}, f32[16,4,8,1280]{3,2,1,0:T(8,128)S(1)}) custom-call(f32[16,1024]{1,0:T(8,128)S(1)} %get-tuple-element.51.far_gate, f32[16,1024]{1,0:T(8,128)S(1)} %get-tuple-element.52.inverse, f32[8,4,8,1024]{3,2,1,0:T(8,128)S(1)} %shard_map.49.upper, f32[8,4,8,1024]{3,2,1,0:T(8,128)S(1)} %shard_map.51.lower, ...), custom_call_target="tpu_custom_call" | custom-call | tf_op jit(solution)/shard_map/pallas_call | solution.py:26
  37.0 2.6 %collective-permute-done.14.refs_0_.refs_1_.partner_end = f32[4,8,1024]{2,1,0:T(8,128)S(1)} collective-permute-done((f32[4,8,1024]{2,1,0:T(8,128)S(1)}, f32[4,8,1024]{2,1,0:T(8,128)S(1)}, u32[]{:S(2)}, u32[]{:S(2)}) %collective-permute-start.14) | collective-permute-done | bytes 131104 | tf_op jit(solution)/shard_map/ppermute | solution.py:457
  39.9 2.6 %collective-permute-start.15 = (f32[4,8,1024]{2,1,0:T(8,128)S(1)}, f32[4,8,1024]{2,1,0:T(8,128)S(1)}, u32[]{:S(2)}, u32[]{:S(2)}) collective-permute-start(f32[4,8,1024]{2,1,0:T(8,128)S(1)} %get-tuple-element.57.refs_8_), channel_id=1, source_target_pairs={{32,96},{192,128},{0,32},{224,192},{96,64},{128,160},{64,0},{160,2... | collective-permute-start | bytes 393224 | tf_op jit(solution)/shard_map/ppermute | solution.py:457
  42.4 2.2 %collective-permute-done.16.raw = f32[3,16,1024]{2,1,0:T(8,128)S(1)} collective-permute-done((f32[3,16,1024]{2,1,0:T(8,128)S(1)}, f32[3,16,1024]{2,1,0:T(8,128)S(1)}, u32[]{:S(2)}, u32[]{:S(2)}) %collective-permute-start.16) | collective-permute-done | bytes 196640 | tf_op jit(solution)/shard_map/ppermute | solution.py:457
  44.6 1.4 %shard_map.55 = (f32[3,16,1280]{2,1,0:T(8,128)S(1)}, f32[16,4,8,1280]{3,2,1,0:T(8,128)S(1)}) custom-call(f32[3,16,1024]{2,1,0:T(8,128)S(1)} %collective-permute-done.16.raw, f32[32,128]{1,0:T(8,128)S(1)} %get-tuple-element.49.bias), custom_call_target="tpu_custom_call" | custom-call | tf_op jit(solution)/shard_map/pallas_call | solution.py:26
  46.4 5.7 %collective-permute-start.17 = (f32[4,8,1024]{2,1,0:T(8,128)S(1)}, f32[4,8,1024]{2,1,0:T(8,128)S(1)}, u32[]{:S(2)}, u32[]{:S(2)}) collective-permute-start(f32[4,8,1024]{2,1,0:T(8,128)S(1)} %get-tuple-element.62.refs_8_), channel_id=1, source_target_pairs={{96,160},{128,64},{32,96},{192,128},{160,192},{64,32},{0,224},{224... | collective-permute-start | bytes 393224 | tf_op jit(solution)/shard_map/ppermute | solution.py:457
  52.1 3.0 %collective-permute-done.17.refs_0_ = f32[4,8,1024]{2,1,0:T(8,128)S(1)} collective-permute-done((f32[4,8,1024]{2,1,0:T(8,128)S(1)}, f32[4,8,1024]{2,1,0:T(8,128)S(1)}, u32[]{:S(2)}, u32[]{:S(2)}) %collective-permute-start.17) | collective-permute-done | bytes 131104 | tf_op jit(solution)/shard_map/ppermute | solution.py:457
  55.6 3.1 %collective-permute-start.18 = (f32[4,8,1024]{2,1,0:T(8,128)S(1)}, f32[4,8,1024]{2,1,0:T(8,128)S(1)}, u32[]{:S(2)}, u32[]{:S(2)}) collective-permute-start(f32[4,8,1024]{2,1,0:T(8,128)S(1)} %get-tuple-element.64), channel_id=1, source_target_pairs={{32,64},{64,32},{96,128},{128,96},{160,192},{192,160},{0,224},{224... | collective-permute-start | bytes 393224 | tf_op jit(solution)/shard_map/ppermute | solution.py:457
  58.8 4.7 %collective-permute-done.19.far_in = f32[4,8,1024]{2,1,0:T(8,128)S(1)} collective-permute-done((f32[4,8,1024]{2,1,0:T(8,128)S(1)}, f32[4,8,1024]{2,1,0:T(8,128)S(1)}, u32[]{:S(2)}, u32[]{:S(2)}) %collective-permute-start.19) | collective-permute-done | bytes 131104 | tf_op jit(solution)/shard_map/ppermute | solution.py:457
  63.4 3.9 %shard_map.58 = bf16[16,32,1024]{2,1,0:T(8,128)(2,1)} custom-call(f32[4,8,1024]{2,1,0:T(8,128)S(1)} %collective-permute-done.18.near_in, f32[4,8,1024]{2,1,0:T(8,128)S(1)} %collective-permute-done.19.far_in, f32[4,8,1024]{2,1,0:T(8,128)S(1)} %collective-permute-done.14.refs_0_.refs_1_.partner_end, f32[16,4,8,1280]{3,2,1,0:T(8,128)S(1)} %get-tuple-element.59.refs_2_.pd, ...), custom_call_target="tpu_custom_call" | custom-call | tf_op jit(solution)/shard_map/pallas_call | solution.py:477
  (21 shorter events, 1.7 us)
Async XLA Ops:
  2.6 1.6 %collective-permute-start = (f32[4,7,16,128]{3,2,1,0:T(8,128)S(1)}, f32[4,7,16,128]{3,2,1,0:T(8,128)S(1)}, u32[]{:S(2)}, u32[]{:S(2)}) collective-permute-start(f32[4,7,16,128]{3,2,1,0:T(8,128)S(1)} %get-tuple-element.38), channel_id=1, source_target_pairs={{0,1},{1,0},{2,3},{3,2},{4,5},{5,4},{6,7},{7,6},{8,9},{9,8},{10,11... | collective-permute-start | bytes 688136 | tf_op jit(solution)/shard_map/ppermute | solution.py:395
  4.2 6.6 %collective-permute-start.1 = (f32[7,16,128]{2,1,0:T(8,128)S(1)}, f32[7,16,128]{2,1,0:T(8,128)S(1)}, u32[]{:S(2)}, u32[]{:S(2)}) collective-permute-start(f32[7,16,128]{2,1,0:T(8,128)S(1)} %get-tuple-element.40), channel_id=1, source_target_pairs={{0,2},{1,3},{2,4},{3,5},{4,6},{5,7},{6,0},{7,1},{8,10},{9,11},{10,... | collective-permute-start | bytes 172040 | tf_op jit(solution)/shard_map/ppermute | solution.py:395
  5.8 5.9 %collective-permute-start.2 = (f32[7,16,128]{2,1,0:T(8,128)S(1)}, f32[7,16,128]{2,1,0:T(8,128)S(1)}, u32[]{:S(2)}, u32[]{:S(2)}) collective-permute-start(f32[7,16,128]{2,1,0:T(8,128)S(1)} %get-tuple-element.41), channel_id=1, source_target_pairs={{0,4},{1,5},{2,6},{3,7},{4,0},{5,1},{6,2},{7,3},{8,12},{9,13},{10,... | collective-permute-start | bytes 172040 | tf_op jit(solution)/shard_map/ppermute | solution.py:395
  8.5 4.2 %collective-permute-start.3 = (f32[7,16,128]{2,1,0:T(8,128)S(1)}, f32[7,16,128]{2,1,0:T(8,128)S(1)}, u32[]{:S(2)}, u32[]{:S(2)}) collective-permute-start(f32[7,16,128]{2,1,0:T(8,128)S(1)} %get-tuple-element.42), channel_id=1, source_target_pairs={{0,6},{1,7},{2,0},{3,1},{4,2},{5,3},{6,4},{7,5},{8,14},{9,15},{10,... | collective-permute-start | bytes 172040 | tf_op jit(solution)/shard_map/ppermute | solution.py:395
  12.7 4.3 %collective-permute-start.6 = (f32[7,16,128]{2,1,0:T(8,128)S(1)}, f32[7,16,128]{2,1,0:T(8,128)S(1)}, u32[]{:S(2)}, u32[]{:S(2)}) collective-permute-start(f32[7,16,128]{2,1,0:T(8,128)S(1)} %shard_map.48.a), channel_id=1, source_target_pairs={{0,8},{1,9},{2,10},{3,11},{4,12},{5,13},{6,14},{7,15},{8,16},{9,17... | collective-permute-start | bytes 172040 | tf_op jit(solution)/shard_map/ppermute | solution.py:395
  13.3 5.7 %collective-permute-start.5 = (f32[7,16,128]{2,1,0:T(8,128)S(1)}, f32[7,16,128]{2,1,0:T(8,128)S(1)}, u32[]{:S(2)}, u32[]{:S(2)}) collective-permute-start(f32[7,16,128]{2,1,0:T(8,128)S(1)} %shard_map.48.a), channel_id=1, source_target_pairs={{0,16},{1,17},{2,18},{3,19},{4,20},{5,21},{6,22},{7,23},{8,24},{9,... | collective-permute-start | bytes 172040 | tf_op jit(solution)/shard_map/ppermute | solution.py:395
  15.6 5.4 %collective-permute-start.4 = (f32[7,16,128]{2,1,0:T(8,128)S(1)}, f32[7,16,128]{2,1,0:T(8,128)S(1)}, u32[]{:S(2)}, u32[]{:S(2)}) collective-permute-start(f32[7,16,128]{2,1,0:T(8,128)S(1)} %shard_map.48.a), channel_id=1, source_target_pairs={{0,24},{1,25},{2,26},{3,27},{4,28},{5,29},{6,30},{7,31},{8,0},{9,1... | collective-permute-start | bytes 172040 | tf_op jit(solution)/shard_map/ppermute | solution.py:395
  21.0 5.5 %collective-permute-start.9 = (f32[7,16,128]{2,1,0:T(8,128)S(1)}, f32[7,16,128]{2,1,0:T(8,128)S(1)}, u32[]{:S(2)}, u32[]{:S(2)}) collective-permute-start(f32[7,16,128]{2,1,0:T(8,128)S(1)} %shard_map.50.p0), channel_id=1, source_target_pairs={{0,2},{1,3},{2,4},{3,5},{4,6},{5,7},{6,0},{7,1},{8,10},{9,11},{10,... | collective-permute-start | bytes 172040 | tf_op jit(solution)/shard_map/ppermute | solution.py:395
  21.6 6.4 %collective-permute-start.8 = (f32[7,16,128]{2,1,0:T(8,128)S(1)}, f32[7,16,128]{2,1,0:T(8,128)S(1)}, u32[]{:S(2)}, u32[]{:S(2)}) collective-permute-start(f32[7,16,128]{2,1,0:T(8,128)S(1)} %shard_map.50.p0), channel_id=1, source_target_pairs={{0,4},{1,5},{2,6},{3,7},{4,0},{5,1},{6,2},{7,3},{8,12},{9,13},{10,... | collective-permute-start | bytes 172040 | tf_op jit(solution)/shard_map/ppermute | solution.py:395
  25.2 4.2 %collective-permute-start.7 = (f32[7,16,128]{2,1,0:T(8,128)S(1)}, f32[7,16,128]{2,1,0:T(8,128)S(1)}, u32[]{:S(2)}, u32[]{:S(2)}) collective-permute-start(f32[7,16,128]{2,1,0:T(8,128)S(1)} %shard_map.50.p0), channel_id=1, source_target_pairs={{0,6},{1,7},{2,0},{3,1},{4,2},{5,3},{6,4},{7,5},{8,14},{9,15},{10,... | collective-permute-start | bytes 172040 | tf_op jit(solution)/shard_map/ppermute | solution.py:395
  25.3 4.1 %collective-permute-start.10 = (f32[7,16,128]{2,1,0:T(8,128)S(1)}, f32[7,16,128]{2,1,0:T(8,128)S(1)}, u32[]{:S(2)}, u32[]{:S(2)}) collective-permute-start(f32[7,16,128]{2,1,0:T(8,128)S(1)} %shard_map.50.p0), channel_id=1, source_target_pairs={{0,1},{1,0},{2,3},{3,2},{4,5},{5,4},{6,7},{7,6},{8,9},{9,8},{10,11... | collective-permute-start | bytes 172040 | tf_op jit(solution)/shard_map/ppermute | solution.py:395
  26.5 2.9 %collective-permute-start.13 = (f32[7,16,128]{2,1,0:T(8,128)S(1)}, f32[7,16,128]{2,1,0:T(8,128)S(1)}, u32[]{:S(2)}, u32[]{:S(2)}) collective-permute-start(f32[7,16,128]{2,1,0:T(8,128)S(1)} %collective-permute-done.9.p3), channel_id=1, source_target_pairs={{0,1},{1,0},{2,3},{3,2},{4,5},{5,4},{6,7},{7,6},{8,9},{9,8},{10,11... | collective-permute-start | bytes 172040 | tf_op jit(solution)/shard_map/ppermute | solution.py:395
  28.0 1.4 %collective-permute-start.12 = (f32[7,16,128]{2,1,0:T(8,128)S(1)}, f32[7,16,128]{2,1,0:T(8,128)S(1)}, u32[]{:S(2)}, u32[]{:S(2)}) collective-permute-start(f32[7,16,128]{2,1,0:T(8,128)S(1)} %collective-permute-done.8.p2), channel_id=1, source_target_pairs={{0,1},{1,0},{2,3},{3,2},{4,5},{5,4},{6,7},{7,6},{8,9},{9,8},{10,11... | collective-permute-start | bytes 172040 | tf_op jit(solution)/shard_map/ppermute | solution.py:395
  29.4 1.2 %collective-permute-start.11 = (f32[7,16,128]{2,1,0:T(8,128)S(1)}, f32[7,16,128]{2,1,0:T(8,128)S(1)}, u32[]{:S(2)}, u32[]{:S(2)}) collective-permute-start(f32[7,16,128]{2,1,0:T(8,128)S(1)} %collective-permute-done.7.p1), channel_id=1, source_target_pairs={{0,1},{1,0},{2,3},{3,2},{4,5},{5,4},{6,7},{7,6},{8,9},{9,8},{10,11... | collective-permute-start | bytes 172040 | tf_op jit(solution)/shard_map/ppermute | solution.py:395
  33.0 6.6 %collective-permute-start.14 = (f32[4,8,1024]{2,1,0:T(8,128)S(1)}, f32[4,8,1024]{2,1,0:T(8,128)S(1)}, u32[]{:S(2)}, u32[]{:S(2)}) collective-permute-start(f32[4,8,1024]{2,1,0:T(8,128)S(1)} %get-tuple-element.50), channel_id=1, source_target_pairs={{0,32},{32,0},{64,96},{96,64},{128,160},{160,128},{192,224},{224,1... | collective-permute-start | bytes 393224 | tf_op jit(solution)/shard_map/ppermute | solution.py:457
  35.2 9.4 %collective-permute-start.16 = (f32[3,16,1024]{2,1,0:T(8,128)S(1)}, f32[3,16,1024]{2,1,0:T(8,128)S(1)}, u32[]{:S(2)}, u32[]{:S(2)}) collective-permute-start(f32[3,16,1024]{2,1,0:T(8,128)S(1)} %get-tuple-element.58), channel_id=1, source_target_pairs={{0,32},{32,0},{64,96},{96,64},{128,160},{160,128},{192,224},{224,1... | collective-permute-start | bytes 589832 | tf_op jit(solution)/shard_map/ppermute | solution.py:457
  39.9 6.3 %collective-permute-start.15 = (f32[4,8,1024]{2,1,0:T(8,128)S(1)}, f32[4,8,1024]{2,1,0:T(8,128)S(1)}, u32[]{:S(2)}, u32[]{:S(2)}) collective-permute-start(f32[4,8,1024]{2,1,0:T(8,128)S(1)} %get-tuple-element.57.refs_8_), channel_id=1, source_target_pairs={{32,96},{192,128},{0,32},{224,192},{96,64},{128,160},{64,0},{160,2... | collective-permute-start | bytes 393224 | tf_op jit(solution)/shard_map/ppermute | solution.py:457
  46.4 8.7 %collective-permute-start.17 = (f32[4,8,1024]{2,1,0:T(8,128)S(1)}, f32[4,8,1024]{2,1,0:T(8,128)S(1)}, u32[]{:S(2)}, u32[]{:S(2)}) collective-permute-start(f32[4,8,1024]{2,1,0:T(8,128)S(1)} %get-tuple-element.62.refs_8_), channel_id=1, source_target_pairs={{96,160},{128,64},{32,96},{192,128},{160,192},{64,32},{0,224},{224... | collective-permute-start | bytes 393224 | tf_op jit(solution)/shard_map/ppermute | solution.py:457
  55.4 8.1 %collective-permute-start.19 = (f32[4,8,1024]{2,1,0:T(8,128)S(1)}, f32[4,8,1024]{2,1,0:T(8,128)S(1)}, u32[]{:S(2)}, u32[]{:S(2)}) collective-permute-start(f32[4,8,1024]{2,1,0:T(8,128)S(1)} %get-tuple-element.64), channel_id=1, source_target_pairs={{160,224},{64,0},{128,160},{96,64},{224,192},{0,32},{32,96},{192,1... | collective-permute-start | bytes 393224 | tf_op jit(solution)/shard_map/ppermute | solution.py:457
  55.6 7.8 %collective-permute-start.18 = (f32[4,8,1024]{2,1,0:T(8,128)S(1)}, f32[4,8,1024]{2,1,0:T(8,128)S(1)}, u32[]{:S(2)}, u32[]{:S(2)}) collective-permute-start(f32[4,8,1024]{2,1,0:T(8,128)S(1)} %get-tuple-element.64), channel_id=1, source_target_pairs={{32,64},{64,32},{96,128},{128,96},{160,192},{192,160},{0,224},{224... | collective-permute-start | bytes 393224 | tf_op jit(solution)/shard_map/ppermute | solution.py:457

commit v4 on v3

--- a/solution.py
+++ b/solution.py
@@ -235,7 +235,12 @@
         widen(taps, (k, slice(None)), tiles_of(tap))
 
 
-def near_side(p0, p1, p2, p3, q0, q1, q2, q3, upper, lower, bias, near_taps, far_taps, far_gate, inverse, raw, decay, drive, kept, end, far_raw):
+def half_line(core, half):
+    size = half.shape[2]
+    return pl.ds(pl.multiple_of(core * size, LANES), size)
+
+
+def near_side(p0, p1, p2, p3, q0, q1, q2, q3, upper, lower, bias, near_taps, far_taps, far_gate, inverse, raw, decay, drive, kept, end, raw_half, far_raw):
     core, x = place()
     odd = parity()
     rows = raw.shape[1]
@@ -249,6 +254,7 @@
                 far_raw[k, :, at] = piece[far + k]
             far_gate[:, at] = piece[far + 2]
             inverse[:, at] = piece[6]
+    raw_half[...] = raw[:, :, half_line(core, raw_half)]
     put_taps(near_taps, raw[0], raw[1])
     put_taps(far_taps, far_raw[0], far_raw[1])
     bias_column = bias[:, :1]
@@ -277,18 +283,25 @@
     lax.fori_loop(0, decay.shape[0], step, 0, unroll=4)
 
 
-def partner_side(raw, bias, taps, decay):
-    bias_column = bias[:, :1]
-    put_taps(taps, raw[0], raw[1])
-    every = slice(None)
-
-    def step(h, carry):
-        root = rate_root(raw[2, pl.ds(h, 1), :], bias_column)
-        line = (1.0 - root * root).reshape(*decay.shape[1:3], raw.shape[2])
-        widen(decay, (h, every, every), tiles_of(line))
-        return carry
-
-    lax.fori_loop(0, decay.shape[0], step, 0, unroll=4)
+def partner_side(first, own_half, other_half, bias, taps, decay, raw):
+    core, _ = place()
+    _, when = turn()
+
+    @pl.when(when == 1 if first else when > 1)
+    def _():
+        bias_column = bias[:, :1]
+        raw[:, :, half_line(core, own_half)] = own_half[...]
+        raw[:, :, half_line(core ^ 1, own_half)] = other_half[...]
+        put_taps(taps, raw[0], raw[1])
+        every = slice(None)
+
+        def step(h, carry):
+            root = rate_root(raw[2, pl.ds(h, 1), :], bias_column)
+            line = (1.0 - root * root).reshape(*decay.shape[1:3], raw.shape[2])
+            widen(decay, (h, every, every), tiles_of(line))
+            return carry
+
+        lax.fori_loop(0, decay.shape[0], step, 0, unroll=4)
 
 
 def scan_rows(state, upward, decay, drive, taps, emit):
@@ -444,11 +457,11 @@
     wider = f32(rows, chans // 8, 8, cols + 2 * LANES)
     taps = f32(3, rows, cols + 2 * LANES)
     line, lines = f32(rows, cols), f32(3, rows, cols)
-    near_taps, far_taps, far_gate, inverse, raw, near_decay, near_drive, kept, end = pl.pallas_call(
+    near_taps, far_taps, far_gate, inverse, _, near_decay, near_drive, kept, end, raw_half = pl.pallas_call(
         near_side,
-        out_shape=(taps, taps, line, line, lines, wider, wider, block, state),
+        out_shape=(taps, taps, line, line, lines, wider, wider, block, state, f32(3, rows, cols // 2)),
         in_specs=[VMEM] * 11,
-        out_specs=(VMEM,) * 9,
+        out_specs=(VMEM,) * 10,
         scratch_shapes=[pltpu.VMEM((2, rows, cols), jnp.float32)],
         compiler_params=pltpu.CompilerParams(vmem_limit_bytes=24 << 20),
     )(*pieces, *gained, bias)
@@ -460,14 +473,24 @@
     partner_end = along_rows(end, swap)
     far_decay, far_drive = call(far_side, (wider, wider), far_gate, inverse, *gained, bias)
     far = (far_decay, far_drive, far_taps)
-    partner_raw = along_rows(raw, swap)
+    own_half = along_rows(raw_half, swap)
+    other_half = other_core(own_half)
     kept, leaving = call(
         functools.partial(far_stage, 0), (block, state), partner_end, partner_end, *far, kept, aliases={5: 0}
     )
-    partner_taps, partner_decay = call(partner_side, (taps, wider), partner_raw, bias)
-    partner = (partner_end, partner_decay, partner_taps)
     for stage, pairs in ((1, FIRST_HOP), (2, SECOND_HOP)):
         arrived = along_rows(leaving, pairs)
+        if stage == 2:
+            leaving, own_half = lax.optimization_barrier((leaving, own_half))
+        partner_taps, partner_decay = pl.pallas_call(
+            functools.partial(partner_side, stage == 1),
+            out_shape=(taps, wider),
+            in_specs=[VMEM] * 3,
+            out_specs=(VMEM,) * 2,
+            scratch_shapes=[pltpu.VMEM((3, rows, cols), jnp.float32)],
+            compiler_params=pltpu.CompilerParams(vmem_limit_bytes=24 << 20),
+        )(own_half, other_half, bias)
+        partner = (partner_end, partner_decay, partner_taps)
         kept, leaving = call(
             functools.partial(far_stage, stage), (block, state), arrived, *partner, *far, kept, leaving,
             aliases={7: 0, 8: 1},

time: 67.8 us -> 67.5 us (level)
  Pallas kernels: 14.5 us -> 15.2 us
    ppermute x6, waiting for transfers between devices: 12.7 us -> 10.7 us  [along_rows(): return lax.ppermute(value, 'rows', pairs)]
    pallas_call x0 -> x2, Pallas kernels: none -> 1.38 us  [shards(): pl.pallas_call(functools.partial(partner_side, stage == 1), out_shape=(ta...]
    pallas_call x10 -> x9, Pallas kernels: 5.63 us -> 4.26 us  [call(): pl.pallas_call(kernel, out_shape=outs, in_specs=[VMEM] * len(args), out_s...]
    ppermute x14 -> x15, waiting for transfers between devices: 13.1 us -> 14.4 us  [chan_shift(): return lax.ppermute(value, 'chan', [(i, target(i)) for i in range(32)])]
    pallas_call x1, Pallas kernels: 2.39 us -> 3.08 us  [shards(): pl.pallas_call(near_side, out_shape=(taps, taps, line, line, lines, wider...]
    ppermute x14 -> x15, starting transfers between devices: 13.1 us -> 13.1 us  [chan_shift(): return lax.ppermute(value, 'chan', [(i, target(i)) for i in range(32)])]
  transfers between devices with their start and end apart: 20 -> 21, of which waited for: 15 -> 15; matrix products, arithmetic and copies ran while one was open for 0% -> 0% of each run, Pallas kernels for 7% -> 7%
where the time goes in v4:
time: 67.5 us; the launch traced here: 67.4 us
  starting transfers between devices  26.7 us (40%)
  waiting for transfers between devices  25.2 us (37%)
  Pallas kernels  15.2 us (23%)
    ppermute x15, waiting for transfers between devices, chan_shift(): return lax.ppermute(value, 'chan', [(i, target(i)) for i in range(32)])  14.4 us
    ppermute x6, starting transfers between devices, along_rows(): return lax.ppermute(value, 'rows', pairs)  13.6 us
    ppermute x15, starting transfers between devices, chan_shift(): return lax.ppermute(value, 'chan', [(i, target(i)) for i in range(32)])  13.1 us
    ppermute x6, waiting for transfers between devices, along_rows(): return lax.ppermute(value, 'rows', pairs)  10.7 us
    pallas_call x9, Pallas kernels, call(): pl.pallas_call(kernel, out_shape=outs, in_specs=[VMEM] * len(args), out_s...  4.26 us
    pallas_call x1, Pallas kernels, shards(): pl.pallas_call(last_stage, out_shape=jax.ShapeDtypeStruct(feats.shape, jn...  3.94 us
    pallas_call x1, Pallas kernels, shards(): pl.pallas_call(near_side, out_shape=(taps, taps, line, line, lines, wider...  3.08 us
    pallas_call x1, Pallas kernels, shards(): pl.pallas_call(project, out_shape=(half, half, jax.ShapeDtypeStruct(feats...  2.57 us
  transfers between devices with their start and end apart: 21, of which 15 were waited for; matrix products, arithmetic and copies ran while one was open for 0% of the time, Pallas kernels for 7%

profile of v4, /device:TPU:24, one launch (start us, length us, event | category | flops | bytes accessed | tf_op | source)
XLA Modules:
  0.0 67.4 jit_solution(12736383307504155407)
XLA Ops:
  0.0 2.6 %shard_map.46 = (f32[4,7,16,128]{3,2,1,0:T(8,128)S(1)}, f32[4,7,16,128]{3,2,1,0:T(8,128)S(1)}, bf16[16,32,1024]{2,1,0:T(8,128)(2,1)S(1)}, f32[32,128]{1,0:T(8,128)S(1)}, f32[32,128]{1,0:T(8,128)S(1)}) custom-call(bf16[16,32,1024]{2,1,0:T(8,128)(2,1)} %feats_in.1, f32[1,32]{1,0:T(1,128)} %bitcast.2, f32[8,32]{1,0:T(8,128)} %weight_in.1, f32[1,32]{1,0:T(1,128)} %bitcast.3), custom_call_target="tpu_custom_call" | custom-call | tf_op jit(solution)/shard_map/pallas_call | solution.py:430
  2.7 1.5 %collective-permute-done.arrived = f32[4,7,16,128]{3,2,1,0:T(8,128)S(1)} collective-permute-done((f32[4,7,16,128]{3,2,1,0:T(8,128)S(1)}, f32[4,7,16,128]{3,2,1,0:T(8,128)S(1)}, u32[]{:S(2)}, u32[]{:S(2)}) %collective-permute-start) | collective-permute-done | bytes 229408 | tf_op jit(solution)/shard_map/ppermute | solution.py:408
  4.2 1.6 %collective-permute-start.1 = (f32[7,16,128]{2,1,0:T(8,128)S(1)}, f32[7,16,128]{2,1,0:T(8,128)S(1)}, u32[]{:S(2)}, u32[]{:S(2)}) collective-permute-start(f32[7,16,128]{2,1,0:T(8,128)S(1)} %get-tuple-element.44), channel_id=1, source_target_pairs={{0,2},{1,3},{2,4},{3,5},{4,6},{5,7},{6,0},{7,1},{8,10},{9,11},{10,... | collective-permute-start | bytes 172040 | tf_op jit(solution)/shard_map/ppermute | solution.py:408
  5.8 2.7 %collective-permute-start.2 = (f32[7,16,128]{2,1,0:T(8,128)S(1)}, f32[7,16,128]{2,1,0:T(8,128)S(1)}, u32[]{:S(2)}, u32[]{:S(2)}) collective-permute-start(f32[7,16,128]{2,1,0:T(8,128)S(1)} %get-tuple-element.45), channel_id=1, source_target_pairs={{0,4},{1,5},{2,6},{3,7},{4,0},{5,1},{6,2},{7,3},{8,12},{9,13},{10,... | collective-permute-start | bytes 172040 | tf_op jit(solution)/shard_map/ppermute | solution.py:408
  8.5 1.4 %collective-permute-start.3 = (f32[7,16,128]{2,1,0:T(8,128)S(1)}, f32[7,16,128]{2,1,0:T(8,128)S(1)}, u32[]{:S(2)}, u32[]{:S(2)}) collective-permute-start(f32[7,16,128]{2,1,0:T(8,128)S(1)} %get-tuple-element.46), channel_id=1, source_target_pairs={{0,6},{1,7},{2,0},{3,1},{4,2},{5,3},{6,4},{7,5},{8,14},{9,15},{10,... | collective-permute-start | bytes 172040 | tf_op jit(solution)/shard_map/ppermute | solution.py:408
  9.9 0.8 %shard_map.49.upper = f32[8,4,8,1024]{3,2,1,0:T(8,128)S(1)} custom-call(bf16[16,32,1024]{2,1,0:T(8,128)(2,1)S(1)} %get-tuple-element.47.feats, f32[32,128]{1,0:T(8,128)S(1)} %get-tuple-element.48.gain_column), custom_call_target="tpu_custom_call" | custom-call | tf_op jit(solution)/shard_map/pallas_call | solution.py:26
  10.8 0.8 %collective-permute-done.2.c = f32[7,16,128]{2,1,0:T(8,128)S(1)} collective-permute-done((f32[7,16,128]{2,1,0:T(8,128)S(1)}, f32[7,16,128]{2,1,0:T(8,128)S(1)}, u32[]{:S(2)}, u32[]{:S(2)}) %collective-permute-start.2) | collective-permute-done | bytes 57376 | tf_op jit(solution)/shard_map/ppermute | solution.py:408
  11.6 1.0 %collective-permute-done.3.d = f32[7,16,128]{2,1,0:T(8,128)S(1)} collective-permute-done((f32[7,16,128]{2,1,0:T(8,128)S(1)}, f32[7,16,128]{2,1,0:T(8,128)S(1)}, u32[]{:S(2)}, u32[]{:S(2)}) %collective-permute-start.3) | collective-permute-done | bytes 57376 | tf_op jit(solution)/shard_map/ppermute | solution.py:408
  12.7 0.6 collective-permute-start.6
  13.3 2.3 %collective-permute-start.5 = (f32[7,16,128]{2,1,0:T(8,128)S(1)}, f32[7,16,128]{2,1,0:T(8,128)S(1)}, u32[]{:S(2)}, u32[]{:S(2)}) collective-permute-start(f32[7,16,128]{2,1,0:T(8,128)S(1)} %shard_map.48.a), channel_id=1, source_target_pairs={{0,16},{1,17},{2,18},{3,19},{4,20},{5,21},{6,22},{7,23},{8,24},{9,... | collective-permute-start | bytes 172040 | tf_op jit(solution)/shard_map/ppermute | solution.py:408
  15.6 0.8 %shard_map.51.lower = f32[8,4,8,1024]{3,2,1,0:T(8,128)S(1)} custom-call(bf16[16,32,1024]{2,1,0:T(8,128)(2,1)S(1)} %get-tuple-element.47.feats, f32[32,128]{1,0:T(8,128)S(1)} %get-tuple-element.48.gain_column), custom_call_target="tpu_custom_call" | custom-call | tf_op jit(solution)/shard_map/pallas_call | solution.py:26
  16.9 2.0 %collective-permute-done.5.c = f32[7,16,128]{2,1,0:T(8,128)S(1)} collective-permute-done((f32[7,16,128]{2,1,0:T(8,128)S(1)}, f32[7,16,128]{2,1,0:T(8,128)S(1)}, u32[]{:S(2)}, u32[]{:S(2)}) %collective-permute-start.5) | collective-permute-done | bytes 57376 | tf_op jit(solution)/shard_map/ppermute | solution.py:408
  19.0 2.0 %collective-permute-done.4.b = f32[7,16,128]{2,1,0:T(8,128)S(1)} collective-permute-done((f32[7,16,128]{2,1,0:T(8,128)S(1)}, f32[7,16,128]{2,1,0:T(8,128)S(1)}, u32[]{:S(2)}, u32[]{:S(2)}) %collective-permute-start.4) | collective-permute-done | bytes 57376 | tf_op jit(solution)/shard_map/ppermute | solution.py:408
  21.0 0.6 collective-permute-start.9
  21.6 3.6 %collective-permute-start.8 = (f32[7,16,128]{2,1,0:T(8,128)S(1)}, f32[7,16,128]{2,1,0:T(8,128)S(1)}, u32[]{:S(2)}, u32[]{:S(2)}) collective-permute-start(f32[7,16,128]{2,1,0:T(8,128)S(1)} %shard_map.50.p0), channel_id=1, source_target_pairs={{0,4},{1,5},{2,6},{3,7},{4,0},{5,1},{6,2},{7,3},{8,12},{9,13},{10,... | collective-permute-start | bytes 172040 | tf_op jit(solution)/shard_map/ppermute | solution.py:408
  25.3 1.1 %collective-permute-done.9.p3 = f32[7,16,128]{2,1,0:T(8,128)S(1)} collective-permute-done((f32[7,16,128]{2,1,0:T(8,128)S(1)}, f32[7,16,128]{2,1,0:T(8,128)S(1)}, u32[]{:S(2)}, u32[]{:S(2)}) %collective-permute-start.9) | collective-permute-done | bytes 57376 | tf_op jit(solution)/shard_map/ppermute | solution.py:408
  26.5 1.5 %collective-permute-done.8.p2 = f32[7,16,128]{2,1,0:T(8,128)S(1)} collective-permute-done((f32[7,16,128]{2,1,0:T(8,128)S(1)}, f32[7,16,128]{2,1,0:T(8,128)S(1)}, u32[]{:S(2)}, u32[]{:S(2)}) %collective-permute-start.8) | collective-permute-done | bytes 57376 | tf_op jit(solution)/shard_map/ppermute | solution.py:408
  28.0 1.4 %collective-permute-done.7.p1 = f32[7,16,128]{2,1,0:T(8,128)S(1)} collective-permute-done((f32[7,16,128]{2,1,0:T(8,128)S(1)}, f32[7,16,128]{2,1,0:T(8,128)S(1)}, u32[]{:S(2)}, u32[]{:S(2)}) %collective-permute-start.7) | collective-permute-done | bytes 57376 | tf_op jit(solution)/shard_map/ppermute | solution.py:408
  29.4 1.2 %collective-permute-done.11.q1 = f32[7,16,128]{2,1,0:T(8,128)S(1)} collective-permute-done((f32[7,16,128]{2,1,0:T(8,128)S(1)}, f32[7,16,128]{2,1,0:T(8,128)S(1)}, u32[]{:S(2)}, u32[]{:S(2)}) %collective-permute-start.11) | collective-permute-done | bytes 57376 | tf_op jit(solution)/shard_map/ppermute | solution.py:408
  30.6 3.1 %shard_map.52 = (f32[3,16,1280]{2,1,0:T(8,128)S(1)}, f32[3,16,1280]{2,1,0:T(8,128)S(1)}, f32[16,1024]{1,0:T(8,128)S(1)}, f32[16,1024]{1,0:T(8,128)S(1)}, f32[3,1...) custom-call(f32[7,16,128]{2,1,0:T(8,128)S(1)} %shard_map.50.p0, ...), custom_call_target="tpu_custom_call" | custom-call | tf_op jit(solution)/shard_map/pallas_call | solution.py:460
  33.7 1.9 %collective-permute-start.14 = (f32[4,8,1024]{2,1,0:T(8,128)S(1)}, f32[4,8,1024]{2,1,0:T(8,128)S(1)}, u32[]{:S(2)}, u32[]{:S(2)}) collective-permute-start(f32[4,8,1024]{2,1,0:T(8,128)S(1)} %get-tuple-element.54), channel_id=1, source_target_pairs={{0,32},{32,0},{64,96},{96,64},{128,160},{160,128},{192,224},{224,1... | collective-permute-start | bytes 393224 | tf_op jit(solution)/shard_map/ppermute | solution.py:470
  35.7 1.7 %shard_map.53 = (f32[16,4,8,1280]{3,2,1,0:T(8,128)S(1)}, f32[16,4,8,1280]{3,2,1,0:T(8,128)S(1)}) custom-call(f32[16,1024]{1,0:T(8,128)S(1)} %get-tuple-element.55.far_gate, f32[16,1024]{1,0:T(8,128)S(1)} %get-tuple-element.56.inverse, f32[8,4,8,1024]{3,2,1,0:T(8,128)S(1)} %shard_map.49.upper, f32[8,4,8,1024]{3,2,1,0:T(8,128)S(1)} %shard_map.51.lower, ...), custom_call_target="tpu_custom_call" | custom-call | tf_op jit(solution)/shard_map/pallas_call | solution.py:26
  37.4 2.6 %collective-permute-done.14.refs_0_.refs_1_.partner_end = f32[4,8,1024]{2,1,0:T(8,128)S(1)} collective-permute-done((f32[4,8,1024]{2,1,0:T(8,128)S(1)}, f32[4,8,1024]{2,1,0:T(8,128)S(1)}, u32[]{:S(2)}, u32[]{:S(2)}) %collective-permute-start.14) | collective-permute-done | bytes 131104 | tf_op jit(solution)/shard_map/ppermute | solution.py:470
  40.3 2.5 %collective-permute-start.15 = (f32[4,8,1024]{2,1,0:T(8,128)S(1)}, f32[4,8,1024]{2,1,0:T(8,128)S(1)}, u32[]{:S(2)}, u32[]{:S(2)}) collective-permute-start(f32[4,8,1024]{2,1,0:T(8,128)S(1)} %get-tuple-element.61.refs_8_), channel_id=1, source_target_pairs={{32,96},{192,128},{0,32},{224,192},{96,64},{128,160},{64,0},{160,2... | collective-permute-start | bytes 393224 | tf_op jit(solution)/shard_map/ppermute | solution.py:470
  42.9 1.3 %collective-permute-done.17.other_half = f32[3,16,512]{2,1,0:T(8,128)S(1)} collective-permute-done((f32[3,16,512]{2,1,0:T(8,128)S(1)}, f32[3,16,512]{2,1,0:T(8,128)S(1)}, u32[]{:S(2)}, u32[]{:S(2)}) %collective-permute-start.17) | collective-permute-done | bytes 98336 | tf_op jit(solution)/shard_map/ppermute | solution.py:408
  44.2 2.4 %collective-permute-done.15.refs_0_ = f32[4,8,1024]{2,1,0:T(8,128)S(1)} collective-permute-done((f32[4,8,1024]{2,1,0:T(8,128)S(1)}, f32[4,8,1024]{2,1,0:T(8,128)S(1)}, u32[]{:S(2)}, u32[]{:S(2)}) %collective-permute-start.15) | collective-permute-done | bytes 131104 | tf_op jit(solution)/shard_map/ppermute | solution.py:470
  46.9 5.6 %collective-permute-start.18 = (f32[4,8,1024]{2,1,0:T(8,128)S(1)}, f32[4,8,1024]{2,1,0:T(8,128)S(1)}, u32[]{:S(2)}, u32[]{:S(2)}) collective-permute-start(f32[4,8,1024]{2,1,0:T(8,128)S(1)} %get-tuple-element.71.refs_8_), channel_id=1, source_target_pairs={{96,160},{128,64},{32,96},{192,128},{160,192},{64,32},{0,224},{224... | collective-permute-start | bytes 393224 | tf_op jit(solution)/shard_map/ppermute | solution.py:470
  52.5 1.4 %shard_map.57 = (f32[3,16,1280]{2,1,0:T(8,128)S(1)}, f32[16,4,8,1280]{3,2,1,0:T(8,128)S(1)}) custom-call(f32[3,16,512]{2,1,0:T(8,128)S(1)} %collective-permute-done.16.own_half, f32[3,16,512]{2,1,0:T(8,128)S(1)} %collective-permute-done.17.other_half, f32[32,128]{1,0:T(8,128)S(1)} %get-tuple-element.53.bias), custom_call_target="tpu_custom_call" | custom-call | tf_op jit(solution)/shard_map/pallas_call | solution.py:485
  53.9 1.6 %collective-permute-done.18.refs_0_ = f32[4,8,1024]{2,1,0:T(8,128)S(1)} collective-permute-done((f32[4,8,1024]{2,1,0:T(8,128)S(1)}, f32[4,8,1024]{2,1,0:T(8,128)S(1)}, u32[]{:S(2)}, u32[]{:S(2)}) %collective-permute-start.18) | collective-permute-done | bytes 131104 | tf_op jit(solution)/shard_map/ppermute | solution.py:470
  56.0 3.1 %collective-permute-start.19 = (f32[4,8,1024]{2,1,0:T(8,128)S(1)}, f32[4,8,1024]{2,1,0:T(8,128)S(1)}, u32[]{:S(2)}, u32[]{:S(2)}) collective-permute-start(f32[4,8,1024]{2,1,0:T(8,128)S(1)} %get-tuple-element.72), channel_id=1, source_target_pairs={{32,64},{64,32},{96,128},{128,96},{160,192},{192,160},{0,224},{224... | collective-permute-start | bytes 393224 | tf_op jit(solution)/shard_map/ppermute | solution.py:470
  59.1 4.1 %collective-permute-done.20.far_in = f32[4,8,1024]{2,1,0:T(8,128)S(1)} collective-permute-done((f32[4,8,1024]{2,1,0:T(8,128)S(1)}, f32[4,8,1024]{2,1,0:T(8,128)S(1)}, u32[]{:S(2)}, u32[]{:S(2)}) %collective-permute-start.20) | collective-permute-done | bytes 131104 | tf_op jit(solution)/shard_map/ppermute | solution.py:470
  63.3 3.9 %shard_map.59 = bf16[16,32,1024]{2,1,0:T(8,128)(2,1)} custom-call(f32[4,8,1024]{2,1,0:T(8,128)S(1)} %collective-permute-done.19.near_in, f32[4,8,1024]{2,1,0:T(8,128)S(1)} %collective-permute-done.20.far_in, f32[4,8,1024]{2,1,0:T(8,128)S(1)} %collective-permute-done.14.refs_0_.refs_1_.partner_end, f32[16,4,8,1280]{3,2,1,0:T(8,128)S(1)} %get-tuple-element.68.refs_2_.pd, ...), custom_call_target="tpu_custom_call" | custom-call | tf_op jit(solution)/shard_map/pallas_call | solution.py:500
  (24 shorter events, 2.1 us)
Async XLA Ops:
  2.6 1.6 %collective-permute-start = (f32[4,7,16,128]{3,2,1,0:T(8,128)S(1)}, f32[4,7,16,128]{3,2,1,0:T(8,128)S(1)}, u32[]{:S(2)}, u32[]{:S(2)}) collective-permute-start(f32[4,7,16,128]{3,2,1,0:T(8,128)S(1)} %get-tuple-element.42), channel_id=1, source_target_pairs={{0,1},{1,0},{2,3},{3,2},{4,5},{5,4},{6,7},{7,6},{8,9},{9,8},{10,11... | collective-permute-start | bytes 688136 | tf_op jit(solution)/shard_map/ppermute | solution.py:408
  4.2 6.6 %collective-permute-start.1 = (f32[7,16,128]{2,1,0:T(8,128)S(1)}, f32[7,16,128]{2,1,0:T(8,128)S(1)}, u32[]{:S(2)}, u32[]{:S(2)}) collective-permute-start(f32[7,16,128]{2,1,0:T(8,128)S(1)} %get-tuple-element.44), channel_id=1, source_target_pairs={{0,2},{1,3},{2,4},{3,5},{4,6},{5,7},{6,0},{7,1},{8,10},{9,11},{10,... | collective-permute-start | bytes 172040 | tf_op jit(solution)/shard_map/ppermute | solution.py:408
  5.8 5.9 %collective-permute-start.2 = (f32[7,16,128]{2,1,0:T(8,128)S(1)}, f32[7,16,128]{2,1,0:T(8,128)S(1)}, u32[]{:S(2)}, u32[]{:S(2)}) collective-permute-start(f32[7,16,128]{2,1,0:T(8,128)S(1)} %get-tuple-element.45), channel_id=1, source_target_pairs={{0,4},{1,5},{2,6},{3,7},{4,0},{5,1},{6,2},{7,3},{8,12},{9,13},{10,... | collective-permute-start | bytes 172040 | tf_op jit(solution)/shard_map/ppermute | solution.py:408
  8.5 4.2 %collective-permute-start.3 = (f32[7,16,128]{2,1,0:T(8,128)S(1)}, f32[7,16,128]{2,1,0:T(8,128)S(1)}, u32[]{:S(2)}, u32[]{:S(2)}) collective-permute-start(f32[7,16,128]{2,1,0:T(8,128)S(1)} %get-tuple-element.46), channel_id=1, source_target_pairs={{0,6},{1,7},{2,0},{3,1},{4,2},{5,3},{6,4},{7,5},{8,14},{9,15},{10,... | collective-permute-start | bytes 172040 | tf_op jit(solution)/shard_map/ppermute | solution.py:408
  12.7 4.3 %collective-permute-start.6 = (f32[7,16,128]{2,1,0:T(8,128)S(1)}, f32[7,16,128]{2,1,0:T(8,128)S(1)}, u32[]{:S(2)}, u32[]{:S(2)}) collective-permute-start(f32[7,16,128]{2,1,0:T(8,128)S(1)} %shard_map.48.a), channel_id=1, source_target_pairs={{0,8},{1,9},{2,10},{3,11},{4,12},{5,13},{6,14},{7,15},{8,16},{9,17... | collective-permute-start | bytes 172040 | tf_op jit(solution)/shard_map/ppermute | solution.py:408
  13.3 5.7 %collective-permute-start.5 = (f32[7,16,128]{2,1,0:T(8,128)S(1)}, f32[7,16,128]{2,1,0:T(8,128)S(1)}, u32[]{:S(2)}, u32[]{:S(2)}) collective-permute-start(f32[7,16,128]{2,1,0:T(8,128)S(1)} %shard_map.48.a), channel_id=1, source_target_pairs={{0,16},{1,17},{2,18},{3,19},{4,20},{5,21},{6,22},{7,23},{8,24},{9,... | collective-permute-start | bytes 172040 | tf_op jit(solution)/shard_map/ppermute | solution.py:408
  15.6 5.4 %collective-permute-start.4 = (f32[7,16,128]{2,1,0:T(8,128)S(1)}, f32[7,16,128]{2,1,0:T(8,128)S(1)}, u32[]{:S(2)}, u32[]{:S(2)}) collective-permute-start(f32[7,16,128]{2,1,0:T(8,128)S(1)} %shard_map.48.a), channel_id=1, source_target_pairs={{0,24},{1,25},{2,26},{3,27},{4,28},{5,29},{6,30},{7,31},{8,0},{9,1... | collective-permute-start | bytes 172040 | tf_op jit(solution)/shard_map/ppermute | solution.py:408
  21.0 5.5 %collective-permute-start.9 = (f32[7,16,128]{2,1,0:T(8,128)S(1)}, f32[7,16,128]{2,1,0:T(8,128)S(1)}, u32[]{:S(2)}, u32[]{:S(2)}) collective-permute-start(f32[7,16,128]{2,1,0:T(8,128)S(1)} %shard_map.50.p0), channel_id=1, source_target_pairs={{0,2},{1,3},{2,4},{3,5},{4,6},{5,7},{6,0},{7,1},{8,10},{9,11},{10,... | collective-permute-start | bytes 172040 | tf_op jit(solution)/shard_map/ppermute | solution.py:408
  21.6 6.4 %collective-permute-start.8 = (f32[7,16,128]{2,1,0:T(8,128)S(1)}, f32[7,16,128]{2,1,0:T(8,128)S(1)}, u32[]{:S(2)}, u32[]{:S(2)}) collective-permute-start(f32[7,16,128]{2,1,0:T(8,128)S(1)} %shard_map.50.p0), channel_id=1, source_target_pairs={{0,4},{1,5},{2,6},{3,7},{4,0},{5,1},{6,2},{7,3},{8,12},{9,13},{10,... | collective-permute-start | bytes 172040 | tf_op jit(solution)/shard_map/ppermute | solution.py:408
  25.2 4.2 %collective-permute-start.7 = (f32[7,16,128]{2,1,0:T(8,128)S(1)}, f32[7,16,128]{2,1,0:T(8,128)S(1)}, u32[]{:S(2)}, u32[]{:S(2)}) collective-permute-start(f32[7,16,128]{2,1,0:T(8,128)S(1)} %shard_map.50.p0), channel_id=1, source_target_pairs={{0,6},{1,7},{2,0},{3,1},{4,2},{5,3},{6,4},{7,5},{8,14},{9,15},{10,... | collective-permute-start | bytes 172040 | tf_op jit(solution)/shard_map/ppermute | solution.py:408
  25.3 4.1 %collective-permute-start.10 = (f32[7,16,128]{2,1,0:T(8,128)S(1)}, f32[7,16,128]{2,1,0:T(8,128)S(1)}, u32[]{:S(2)}, u32[]{:S(2)}) collective-permute-start(f32[7,16,128]{2,1,0:T(8,128)S(1)} %shard_map.50.p0), channel_id=1, source_target_pairs={{0,1},{1,0},{2,3},{3,2},{4,5},{5,4},{6,7},{7,6},{8,9},{9,8},{10,11... | collective-permute-start | bytes 172040 | tf_op jit(solution)/shard_map/ppermute | solution.py:408
  26.5 2.9 %collective-permute-start.13 = (f32[7,16,128]{2,1,0:T(8,128)S(1)}, f32[7,16,128]{2,1,0:T(8,128)S(1)}, u32[]{:S(2)}, u32[]{:S(2)}) collective-permute-start(f32[7,16,128]{2,1,0:T(8,128)S(1)} %collective-permute-done.9.p3), channel_id=1, source_target_pairs={{0,1},{1,0},{2,3},{3,2},{4,5},{5,4},{6,7},{7,6},{8,9},{9,8},{10,11... | collective-permute-start | bytes 172040 | tf_op jit(solution)/shard_map/ppermute | solution.py:408
  28.0 1.4 %collective-permute-start.12 = (f32[7,16,128]{2,1,0:T(8,128)S(1)}, f32[7,16,128]{2,1,0:T(8,128)S(1)}, u32[]{:S(2)}, u32[]{:S(2)}) collective-permute-start(f32[7,16,128]{2,1,0:T(8,128)S(1)} %collective-permute-done.8.p2), channel_id=1, source_target_pairs={{0,1},{1,0},{2,3},{3,2},{4,5},{5,4},{6,7},{7,6},{8,9},{9,8},{10,11... | collective-permute-start | bytes 172040 | tf_op jit(solution)/shard_map/ppermute | solution.py:408
  29.4 1.2 %collective-permute-start.11 = (f32[7,16,128]{2,1,0:T(8,128)S(1)}, f32[7,16,128]{2,1,0:T(8,128)S(1)}, u32[]{:S(2)}, u32[]{:S(2)}) collective-permute-start(f32[7,16,128]{2,1,0:T(8,128)S(1)} %collective-permute-done.7.p1), channel_id=1, source_target_pairs={{0,1},{1,0},{2,3},{3,2},{4,5},{5,4},{6,7},{7,6},{8,9},{9,8},{10,11... | collective-permute-start | bytes 172040 | tf_op jit(solution)/shard_map/ppermute | solution.py:408
  33.7 6.3 %collective-permute-start.14 = (f32[4,8,1024]{2,1,0:T(8,128)S(1)}, f32[4,8,1024]{2,1,0:T(8,128)S(1)}, u32[]{:S(2)}, u32[]{:S(2)}) collective-permute-start(f32[4,8,1024]{2,1,0:T(8,128)S(1)} %get-tuple-element.54), channel_id=1, source_target_pairs={{0,32},{32,0},{64,96},{96,64},{128,160},{160,128},{192,224},{224,1... | collective-permute-start | bytes 393224 | tf_op jit(solution)/shard_map/ppermute | solution.py:470
  35.6 7.2 %collective-permute-start.16 = (f32[3,16,512]{2,1,0:T(8,128)S(1)}, f32[3,16,512]{2,1,0:T(8,128)S(1)}, u32[]{:S(2)}, u32[]{:S(2)}) collective-permute-start(f32[3,16,512]{2,1,0:T(8,128)S(1)} %get-tuple-element.62), channel_id=1, source_target_pairs={{0,32},{32,0},{64,96},{96,64},{128,160},{160,128},{192,224},{224,1... | collective-permute-start | bytes 294920 | tf_op jit(solution)/shard_map/ppermute | solution.py:470
  40.3 6.3 %collective-permute-start.15 = (f32[4,8,1024]{2,1,0:T(8,128)S(1)}, f32[4,8,1024]{2,1,0:T(8,128)S(1)}, u32[]{:S(2)}, u32[]{:S(2)}) collective-permute-start(f32[4,8,1024]{2,1,0:T(8,128)S(1)} %get-tuple-element.61.refs_8_), channel_id=1, source_target_pairs={{32,96},{192,128},{0,32},{224,192},{96,64},{128,160},{64,0},{160,2... | collective-permute-start | bytes 393224 | tf_op jit(solution)/shard_map/ppermute | solution.py:470
  42.9 1.3 %collective-permute-start.17 = (f32[3,16,512]{2,1,0:T(8,128)S(1)}, f32[3,16,512]{2,1,0:T(8,128)S(1)}, u32[]{:S(2)}, u32[]{:S(2)}) collective-permute-start(f32[3,16,512]{2,1,0:T(8,128)S(1)} %collective-permute-done.16.own_half), channel_id=1, source_target_pairs={{0,1},{1,0},{2,3},{3,2},{4,5},{5,4},{6,7},{7,6},{8,9},{9,8},{10,11... | collective-permute-start | bytes 294920 | tf_op jit(solution)/shard_map/ppermute | solution.py:408
  46.9 8.6 %collective-permute-start.18 = (f32[4,8,1024]{2,1,0:T(8,128)S(1)}, f32[4,8,1024]{2,1,0:T(8,128)S(1)}, u32[]{:S(2)}, u32[]{:S(2)}) collective-permute-start(f32[4,8,1024]{2,1,0:T(8,128)S(1)} %get-tuple-element.71.refs_8_), channel_id=1, source_target_pairs={{96,160},{128,64},{32,96},{192,128},{160,192},{64,32},{0,224},{224... | collective-permute-start | bytes 393224 | tf_op jit(solution)/shard_map/ppermute | solution.py:470
  55.7 7.5 %collective-permute-start.20 = (f32[4,8,1024]{2,1,0:T(8,128)S(1)}, f32[4,8,1024]{2,1,0:T(8,128)S(1)}, u32[]{:S(2)}, u32[]{:S(2)}) collective-permute-start(f32[4,8,1024]{2,1,0:T(8,128)S(1)} %get-tuple-element.72), channel_id=1, source_target_pairs={{160,224},{64,0},{128,160},{96,64},{224,192},{0,32},{32,96},{192,1... | collective-permute-start | bytes 393224 | tf_op jit(solution)/shard_map/ppermute | solution.py:470
  56.0 7.3 %collective-permute-start.19 = (f32[4,8,1024]{2,1,0:T(8,128)S(1)}, f32[4,8,1024]{2,1,0:T(8,128)S(1)}, u32[]{:S(2)}, u32[]{:S(2)}) collective-permute-start(f32[4,8,1024]{2,1,0:T(8,128)S(1)} %get-tuple-element.72), channel_id=1, source_target_pairs={{32,64},{64,32},{96,128},{128,96},{160,192},{192,160},{0,224},{224... | collective-permute-start | bytes 393224 | tf_op jit(solution)/shard_map/ppermute | solution.py:470
